TPU v7x, 256 devices: a whole 4x4x8 slice. The times are simulated.
256 devices in a mesh: dp: 32 (over x_hi, z, core), tensor: 8 (over y, x_lo).
Axes of the slice: x: 4 (x_hi: 2, x_lo: 2; x = x_hi * 2 + x_lo), y: 4, z: 8, core: 2. Of those that a mesh axis runs over, the one named last changes fastest.
Arguments:
- tokens: bfloat16 [32768, 8192], P(('dp', 'tensor')), may hold values from -6 to 6
- out_grad: bfloat16 [32768, 26624], P('dp', 'tensor')
- delta: float32 [8, 128, 128, 128], P('tensor', 'dp'), may hold values from -3 to 3
- block_rows: int32 [1024], P('tensor'), may hold values from 0 to 63, as said below
- block_cols: int32 [1024], P('tensor'), may hold values from 0 to 25, as said below
- block_count: int32 [8], P('tensor'), may hold values from 1 to 128, as said below
Outputs:
- new_delta: float32 [8, 128, 128, 128], P('tensor', 'dp')
Inputs may be any that keep to these rules, and one draw needn't show every extreme that they name: `block_rows`: entry t * 128 + k names the row block of slot k of tensor shard t; the slots of one shard name distinct pairs of row and column block. `block_cols`: entry t * 128 + k names the column block, counted within shard t's columns, of slot k of shard t. Slots 0 to block_count[t] - 1 of shard t are live, the rest are padding; some shard has all 128 live.
All inputs are finite; a program needn't handle non-finite values.
Results may differ from a plain program's by a relative error of at most 0.0003.
Values may be sent and summed in bfloat16 or wider, within the bound.
No kernel may reach another device: no remote copies, remote signals or barrier semaphores. Data moves between devices by JAX's collectives and lax.ppermute only.
A program may use at most 192 MiB of HBM per device.

v0:
```python
import math

import jax
import jax.numpy as jnp
from jax import lax
from jax.sharding import PartitionSpec as P

GROUP = 32


def on_device(tokens, out_grad, delta, block_rows, block_cols, block_count):
    slot_count = block_rows.shape[0]
    block_size = delta.shape[-1]
    row_blocks = tokens.shape[1] // block_size
    col_blocks = out_grad.shape[1] // block_size
    group_trips = slot_count // GROUP
    zero_grads = jnp.zeros((slot_count, block_size, block_size), jnp.float32)
    shard_rows = lax.all_gather(tokens, "tensor", axis=0, tiled=True)
    row_count = shard_rows.shape[0]
    token_tiles = shard_rows.reshape(row_count, row_blocks, block_size)
    grad_tiles = out_grad.reshape(row_count, col_blocks, block_size)

    def one_group(group_index, partial_sum):
        row_ids = lax.dynamic_slice_in_dim(block_rows, group_index * GROUP, GROUP)
        col_ids = lax.dynamic_slice_in_dim(block_cols, group_index * GROUP, GROUP)
        token_cols = jnp.take(token_tiles, row_ids, axis=1)
        grad_cols = jnp.take(grad_tiles, col_ids, axis=1)
        partial_value = jnp.einsum(
            "rkc,rkd->kcd", token_cols, grad_cols, preferred_element_type=jnp.float32
        )
        previous = lax.dynamic_slice_in_dim(partial_sum, group_index * GROUP, GROUP, 0)
        return lax.dynamic_update_slice_in_dim(
            partial_sum, previous + partial_value, group_index * GROUP, 0
        )

    block_grads = lax.fori_loop(0, group_trips, one_group, zero_grads)
    live_mask = (jnp.arange(slot_count, dtype=jnp.int32) < block_count[0]).astype(jnp.float32)
    block_grads = block_grads * live_mask[:, None, None]
    cycle_size = lax.axis_size("tensor")
    norm_limit = block_size * math.sqrt(cycle_size * slot_count)
    share_len = delta.shape[1]
    summed = lax.psum(block_grads, "dp")
    square_sum = lax.psum(jnp.sum(summed * summed), "tensor")
    own_share = lax.dynamic_slice_in_dim(summed, lax.axis_index("dp") * share_len, share_len, 0)
    factor = jnp.minimum(jnp.float32(1.0), norm_limit / jnp.sqrt(square_sum + 1e-06))
    return delta - 0.5 * factor * own_share[None]


def solution(mesh):
    return jax.shard_map(
        on_device,
        mesh=mesh,
        in_specs=(
            P(("dp", "tensor"), None),
            P("dp", "tensor"),
            P("tensor", "dp", None, None),
            P("tensor"),
            P("tensor"),
            P("tensor"),
        ),
        out_specs=P("tensor", "dp", None, None),
        check_vma=False,
    )
```

profile of v0, /device:TPU:4, one launch (start us, length us, event | category | flops | bytes accessed | tf_op | source)
XLA Modules:
  0.0 820.8 jit_solution(13977758874296105967)
XLA Ops:
  6.5 4.1 copy.13
  10.7 10.0 %copy.14 = bf16[1024,3328]{0,1:T(8,128)(2,1)} copy(bf16[1024,3328]{1,0:T(8,128)(2,1)} %param.9) | data formatting | bytes 13631488 | tf_op args[1]
  20.7 10.0 %copy.16 = bf16[1024,26,128]{2,0,1:T(8,128)(2,1)} copy(bf16[1024,26,128]{0,2,1:T(8,128)(2,1)} %bitcast.20) | data formatting | bytes 13631488 | tf_op jit(solution)/shard_map/while | solution.py:36
  31.3 310.0 %all-gather.2.cloned.1.call-done = bf16[1024,8192]{0,1:T(8,128)(2,1)} async-done(((bf16[128,8192]{0,1:T(8,128)(2,1)}), bf16[1024,8192]{0,1:T(8,128)(2,1)}) %all-gather.2.cloned.1.call-update) | async-done | bytes 16777232 | tf_op jit(solution)/shard_map/all_gather | solution.py:18
  341.3 22.4 %copy.15 = bf16[1024,64,128]{2,0,1:T(8,128)(2,1)} copy(bf16[1024,64,128]{0,2,1:T(8,128)(2,1)} %bitcast.21) | data formatting | bytes 33554432 | tf_op jit(solution)/shard_map/while | solution.py:36
  363.7 4.3 broadcast_in_dim.47
  368.0 118.7 %while.13 = (s32[]{:T(128)}, f32[128,128,128]{2,1,0:T(8,128)}, s32[128]{0:T(128)S(1)}, bf16[1024,64,128]{2,0,1:T(8,128)(2,1)}, s32[128]{0:T(128)S(1)}, /*index=5...) while((s32[]{:T(128)}, f32[128,128,128]{2,1,0:T(8,128)}, s32[128]{0:T(128)S(1)}, ...), condition=%wide.region_1.0_spmd, body=%wide.region_0.1_spmd.sunk | while | flops 1082657152 | bytes 54535460 | solution.py:36
  368.0 8.0 gather_fusion
  376.0 10.8 %gather_fusion.1 = bf16[32,1024,128]{2,1,0:T(8,128)(2,1)} fusion(bf16[1024,64,128]{2,0,1:T(8,128)(2,1)} %get-tuple-element.213, s32[1024]{0:T(1024)S(1)} %pad_clamp_fusion.5), kind=kCustom, calls=%fused_computation.clone.1 | custom fusion | bytes 16777344 | tf_op jit(solution)/shard_map/while/body/eval_jaxpr/jit(_take)/gather | solution.py:26
  386.8 10.8 %add_dynamic-update-slice_fusion.2 = f32[128,128,128]{2,1,0:T(8,128)} fusion(f32[128,128,128]{2,1,0:T(8,128)} %get-tuple-element.201, s32[]{:T(128)S(6)} %select_n.70, bf16[32,1024,128]{2,1,0:T(8,128)(2,1)} %gather_fusion, pred[32]{0:T(512)(128)(4,1)S(1)} %get-tuple-element.187, bf16[32,1024,128]{2,1,0:T(8,128)(2,1)} %gather_fusion.1, ...), kind=kOutput, calls=%fused_computation.10.clone.1 | convolution fusion | flops 1082654720 | bytes 20971588 | tf_op jit(solution)/shard_map/while/body/eval_jaxpr/rkc,rkd->kcd/dot_general | solution.py:28
  397.7 7.9 gather_fusion
  405.6 10.8 %gather_fusion.1 = bf16[32,1024,128]{2,1,0:T(8,128)(2,1)} fusion(bf16[1024,64,128]{2,0,1:T(8,128)(2,1)} %get-tuple-element.213, s32[1024]{0:T(1024)S(1)} %pad_clamp_fusion.5), kind=kCustom, calls=%fused_computation.clone.1 | custom fusion | bytes 16777344 | tf_op jit(solution)/shard_map/while/body/eval_jaxpr/jit(_take)/gather | solution.py:26
  416.4 10.9 %add_dynamic-update-slice_fusion.2 = f32[128,128,128]{2,1,0:T(8,128)} fusion(f32[128,128,128]{2,1,0:T(8,128)} %get-tuple-element.201, s32[]{:T(128)S(6)} %select_n.70, bf16[32,1024,128]{2,1,0:T(8,128)(2,1)} %gather_fusion, pred[32]{0:T(512)(128)(4,1)S(1)} %get-tuple-element.187, bf16[32,1024,128]{2,1,0:T(8,128)(2,1)} %gather_fusion.1, ...), kind=kOutput, calls=%fused_computation.10.clone.1 | convolution fusion | flops 1082654720 | bytes 20971588 | tf_op jit(solution)/shard_map/while/body/eval_jaxpr/rkc,rkd->kcd/dot_general | solution.py:28
  427.4 8.0 gather_fusion
  435.4 10.8 %gather_fusion.1 = bf16[32,1024,128]{2,1,0:T(8,128)(2,1)} fusion(bf16[1024,64,128]{2,0,1:T(8,128)(2,1)} %get-tuple-element.213, s32[1024]{0:T(1024)S(1)} %pad_clamp_fusion.5), kind=kCustom, calls=%fused_computation.clone.1 | custom fusion | bytes 16777344 | tf_op jit(solution)/shard_map/while/body/eval_jaxpr/jit(_take)/gather | solution.py:26
  446.1 10.8 %add_dynamic-update-slice_fusion.2 = f32[128,128,128]{2,1,0:T(8,128)} fusion(f32[128,128,128]{2,1,0:T(8,128)} %get-tuple-element.201, s32[]{:T(128)S(6)} %select_n.70, bf16[32,1024,128]{2,1,0:T(8,128)(2,1)} %gather_fusion, pred[32]{0:T(512)(128)(4,1)S(1)} %get-tuple-element.187, bf16[32,1024,128]{2,1,0:T(8,128)(2,1)} %gather_fusion.1, ...), kind=kOutput, calls=%fused_computation.10.clone.1 | convolution fusion | flops 1082654720 | bytes 20971588 | tf_op jit(solution)/shard_map/while/body/eval_jaxpr/rkc,rkd->kcd/dot_general | solution.py:28
  457.1 7.9 gather_fusion
  465.0 10.8 %gather_fusion.1 = bf16[32,1024,128]{2,1,0:T(8,128)(2,1)} fusion(bf16[1024,64,128]{2,0,1:T(8,128)(2,1)} %get-tuple-element.213, s32[1024]{0:T(1024)S(1)} %pad_clamp_fusion.5), kind=kCustom, calls=%fused_computation.clone.1 | custom fusion | bytes 16777344 | tf_op jit(solution)/shard_map/while/body/eval_jaxpr/jit(_take)/gather | solution.py:26
  475.8 10.8 %add_dynamic-update-slice_fusion.2 = f32[128,128,128]{2,1,0:T(8,128)} fusion(f32[128,128,128]{2,1,0:T(8,128)} %get-tuple-element.201, s32[]{:T(128)S(6)} %select_n.70, bf16[32,1024,128]{2,1,0:T(8,128)(2,1)} %gather_fusion, pred[32]{0:T(512)(128)(4,1)S(1)} %get-tuple-element.187, bf16[32,1024,128]{2,1,0:T(8,128)(2,1)} %gather_fusion.1, ...), kind=kOutput, calls=%fused_computation.10.clone.1 | convolution fusion | flops 1082654720 | bytes 20971588 | tf_op jit(solution)/shard_map/while/body/eval_jaxpr/rkc,rkd->kcd/dot_general | solution.py:28
  486.6 7.2 broadcast_multiply_fusion
  493.9 291.6 %all-reduce.2.cloned.1.call-done = f32[128,128,128]{2,1,0:T(8,128)} async-done(((f32[128,128,128]{2,1,0:T(8,128)}), f32[128,128,128]{2,1,0:T(8,128)}) %all-reduce.2.cloned.1.call-update) | async-done | bytes 8388624 | tf_op jit(solution)/shard_map/psum | solution.py:42
  785.5 6.1 multiply_reduce_fusion
  791.6 20.0 %psum.15 = f32[]{:T(128)} all-reduce(f32[]{:T(128)} %multiply_reduce_fusion), channel_id=1, replica_groups=mesh['dp'=32,'tensor'=8] {'tensor'}, use_global_device_ids=true, to_apply=%region_4.5 | all-reduce | flops 1 | bytes 8 | tf_op jit(solution)/shard_map/psum | solution.py:43
  812.3 1.7 bitcast_subtract_fusion
  (23 shorter events, 0.5 us)
Async XLA Ops:
  6.5 334.8 %all-gather.2.cloned.1.call-start = ((), (), s32[]{:S(2)}) async-start(), calls=%async_computation | async-start | bytes 18874368 | tf_op jit(solution)/shard_map/all_gather | solution.py:18
  10.6 774.8 %all-reduce.2.cloned.1.call-start = ((), (), s32[]{:S(2)}) async-start(), calls=%async_computation.1 | async-start | bytes 16777216 | tf_op jit(solution)/shard_map/psum | solution.py:42
  363.7 4.3 copy-start.1
  363.7 4.3 copy-start.2
  493.8 318.5 %copy-start = (f32[1,4,128,128]{3,2,1,0:T(8,128)S(1)}, f32[1,4,128,128]{3,2,1,0:T(8,128)}, u32[]{:S(2)}) copy-start(f32[1,4,128,128]{3,2,1,0:T(8,128)} %param.10) | copy-start | bytes 786436
Sparse Core Ops, SparseCore 0:
  10.8 330.4 all-gather.1
  494.0 291.4 all-reduce.1
where the time goes:
time: 822 us; the launch traced here: 821 us
  waiting for transfers between devices  602 us (73%)
  local copies, waits for them, and re-layouts  126 us (15%)
  matrix products  43.4 us (5%)
  blocking collectives  20 us (2%)
  other arithmetic  15.4 us (2%)
  between operations  14.8 us (2%)
    all_gather x1, waiting for transfers between devices, on_device(): shard_rows = lax.all_gather(tokens, 'tensor', axis=0, tiled=True)  310 us
    psum x1, waiting for transfers between devices, on_device(): summed = lax.psum(block_grads, 'dp')  292 us
    dot_general x4, matrix products, one_group(): jnp.einsum('rkc,rkd->kcd', token_cols, grad_cols, preferred_element_type=...  43.4 us
    gather x4, local copies, waits for them, and re-layouts, one_group(): token_cols = jnp.take(token_tiles, row_ids, axis=1)  43.1 us
    while x2, local copies, waits for them, and re-layouts, on_device(): block_grads = lax.fori_loop(0, group_trips, one_group, zero_grads)  32.4 us
    gather x4, local copies, waits for them, and re-layouts, one_group(): grad_cols = jnp.take(grad_tiles, col_ids, axis=1)  31.8 us
    psum x1, blocking collectives, on_device(): square_sum = lax.psum(jnp.sum(summed * summed), 'tensor')  20 us
  transfers between devices with their start and end apart: 2, of which 2 were waited for; matrix products, arithmetic and copies ran while one was open for 2% of the time, Pallas kernels for 0%

commit v1 on v0

v1 whole, which is shorter than its diff:
```python
import functools
import math

import jax
import jax.numpy as jnp
from jax import lax
from jax.experimental import pallas as pl
from jax.experimental.pallas import tpu as pltpu
from jax.sharding import PartitionSpec as P


UNROLL = 8
X_SWAP = [(t, t ^ 1) for t in range(8)]
Y_UP = [(t, (t + 2) % 8) for t in range(8)]
Y_DOWN = [(t, (t + 6) % 8) for t in range(8)]
CORE_SWAP = [(d, d ^ 1) for d in range(32)]
X_HI_SWAP = [(d, d ^ 16) for d in range(32)]
DIAGONAL = [(d * 8 + t, (d ^ 16) * 8 + (t ^ 1)) for d in range(32) for t in range(8)]


def z_swap(bit):
    return [(d, d ^ (bit * 2)) for d in range(32)]


def z_shift(k):
    return [(d, (d // 16) * 16 + (d + 2 * k) % 16) for d in range(32)]


CORE, Z, X_HI, OWN, BELOW, ABOVE, FAR = range(7)


def grads_kernel(plan, depths, split, with_acc, meta, slots_ref, *refs):
    count = len(plan)
    pieces = refs[:count]
    at = count
    grads = refs[at : at + len(depths)]
    at += len(depths)
    if with_acc:
        acc_hbm = refs[at]
        at += 1
    outs_hbm = refs[at : at + (2 if split else 1)]
    at += len(outs_hbm)
    x_buf, g_buf, o_buf, in_sem, out_sem = refs[at:]
    places = o_buf.shape[0]
    half = places // 2
    copies = []
    row = 0
    for index, size in enumerate(plan):
        copies.append(
            pltpu.make_async_copy(pieces[index], x_buf.at[pl.ds(row, size), :], in_sem.at[len(copies)])
        )
        row += size
    row = 0
    for index, (size, source) in enumerate(depths):
        block = grads[index]
        if source is not None:
            block = block.at[pl.ds(pl.multiple_of(meta[source] * 128, 128), size), :]
        copies.append(
            pltpu.make_async_copy(block, g_buf.at[pl.ds(row, size), :], in_sem.at[len(copies)])
        )
        row += size
    if with_acc:
        copies.append(pltpu.make_async_copy(acc_hbm, o_buf, in_sem.at[len(copies)]))
    for copy in copies:
        copy.start()
    for copy in copies:
        copy.wait()
    core, z, x_hi = meta[CORE], meta[Z], meta[X_HI]
    live = slots_ref[2, 0]

    def slot_of(place):
        part = lax.shift_right_logical(place, 6)
        far_half = lax.bitwise_and(lax.shift_right_logical(place, 5), 1)
        ahead = lax.bitwise_and(lax.shift_right_logical(place, 2), 7)
        owner_core = lax.bitwise_xor(core, 1 - part)
        owner_x = lax.bitwise_xor(x_hi, far_half)
        owner_z = lax.bitwise_and(z + ahead, 7)
        return owner_x * 64 + owner_z * 8 + owner_core * 4 + lax.bitwise_and(place, 3)

    def trip(step, carry):
        values = []
        for u in range(UNROLL):
            place = step * UNROLL + u
            slot = slot_of(place)
            row = pl.multiple_of(slots_ref[0, slot] * 128, 128)
            col = pl.multiple_of(slots_ref[1, slot] * 128, 128)
            value = lax.dot_general(
                x_buf[:, pl.ds(row, 128)],
                g_buf[:, pl.ds(col, 128)],
                (((0,), (0,)), ((), ())),
                preferred_element_type=jnp.float32,
            )
            if with_acc:
                value = o_buf[place] + value
            if split:
                value = jnp.where(slot < live, value, 0.0)
            values.append(value)
        for u in range(UNROLL):
            o_buf[step * UNROLL + u] = values[u]
        return carry

    if split:
        targets = outs_hbm
    else:
        targets = [outs_hbm[0].at[pl.ds(0, half)], outs_hbm[0].at[pl.ds(half, half)]]
    outs = [
        pltpu.make_async_copy(o_buf.at[pl.ds(i * half, half)], targets[i], out_sem.at[i]) for i in range(2)
    ]
    lax.fori_loop(0, half // UNROLL, trip, 0)
    outs[0].start()
    lax.fori_loop(half // UNROLL, places // UNROLL, trip, 0)
    outs[1].start()
    outs[0].wait()
    outs[1].wait()


def partial_grads(meta, slot_table, pieces, grads, sources, split, acc=None):
    plan = tuple(piece.shape[0] for piece in pieces)
    depth = sum(plan)
    depths = tuple((128, source) for source in sources)
    assert depth == 128 * len(depths)
    places = slot_table.shape[1]
    any_spec = pl.BlockSpec(memory_space=pl.ANY)
    block = (places, 128, 128)
    half = jax.ShapeDtypeStruct((places // 2, 128, 128), jnp.float32)
    out_shape = (half, half) if split else (jax.ShapeDtypeStruct(block, jnp.float32),)
    extra = () if acc is None else (acc,)
    operands = (*pieces, *grads, *extra)
    return pl.pallas_call(
        functools.partial(grads_kernel, plan, depths, split, acc is not None),
        out_shape=out_shape,
        in_specs=[pl.BlockSpec(memory_space=pltpu.SMEM)] * 2 + [any_spec] * len(operands),
        out_specs=tuple(any_spec for _ in out_shape),
        scratch_shapes=[
            pltpu.VMEM((depth, pieces[0].shape[1]), jnp.bfloat16),
            pltpu.VMEM((depth, grads[0].shape[1]), jnp.bfloat16),
            pltpu.VMEM(block, jnp.float32),
            pltpu.SemaphoreType.DMA((len(operands),)),
            pltpu.SemaphoreType.DMA((2,)),
        ],
        compiler_params=pltpu.CompilerParams(vmem_limit_bytes=56 * 1024 * 1024),
        cost_estimate=pl.CostEstimate(
            flops=2 * places * 128 * 128 * depth, bytes_accessed=30_000_000, transcendentals=0
        ),
    )(meta, slot_table, *operands)


def on_device(tokens, out_grad, delta, block_rows, block_cols, block_count):
    places = block_rows.shape[0]
    dp = lax.axis_index("dp")
    tp = lax.axis_index("tensor")
    across = lax.bitwise_xor(tp, 1)

    def around(base):
        return [base, lax.bitwise_and(base + 6, 7), lax.bitwise_and(base + 2, 7), lax.bitwise_and(base + 4, 7)]

    def move(value, pairs, axis="tensor"):
        return lax.ppermute(value, axis, pairs)

    meta = jnp.stack(
        [lax.bitwise_and(dp, 1), lax.bitwise_and(dp >> 1, 7), dp >> 4, *around(tp)]
    ).astype(jnp.int32)
    table = jnp.stack([block_rows, block_cols, jnp.broadcast_to(block_count, (places,))])
    part_a, part_b = tokens[:64], tokens[64:]
    theirs = [lax.dynamic_slice_in_dim(out_grad, chunk * 128, 128, 0) for chunk in around(across)]
    below_a, above_b = move(part_a, Y_UP), move(part_b, Y_DOWN)
    table_x = move(table, X_SWAP)
    top = jnp.broadcast_to(jnp.max(jnp.abs(out_grad)).astype(jnp.float32), (8, 128))
    for pairs, axis in (
        (X_SWAP, "tensor"),
        (X_HI_SWAP, "dp"),
        (CORE_SWAP, "dp"),
        (z_swap(1), "dp"),
        (z_swap(2), "dp"),
        (z_swap(4), "dp"),
    ):
        top = jnp.maximum(top, move(top, pairs, axis))
    top = jnp.clip(top[0, 0], 1e-30, 1e37)
    g_own = move(theirs[0], X_SWAP)
    below_b, above_a = move(part_b, Y_UP), move(part_a, Y_DOWN)
    g_below = move(theirs[1], X_SWAP)
    g_above = move(theirs[2], X_SWAP)
    g_far = move(theirs[3], X_SWAP)
    far_a, far_b = move(below_a, Y_UP), move(above_b, Y_DOWN)
    meta_late, shrink, grow = lax.optimization_barrier((meta, 0.25 / top, 4.0 * top))

    (acc,) = partial_grads(
        meta, table_x, (tokens, below_a, below_b, above_a, above_b),
        (g_own, g_below, g_above), (None, None, None), False,
    )
    send, keep = partial_grads(
        meta_late, table, (tokens, below_a, below_b, above_a, above_b, far_a, far_b),
        (out_grad, out_grad, out_grad, out_grad), (OWN, BELOW, ABOVE, FAR), True,
    )
    send_x, keep_x = partial_grads(meta, table_x, (far_a, far_b), (g_far,), (None,), True, acc)
    share = delta.shape[1]
    quarter = places // 4
    ours = (keep + move(send, CORE_SWAP, "dp")) * shrink
    far_half = move(ours[quarter:].astype(jnp.float16), X_HI_SWAP, "dp")
    other = ((keep_x + move(send_x, CORE_SWAP, "dp")) * shrink).astype(jnp.float16)
    near_x = move(other[:quarter], X_SWAP)
    far_x = move(other[quarter:], DIAGONAL, ("dp", "tensor"))
    ours = (
        ours[:quarter]
        + far_half.astype(jnp.float32)
        + near_x.astype(jnp.float32)
        + far_x.astype(jnp.float32)
    )
    packed = ours.astype(jnp.float16)
    grads = ours[:share]
    for k in (4, 3, 5, 2, 6, 1, 7):
        got = move(packed[share * k : share * (k + 1)], z_shift(k), "dp")
        grads = grads + got.astype(jnp.float32)
    grads = grads * grow
    square_sum = jnp.broadcast_to(jnp.sum(grads * grads), (8, 128))
    for axis, size in (("dp", 32), ("tensor", 8)):
        spread = jnp.broadcast_to(square_sum[None], (size, 8, 128))
        square_sum = jnp.sum(lax.all_to_all(spread, axis, 0, 0, tiled=True), axis=0)
    square_sum = square_sum[0, 0]
    norm_limit = 128 * math.sqrt(8 * places)
    factor = jnp.minimum(jnp.float32(1.0), norm_limit / jnp.sqrt(square_sum + 1e-06))
    return delta - 0.5 * factor * grads[None]


def solution(mesh):
    return jax.shard_map(
        on_device,
        mesh=mesh,
        in_specs=(
            P(("dp", "tensor"), None),
            P("dp", "tensor"),
            P("tensor", "dp", None, None),
            P("tensor"),
            P("tensor"),
            P("tensor"),
        ),
        out_specs=P("tensor", "dp", None, None),
        check_vma=False,
    )
```

time: 822 us -> 261 us (0.32)
  waiting for transfers between devices: 602 us -> 119 us
  local copies, waits for them, and re-layouts: 126 us -> 11.5 us
  starting transfers between devices: 0.04 us -> 45.1 us
  matrix products: 43.4 us -> 0 us
  Pallas kernels: 0 us -> 41.7 us
  between operations: 14.8 us -> 2.81 us
    all_gather x1 -> x0, waiting for transfers between devices: 310 us -> none  [on_device(): shard_rows = lax.all_gather(tokens, 'tensor', axis=0, tiled=True)]
    psum x1 -> x0, waiting for transfers between devices: 292 us -> none  [on_device(): summed = lax.psum(block_grads, 'dp')]
    ppermute x0 -> x29, waiting for transfers between devices: none -> 119 us  [move(): return lax.ppermute(value, axis, pairs)]
    gather x8 -> x0, local copies, waits for them, and re-layouts: 74.9 us -> none  [the longest x4 43.1 us: one_group(): token_cols = jnp.take(token_tiles, row_ids, axis=1)]
    ppermute x0 -> x29, starting transfers between devices: none -> 45.1 us  [move(): return lax.ppermute(value, axis, pairs)]
    dot_general x4 -> x0, matrix products: 43.4 us -> none  [one_group(): jnp.einsum('rkc,rkd->kcd', token_cols, grad_cols, preferred_element_type=...]
    pallas_call x0 -> x3, Pallas kernels: none -> 41.7 us  [partial_grads(): pl.pallas_call(functools.partial(grads_kernel, plan, depths, split, acc i...]
    while x2 -> x0, local copies, waits for them, and re-layouts: 32.4 us -> none  [on_device(): block_grads = lax.fori_loop(0, group_trips, one_group, zero_grads)]
  transfers between devices with their start and end apart: 2 -> 29, of which waited for: 2 -> 18; matrix products, arithmetic and copies ran while one was open for 2% -> 6% of each run, Pallas kernels for 0% -> 16%
where the time goes in v1:
time: 261 us; the launch traced here: 259 us
  waiting for transfers between devices  119 us (46%)
  starting transfers between devices  45.1 us (17%)
  Pallas kernels  41.7 us (16%)
  blocking collectives  27.9 us (11%)
  local copies, waits for them, and re-layouts  11.5 us (4%)
  other arithmetic  11.2 us (4%)
  between operations  2.81 us (1%)
    ppermute x29, waiting for transfers between devices, move(): return lax.ppermute(value, axis, pairs)  119 us
    ppermute x29, starting transfers between devices, move(): return lax.ppermute(value, axis, pairs)  45.1 us
    pallas_call x3, Pallas kernels, partial_grads(): pl.pallas_call(functools.partial(grads_kernel, plan, depths, split, acc i...  41.7 us
    all_to_all x2, blocking collectives, on_device(): square_sum = jnp.sum(lax.all_to_all(spread, axis, 0, 0, tiled=True), axis=0)  27.9 us
  transfers between devices with their start and end apart: 29, of which 18 were waited for; matrix products, arithmetic and copies ran while one was open for 6% of the time, Pallas kernels for 16%

profile of v1, /device:TPU:4, one launch (start us, length us, event | category | flops | bytes accessed | tf_op | source)
XLA Modules:
  0.0 259.4 jit_solution(10791752805924685931)
XLA Ops:
  0.0 3.0 %fusion.13 = (bf16[64,8192]{1,0:T(8,128)(2,1)}, bf16[64,8192]{1,0:T(8,128)(2,1)}) fusion(bf16[128,8192]{1,0:T(8,128)(2,1)} %refs_0_.3), kind=kLoop, calls=%fused_computation.25 | loop fusion | bytes 4194304 | tf_op jit(solution)/shard_map/slice | solution.py:164
  3.0 3.0 %collective-permute-start.9 = (bf16[64,8192]{1,0:T(8,128)(2,1)}, bf16[64,8192]{1,0:T(8,128)(2,1)S(1)}, u32[]{:S(2)}, u32[]{:S(2)}) collective-permute-start(bf16[64,8192]{1,0:T(8,128)(2,1)} %get-tuple-element.29), channel_id=1, source_target_pairs={{0,6},{1,7},{2,0},{3,1},{4,2},{5,3},{6,4},{7,5},{8,14},{9,15},{10,... | collective-permute-start | bytes 3145736 | tf_op jit(solution)/shard_map/ppermute | solution.py:158
  6.7 2.7 %collective-permute-start.8 = (bf16[64,8192]{1,0:T(8,128)(2,1)}, bf16[64,8192]{1,0:T(8,128)(2,1)}, u32[]{:S(2)}, u32[]{:S(2)}) collective-permute-start(bf16[64,8192]{1,0:T(8,128)(2,1)} %get-tuple-element.30), channel_id=1, source_target_pairs={{0,6},{1,7},{2,0},{3,1},{4,2},{5,3},{6,4},{7,5},{8,14},{9,15},{10,... | collective-permute-start | bytes 3145736 | tf_op jit(solution)/shard_map/ppermute | solution.py:158
  9.3 4.4 %abs_reduce_fusion = bf16[]{:T(256)} fusion(bf16[1024,3328]{1,0:T(8,128)(2,1)} %refs_10_.1), kind=kLoop, calls=%fused_computation | loop fusion | flops 6815743 | bytes 6815746 | tf_op jit(solution)/shard_map/reduce_max | solution.py:168
  16.4 13.6 %collective-permute-done.9.refs_4_ = bf16[64,8192]{1,0:T(8,128)(2,1)S(1)} collective-permute-done((bf16[64,8192]{1,0:T(8,128)(2,1)}, bf16[64,8192]{1,0:T(8,128)(2,1)S(1)}, u32[]{:S(2)}, u32[]{:S(2)}) %collective-permute-start.9) | collective-permute-done | bytes 1048608 | tf_op jit(solution)/shard_map/ppermute | solution.py:158
  29.9 3.6 %collective-permute-start.11 = (bf16[64,8192]{1,0:T(8,128)(2,1)S(1)}, bf16[64,8192]{1,0:T(8,128)(2,1)S(1)}, u32[]{:S(2)}, u32[]{:S(2)}) collective-permute-start(bf16[64,8192]{1,0:T(8,128)(2,1)S(1)} %collective-permute-done.9.refs_4_), channel_id=1, source_target_pairs={{0,6},{1,7},{2,0},{3,1},{4,2},{5,3},{6,4},{7,5},{8,14},{9,15},{10,... | collective-permute-start | bytes 3145736 | tf_op jit(solution)/shard_map/ppermute | solution.py:158
  34.2 4.6 %collective-permute-done.1 = f32[8,128]{1,0:T(8,128)S(1)} collective-permute-done((f32[8,128]{1,0:T(8,128)S(1)}, f32[8,128]{1,0:T(8,128)S(1)}, u32[]{:S(2)}, u32[]{:S(2)}) %collective-permute-start.1) | collective-permute-done | bytes 4128 | tf_op jit(solution)/shard_map/ppermute | solution.py:158
  43.6 3.3 %collective-permute-start.4 = (f32[8,128]{1,0:T(8,128)S(1)}, f32[8,128]{1,0:T(8,128)S(1)}, u32[]{:S(2)}, u32[]{:S(2)}) collective-permute-start(f32[8,128]{1,0:T(8,128)S(1)} %max.26), channel_id=1, source_target_pairs={{0,32},{8,40},{16,48},{24,56},{32,0},{40,8},{48,16},{56,24},{64,96... | collective-permute-start | bytes 12296 | tf_op jit(solution)/shard_map/ppermute | solution.py:158
  48.5 6.8 %collective-permute-start.5 = (f32[8,128]{1,0:T(8,128)S(1)}, f32[8,128]{1,0:T(8,128)S(1)}, u32[]{:S(2)}, u32[]{:S(2)}) collective-permute-start(f32[8,128]{1,0:T(8,128)S(1)} %max.27), channel_id=1, source_target_pairs={{0,64},{8,72},{16,80},{24,88},{32,96},{40,104},{48,112},{56,120},{... | collective-permute-start | bytes 12296 | tf_op jit(solution)/shard_map/ppermute | solution.py:158
  55.3 3.8 %constant_dynamic-slice_fusion = (bf16[128,3328]{1,0:T(8,128)(2,1)}, bf16[128,3328]{1,0:T(8,128)(2,1)}, bf16[128,3328]{1,0:T(8,128)(2,1)}, bf16[128,3328]{1,0:T(8,128)(2,1)}) fusion(bf16[1024,3328]{1,0:T(8,128)(2,1)} %refs_10_.1, s32[]{:T(128)S(6)} %select_n.15, s32[]{:T(128)S(6)} %select_n.13, s32[]{:T(128)S(6)} %select_n.12, s32[]{:T(128)S(6)} %select_n.14), kind=kLoop, calls=%fused_computation.19 | loop fusion | bytes 6815760 | tf_op jit(solution)/shard_map/dynamic_slice | solution.py:165
  64.9 8.7 %collective-permute-done.11.refs_6_.refs_1_ = bf16[64,8192]{1,0:T(8,128)(2,1)S(1)} collective-permute-done((bf16[64,8192]{1,0:T(8,128)(2,1)S(1)}, bf16[64,8192]{1,0:T(8,128)(2,1)S(1)}, u32[]{:S(2)}, u32[]{:S(2)}) %collective-permute-start.11) | collective-permute-done | bytes 1048608 | tf_op jit(solution)/shard_map/ppermute | solution.py:158
  78.3 16.6 %shard_map.67 = (f32[64,128,128]{2,1,0:T(8,128)}, f32[64,128,128]{2,1,0:T(8,128)}) custom-call(s32[7]{0:T(128)} %stack.40.meta, s32[3,128]{1,0:T(4,128)} %copy-done.6, bf16[128,8192]{1,0:T(8,128)(2,1)} %refs_0_.3, bf16[64,8192]{1,0:T(8,128)(2,1)} %collective-permute-done.6.refs_1_, bf16[64,8192]{1,0:T(8,128)(2,1)} %collective-permute-done.7.refs_2_, ...), custom_call_target="tpu_custom_call" | custom-call | flops 2147483648 | bytes 30000000 | tf_op jit(solution)/shard_map/pallas_call | solution.py:129
  94.8 23.7 %collective-permute-done.14.slots_ref = s32[3,128]{1,0:T(4,128)S(1)} collective-permute-done((s32[3,128]{1,0:T(4,128)S(1)}, s32[3,128]{1,0:T(4,128)S(1)}, u32[]{:S(2)}, u32[]{:S(2)}) %collective-permute-start.14) | collective-permute-done | bytes 1568 | tf_op jit(solution)/shard_map/ppermute | solution.py:158
  119.1 13.5 %shard_map.68.refs_3_ = f32[128,128,128]{2,1,0:T(8,128)} custom-call(s32[7]{0:T(128)} %stack.40.meta, s32[3,128]{1,0:T(4,128)} %copy-done.7, bf16[128,8192]{1,0:T(8,128)(2,1)} %refs_0_.3, bf16[64,8192]{1,0:T(8,128)(2,1)} %collective-permute-done.6.refs_1_, bf16[64,8192]{1,0:T(8,128)(2,1)} %collective-permute-done.7.refs_2_, ...), custom_call_target="tpu_custom_call" | custom-call | flops 1610612736 | bytes 30000000 | tf_op jit(solution)/shard_map/pallas_call | solution.py:129
  134.3 11.6 %shard_map.69 = (f32[64,128,128]{2,1,0:T(8,128)}, f32[64,128,128]{2,1,0:T(8,128)}) custom-call(s32[7]{0:T(128)} %stack.40.meta, s32[3,128]{1,0:T(4,128)} %copy-done.7, bf16[64,8192]{1,0:T(8,128)(2,1)} %copy-done.1, bf16[64,8192]{1,0:T(8,128)(2,1)} %copy-done, bf16[128,3328]{1,0:T(8,128)(2,1)} %collective-permute-done.15.refs_2_, ...), custom_call_target="tpu_custom_call" | custom-call | flops 536870912 | bytes 30000000 | tf_op jit(solution)/shard_map/pallas_call | solution.py:129
  146.0 3.2 %add_multiply_fusion = f32[64,128,128]{2,1,0:T(8,128)S(1)} fusion(f32[64,128,128]{2,1,0:T(8,128)S(1)} %copy-done.2, f32[64,128,128]{2,1,0:T(8,128)} %collective-permute-done.12, f32[]{:T(128)} %bitcast.7), kind=kLoop, calls=%fused_computation.2 | loop fusion | flops 2097152 | bytes 12582916 | tf_op jit(solution)/shard_map/mul | solution.py:198
  150.0 3.3 %collective-permute-done.19 = f32[64,128,128]{2,1,0:T(8,128)S(1)} collective-permute-done((f32[64,128,128]{2,1,0:T(8,128)}, f32[64,128,128]{2,1,0:T(8,128)S(1)}, u32[]{:S(2)}, u32[]{:S(2)}) %collective-permute-start.19) | collective-permute-done | bytes 4194336 | tf_op jit(solution)/shard_map/ppermute | solution.py:158
  156.4 20.7 %collective-permute-done.13 = f16[32,128,128]{2,1,0:T(8,128)(2,1)S(1)} collective-permute-done((f16[32,128,128]{2,1,0:T(8,128)(2,1)S(1)}, f16[32,128,128]{2,1,0:T(8,128)(2,1)S(1)}, u32[]{:S(2)}, u32[]{:S(2)}) %collective-permute-start.13) | collective-permute-done | bytes 1048608 | tf_op jit(solution)/shard_map/ppermute | solution.py:158
  177.1 21.1 %collective-permute-done.20 = f16[32,128,128]{2,1,0:T(8,128)(2,1)S(1)} collective-permute-done((f16[32,128,128]{2,1,0:T(8,128)(2,1)S(1)}, f16[32,128,128]{2,1,0:T(8,128)(2,1)S(1)}, u32[]{:S(2)}, u32[]{:S(2)}) %collective-permute-start.20) | collective-permute-done | bytes 1048608 | tf_op jit(solution)/shard_map/ppermute | solution.py:158
  207.6 4.8 %collective-permute-done.22 = f16[4,128,128]{2,1,0:T(8,128)(2,1)S(1)} collective-permute-done((f16[4,128,128]{2,1,0:T(8,128)(2,1)S(1)}, f16[4,128,128]{2,1,0:T(8,128)(2,1)S(1)}, u32[]{:S(2)}, u32[]{:S(2)}) %collective-permute-start.22) | collective-permute-done | bytes 131104 | tf_op jit(solution)/shard_map/ppermute | solution.py:158
  214.9 3.7 %collective-permute-start.23 = (f16[4,128,128]{2,1,0:T(8,128)(2,1)S(1)}, f16[4,128,128]{2,1,0:T(8,128)(2,1)S(1)}, u32[]{:S(2)}, u32[]{:S(2)}) collective-permute-start(f16[4,128,128]{2,1,0:T(8,128)(2,1)S(1)} %get-tuple-element.37), channel_id=1, source_target_pairs={{0,48},{8,56},{16,64},{24,72},{32,80},{40,88},{48,96},{56,104},{64... | collective-permute-start | bytes 393224 | tf_op jit(solution)/shard_map/ppermute | solution.py:158
  223.5 4.6 %collective-permute-done.23 = f16[4,128,128]{2,1,0:T(8,128)(2,1)S(1)} collective-permute-done((f16[4,128,128]{2,1,0:T(8,128)(2,1)S(1)}, f16[4,128,128]{2,1,0:T(8,128)(2,1)S(1)}, u32[]{:S(2)}, u32[]{:S(2)}) %collective-permute-start.23) | collective-permute-done | bytes 131104 | tf_op jit(solution)/shard_map/ppermute | solution.py:158
  229.5 16.9 %all_to_all.10 = f32[32,8,128]{2,1,0:T(8,128)S(1)} all-to-all(f32[32,8,128]{2,1,0:T(8,128)S(1)} %broadcast_in_dim_broadcast_in_dim_broadcast_in_dim.3), channel_id=1, replica_groups=mesh['dp'=32,'tensor'=8] {'dp'}, dimensions={0} | all-to-all | bytes 262144 | tf_op jit(solution)/shard_map/all_to_all | solution.py:218
  246.5 10.9 %all_to_all.11 = f32[8,8,128]{2,1,0:T(8,128)S(1)} all-to-all(f32[8,8,128]{2,1,0:T(8,128)S(1)} %broadcast_in_dim.5), channel_id=1, replica_groups=mesh['dp'=32,'tensor'=8] {'tensor'}, dimensions={0} | all-to-all | bytes 65536 | tf_op jit(solution)/shard_map/all_to_all | solution.py:218
  (86 shorter events, 44.5 us)
Async XLA Ops:
  3.0 26.9 %collective-permute-start.9 = (bf16[64,8192]{1,0:T(8,128)(2,1)}, bf16[64,8192]{1,0:T(8,128)(2,1)S(1)}, u32[]{:S(2)}, u32[]{:S(2)}) collective-permute-start(bf16[64,8192]{1,0:T(8,128)(2,1)} %get-tuple-element.29), channel_id=1, source_target_pairs={{0,6},{1,7},{2,0},{3,1},{4,2},{5,3},{6,4},{7,5},{8,14},{9,15},{10,... | collective-permute-start | bytes 3145736 | tf_op jit(solution)/shard_map/ppermute | solution.py:158
  6.1 27.6 %collective-permute-start.6 = (bf16[64,8192]{1,0:T(8,128)(2,1)}, bf16[64,8192]{1,0:T(8,128)(2,1)}, u32[]{:S(2)}, u32[]{:S(2)}) collective-permute-start(bf16[64,8192]{1,0:T(8,128)(2,1)} %get-tuple-element.30), channel_id=1, source_target_pairs={{0,2},{1,3},{2,4},{3,5},{4,6},{5,7},{6,0},{7,1},{8,10},{9,11},{10,... | collective-permute-start | bytes 3145736 | tf_op jit(solution)/shard_map/ppermute | solution.py:158
  6.1 55.0 %collective-permute-start.7 = (bf16[64,8192]{1,0:T(8,128)(2,1)}, bf16[64,8192]{1,0:T(8,128)(2,1)}, u32[]{:S(2)}, u32[]{:S(2)}) collective-permute-start(bf16[64,8192]{1,0:T(8,128)(2,1)} %get-tuple-element.29), channel_id=1, source_target_pairs={{0,2},{1,3},{2,4},{3,5},{4,6},{5,7},{6,0},{7,1},{8,10},{9,11},{10,... | collective-permute-start | bytes 3145736 | tf_op jit(solution)/shard_map/ppermute | solution.py:158
  6.7 55.3 %collective-permute-start.8 = (bf16[64,8192]{1,0:T(8,128)(2,1)}, bf16[64,8192]{1,0:T(8,128)(2,1)}, u32[]{:S(2)}, u32[]{:S(2)}) collective-permute-start(bf16[64,8192]{1,0:T(8,128)(2,1)} %get-tuple-element.30), channel_id=1, source_target_pairs={{0,6},{1,7},{2,0},{3,1},{4,2},{5,3},{6,4},{7,5},{8,14},{9,15},{10,... | collective-permute-start | bytes 3145736 | tf_op jit(solution)/shard_map/ppermute | solution.py:158
  14.4 19.2 %collective-permute-start = (f32[8,128]{1,0:T(8,128)S(1)}, f32[8,128]{1,0:T(8,128)S(1)}, u32[]{:S(2)}, u32[]{:S(2)}) collective-permute-start(f32[8,128]{1,0:T(8,128)S(1)} %broadcast_in_dim.4), channel_id=1, source_target_pairs={{0,1},{1,0},{2,3},{3,2},{4,5},{5,4},{6,7},{7,6},{8,9},{9,8},{10,11... | collective-permute-start | bytes 12296 | tf_op jit(solution)/shard_map/ppermute | solution.py:158
  29.9 43.7 %collective-permute-start.11 = (bf16[64,8192]{1,0:T(8,128)(2,1)S(1)}, bf16[64,8192]{1,0:T(8,128)(2,1)S(1)}, u32[]{:S(2)}, u32[]{:S(2)}) collective-permute-start(bf16[64,8192]{1,0:T(8,128)(2,1)S(1)} %collective-permute-done.9.refs_4_), channel_id=1, source_target_pairs={{0,6},{1,7},{2,0},{3,1},{4,2},{5,3},{6,4},{7,5},{8,14},{9,15},{10,... | collective-permute-start | bytes 3145736 | tf_op jit(solution)/shard_map/ppermute | solution.py:158
  33.6 43.4 %collective-permute-start.10 = (bf16[64,8192]{1,0:T(8,128)(2,1)}, bf16[64,8192]{1,0:T(8,128)(2,1)S(1)}, u32[]{:S(2)}, u32[]{:S(2)}) collective-permute-start(bf16[64,8192]{1,0:T(8,128)(2,1)} %collective-permute-done.6.refs_1_), channel_id=1, source_target_pairs={{0,2},{1,3},{2,4},{3,5},{4,6},{5,7},{6,0},{7,1},{8,10},{9,11},{10,... | collective-permute-start | bytes 3145736 | tf_op jit(solution)/shard_map/ppermute | solution.py:158
  48.5 11.4 %collective-permute-start.5 = (f32[8,128]{1,0:T(8,128)S(1)}, f32[8,128]{1,0:T(8,128)S(1)}, u32[]{:S(2)}, u32[]{:S(2)}) collective-permute-start(f32[8,128]{1,0:T(8,128)S(1)} %max.27), channel_id=1, source_target_pairs={{0,64},{8,72},{16,80},{24,88},{32,96},{40,104},{48,112},{56,120},{... | collective-permute-start | bytes 12296 | tf_op jit(solution)/shard_map/ppermute | solution.py:158
  59.9 58.7 %collective-permute-start.18 = (bf16[128,3328]{1,0:T(8,128)(2,1)}, bf16[128,3328]{1,0:T(8,128)(2,1)}, u32[]{:S(2)}, u32[]{:S(2)}) collective-permute-start(bf16[128,3328]{1,0:T(8,128)(2,1)} %get-tuple-element.23), channel_id=1, source_target_pairs={{0,1},{1,0},{2,3},{3,2},{4,5},{5,4},{6,7},{7,6},{8,9},{9,8},{10,11... | collective-permute-start | bytes 2555912 | tf_op jit(solution)/shard_map/ppermute | solution.py:158
  61.1 57.5 %collective-permute-start.16 = (bf16[128,3328]{1,0:T(8,128)(2,1)}, bf16[128,3328]{1,0:T(8,128)(2,1)}, u32[]{:S(2)}, u32[]{:S(2)}) collective-permute-start(bf16[128,3328]{1,0:T(8,128)(2,1)} %get-tuple-element.24), channel_id=1, source_target_pairs={{0,1},{1,0},{2,3},{3,2},{4,5},{5,4},{6,7},{7,6},{8,9},{9,8},{10,11... | collective-permute-start | bytes 2555912 | tf_op jit(solution)/shard_map/ppermute | solution.py:158
  61.9 56.6 %collective-permute-start.17 = (bf16[128,3328]{1,0:T(8,128)(2,1)}, bf16[128,3328]{1,0:T(8,128)(2,1)}, u32[]{:S(2)}, u32[]{:S(2)}) collective-permute-start(bf16[128,3328]{1,0:T(8,128)(2,1)} %get-tuple-element.26), channel_id=1, source_target_pairs={{0,1},{1,0},{2,3},{3,2},{4,5},{5,4},{6,7},{7,6},{8,9},{9,8},{10,11... | collective-permute-start | bytes 2555912 | tf_op jit(solution)/shard_map/ppermute | solution.py:158
  73.6 44.9 %collective-permute-start.14 = (s32[3,128]{1,0:T(4,128)S(1)}, s32[3,128]{1,0:T(4,128)S(1)}, u32[]{:S(2)}, u32[]{:S(2)}) collective-permute-start(s32[3,128]{1,0:T(4,128)S(1)} %add_add_fusion.slots_ref), channel_id=1, source_target_pairs={{0,1},{1,0},{2,3},{3,2},{4,5},{5,4},{6,7},{7,6},{8,9},{9,8},{10,11... | collective-permute-start | bytes 4616 | tf_op jit(solution)/shard_map/ppermute | solution.py:158
  77.0 57.2 %collective-permute-start.15 = (bf16[128,3328]{1,0:T(8,128)(2,1)}, bf16[128,3328]{1,0:T(8,128)(2,1)}, u32[]{:S(2)}, u32[]{:S(2)}) collective-permute-start(bf16[128,3328]{1,0:T(8,128)(2,1)} %get-tuple-element.25), channel_id=1, source_target_pairs={{0,1},{1,0},{2,3},{3,2},{4,5},{5,4},{6,7},{7,6},{8,9},{9,8},{10,11... | collective-permute-start | bytes 2555912 | tf_op jit(solution)/shard_map/ppermute | solution.py:158
  118.5 27.4 %collective-permute-start.12 = (f32[64,128,128]{2,1,0:T(8,128)}, f32[64,128,128]{2,1,0:T(8,128)}, u32[]{:S(2)}, u32[]{:S(2)}) collective-permute-start(f32[64,128,128]{2,1,0:T(8,128)} %get-tuple-element.14), channel_id=1, source_target_pairs={{0,8},{8,0},{16,24},{24,16},{32,40},{40,32},{48,56},{56,48},{64,72... | collective-permute-start | bytes 12582920 | tf_op jit(solution)/shard_map/ppermute | solution.py:158
  149.4 27.7 %collective-permute-start.13 = (f16[32,128,128]{2,1,0:T(8,128)(2,1)S(1)}, f16[32,128,128]{2,1,0:T(8,128)(2,1)S(1)}, u32[]{:S(2)}, u32[]{:S(2)}) collective-permute-start(f16[32,128,128]{2,1,0:T(8,128)(2,1)S(1)} %slice_convert_fusion), channel_id=1, source_target_pairs={{0,128},{8,136},{16,144},{24,152},{32,160},{40,168},{48,176},{56,1... | collective-permute-start | bytes 3145736 | tf_op jit(solution)/shard_map/ppermute | solution.py:158
  155.1 43.0 %collective-permute-start.20 = (f16[32,128,128]{2,1,0:T(8,128)(2,1)S(1)}, f16[32,128,128]{2,1,0:T(8,128)(2,1)S(1)}, u32[]{:S(2)}, u32[]{:S(2)}) collective-permute-start(f16[32,128,128]{2,1,0:T(8,128)(2,1)S(1)} %get-tuple-element.27), channel_id=1, source_target_pairs={{0,1},{1,0},{2,3},{3,2},{4,5},{5,4},{6,7},{7,6},{8,9},{9,8},{10,11... | collective-permute-start | bytes 3145736 | tf_op jit(solution)/shard_map/ppermute | solution.py:158
  156.4 42.6 %collective-permute-start.21 = (f16[32,128,128]{2,1,0:T(8,128)(2,1)S(1)}, f16[32,128,128]{2,1,0:T(8,128)(2,1)S(1)}, u32[]{:S(2)}, u32[]{:S(2)}) collective-permute-start(f16[32,128,128]{2,1,0:T(8,128)(2,1)S(1)} %get-tuple-element.28), channel_id=1, source_target_pairs={{0,129},{1,128},{2,131},{3,130},{4,133},{5,132},{6,135},{7,134},{8... | collective-permute-start | bytes 3145736 | tf_op jit(solution)/shard_map/ppermute | solution.py:158
  200.0 12.4 %collective-permute-start.22 = (f16[4,128,128]{2,1,0:T(8,128)(2,1)S(1)}, f16[4,128,128]{2,1,0:T(8,128)(2,1)S(1)}, u32[]{:S(2)}, u32[]{:S(2)}) collective-permute-start(f16[4,128,128]{2,1,0:T(8,128)(2,1)S(1)} %get-tuple-element.31), channel_id=1, source_target_pairs={{0,64},{8,72},{16,80},{24,88},{32,96},{40,104},{48,112},{56,120},{... | collective-permute-start | bytes 393224 | tf_op jit(solution)/shard_map/ppermute | solution.py:158
  202.3 12.6 %collective-permute-start.28 = (f16[4,128,128]{2,1,0:T(8,128)(2,1)S(1)}, f16[4,128,128]{2,1,0:T(8,128)(2,1)S(1)}, u32[]{:S(2)}, u32[]{:S(2)}) collective-permute-start(f16[4,128,128]{2,1,0:T(8,128)(2,1)S(1)} %get-tuple-element.32), channel_id=1, source_target_pairs={{0,112},{8,120},{16,0},{24,8},{32,16},{40,24},{48,32},{56,40},{64,... | collective-permute-start | bytes 393224 | tf_op jit(solution)/shard_map/ppermute | solution.py:158
  204.7 13.9 %collective-permute-start.27 = (f16[4,128,128]{2,1,0:T(8,128)(2,1)S(1)}, f16[4,128,128]{2,1,0:T(8,128)(2,1)S(1)}, u32[]{:S(2)}, u32[]{:S(2)}) collective-permute-start(f16[4,128,128]{2,1,0:T(8,128)(2,1)S(1)} %get-tuple-element.33), channel_id=1, source_target_pairs={{0,16},{8,24},{16,32},{24,40},{32,48},{40,56},{48,64},{56,72},{64,... | collective-permute-start | bytes 393224 | tf_op jit(solution)/shard_map/ppermute | solution.py:158
  204.7 16.3 %collective-permute-start.26 = (f16[4,128,128]{2,1,0:T(8,128)(2,1)S(1)}, f16[4,128,128]{2,1,0:T(8,128)(2,1)S(1)}, u32[]{:S(2)}, u32[]{:S(2)}) collective-permute-start(f16[4,128,128]{2,1,0:T(8,128)(2,1)S(1)} %get-tuple-element.34), channel_id=1, source_target_pairs={{0,96},{8,104},{16,112},{24,120},{32,0},{40,8},{48,16},{56,24},{64... | collective-permute-start | bytes 393224 | tf_op jit(solution)/shard_map/ppermute | solution.py:158
  207.2 13.8 %collective-permute-start.25 = (f16[4,128,128]{2,1,0:T(8,128)(2,1)S(1)}, f16[4,128,128]{2,1,0:T(8,128)(2,1)S(1)}, u32[]{:S(2)}, u32[]{:S(2)}) collective-permute-start(f16[4,128,128]{2,1,0:T(8,128)(2,1)S(1)} %get-tuple-element.35), channel_id=1, source_target_pairs={{0,32},{8,40},{16,48},{24,56},{32,64},{40,72},{48,80},{56,88},{64,... | collective-permute-start | bytes 393224 | tf_op jit(solution)/shard_map/ppermute | solution.py:158
  212.5 11.0 %collective-permute-start.24 = (f16[4,128,128]{2,1,0:T(8,128)(2,1)S(1)}, f16[4,128,128]{2,1,0:T(8,128)(2,1)S(1)}, u32[]{:S(2)}, u32[]{:S(2)}) collective-permute-start(f16[4,128,128]{2,1,0:T(8,128)(2,1)S(1)} %get-tuple-element.36), channel_id=1, source_target_pairs={{0,80},{8,88},{16,96},{24,104},{32,112},{40,120},{48,0},{56,8},{64... | collective-permute-start | bytes 393224 | tf_op jit(solution)/shard_map/ppermute | solution.py:158
  214.9 13.2 %collective-permute-start.23 = (f16[4,128,128]{2,1,0:T(8,128)(2,1)S(1)}, f16[4,128,128]{2,1,0:T(8,128)(2,1)S(1)}, u32[]{:S(2)}, u32[]{:S(2)}) collective-permute-start(f16[4,128,128]{2,1,0:T(8,128)(2,1)S(1)} %get-tuple-element.37), channel_id=1, source_target_pairs={{0,48},{8,56},{16,64},{24,72},{32,80},{40,88},{48,96},{56,104},{64... | collective-permute-start | bytes 393224 | tf_op jit(solution)/shard_map/ppermute | solution.py:158
  (15 other events, 313.7 us)

commit v2 on v1

--- a/solution.py
+++ b/solution.py
@@ -10,6 +10,7 @@
 
 
 UNROLL = 8
+CHUNKS = 4
 X_SWAP = [(t, t ^ 1) for t in range(8)]
 Y_UP = [(t, (t + 2) % 8) for t in range(8)]
 Y_DOWN = [(t, (t + 6) % 8) for t in range(8)]
@@ -42,7 +43,6 @@
     at += len(outs_hbm)
     x_buf, g_buf, o_buf, in_sem, out_sem = refs[at:]
     places = o_buf.shape[0]
-    half = places // 2
     copies = []
     row = 0
     for index, size in enumerate(plan):
@@ -59,9 +59,18 @@
             pltpu.make_async_copy(block, g_buf.at[pl.ds(row, size), :], in_sem.at[len(copies)])
         )
         row += size
+    piece = places // CHUNKS
+    loads = []
     if with_acc:
-        copies.append(pltpu.make_async_copy(acc_hbm, o_buf, in_sem.at[len(copies)]))
-    for copy in copies:
+        loads = [
+            pltpu.make_async_copy(
+                acc_hbm.at[pl.ds(i * piece, piece)],
+                o_buf.at[pl.ds(i * piece, piece)],
+                in_sem.at[len(copies) + i],
+            )
+            for i in range(CHUNKS)
+        ]
+    for copy in copies + loads:
         copy.start()
     for copy in copies:
         copy.wait()
@@ -99,19 +108,22 @@
             o_buf[step * UNROLL + u] = values[u]
         return carry
 
-    if split:
-        targets = outs_hbm
-    else:
-        targets = [outs_hbm[0].at[pl.ds(0, half)], outs_hbm[0].at[pl.ds(half, half)]]
-    outs = [
-        pltpu.make_async_copy(o_buf.at[pl.ds(i * half, half)], targets[i], out_sem.at[i]) for i in range(2)
-    ]
-    lax.fori_loop(0, half // UNROLL, trip, 0)
-    outs[0].start()
-    lax.fori_loop(half // UNROLL, places // UNROLL, trip, 0)
-    outs[1].start()
-    outs[0].wait()
-    outs[1].wait()
+    stores = []
+    for i in range(CHUNKS):
+        target = outs_hbm[i * len(outs_hbm) // CHUNKS]
+        start = i % (CHUNKS // len(outs_hbm)) * piece
+        stores.append(
+            pltpu.make_async_copy(
+                o_buf.at[pl.ds(i * piece, piece)], target.at[pl.ds(start, piece)], out_sem.at[i]
+            )
+        )
+    for i in range(CHUNKS):
+        if loads:
+            loads[i].wait()
+        lax.fori_loop(i * piece // UNROLL, (i + 1) * piece // UNROLL, trip, 0)
+        stores[i].start()
+    for store in stores:
+        store.wait()
 
 
 def partial_grads(meta, slot_table, pieces, grads, sources, split, acc=None):
@@ -135,8 +147,8 @@
             pltpu.VMEM((depth, pieces[0].shape[1]), jnp.bfloat16),
             pltpu.VMEM((depth, grads[0].shape[1]), jnp.bfloat16),
             pltpu.VMEM(block, jnp.float32),
-            pltpu.SemaphoreType.DMA((len(operands),)),
-            pltpu.SemaphoreType.DMA((2,)),
+            pltpu.SemaphoreType.DMA((len(operands) + CHUNKS,)),
+            pltpu.SemaphoreType.DMA((CHUNKS,)),
         ],
         compiler_params=pltpu.CompilerParams(vmem_limit_bytes=56 * 1024 * 1024),
         cost_estimate=pl.CostEstimate(
@@ -161,57 +173,58 @@
         [lax.bitwise_and(dp, 1), lax.bitwise_and(dp >> 1, 7), dp >> 4, *around(tp)]
     ).astype(jnp.int32)
     table = jnp.stack([block_rows, block_cols, jnp.broadcast_to(block_count, (places,))])
-    part_a, part_b = tokens[:64], tokens[64:]
-    theirs = [lax.dynamic_slice_in_dim(out_grad, chunk * 128, 128, 0) for chunk in around(across)]
-    below_a, above_b = move(part_a, Y_UP), move(part_b, Y_DOWN)
+    chunks = around(across)
+
+    def theirs(source, index):
+        return lax.dynamic_slice_in_dim(source, chunks[index] * 128, 128, 0)
+
+    below, above = move(tokens, Y_UP), move(tokens, Y_DOWN)
+    first_rows, later = lax.optimization_barrier((theirs(out_grad, 0), out_grad))
+    g_own = move(first_rows, X_SWAP)
     table_x = move(table, X_SWAP)
-    top = jnp.broadcast_to(jnp.max(jnp.abs(out_grad)).astype(jnp.float32), (8, 128))
+    g_below, g_above, g_far = (
+        move(theirs(later, i), X_SWAP) for i in (1, 2, 3)
+    )
+    far_a, far_b = move(below[:64], Y_UP), move(above[64:], Y_DOWN)
+    top = jnp.broadcast_to(jnp.max(jnp.abs(later)).astype(jnp.float32), (8, 128))
     for pairs, axis in (
-        (X_SWAP, "tensor"),
-        (X_HI_SWAP, "dp"),
         (CORE_SWAP, "dp"),
         (z_swap(1), "dp"),
         (z_swap(2), "dp"),
         (z_swap(4), "dp"),
+        (X_SWAP, "tensor"),
+        (X_HI_SWAP, "dp"),
     ):
         top = jnp.maximum(top, move(top, pairs, axis))
     top = jnp.clip(top[0, 0], 1e-30, 1e37)
-    g_own = move(theirs[0], X_SWAP)
-    below_b, above_a = move(part_b, Y_UP), move(part_a, Y_DOWN)
-    g_below = move(theirs[1], X_SWAP)
-    g_above = move(theirs[2], X_SWAP)
-    g_far = move(theirs[3], X_SWAP)
-    far_a, far_b = move(below_a, Y_UP), move(above_b, Y_DOWN)
     meta_late, shrink, grow = lax.optimization_barrier((meta, 0.25 / top, 4.0 * top))
 
-    (acc,) = partial_grads(
-        meta, table_x, (tokens, below_a, below_b, above_a, above_b),
-        (g_own, g_below, g_above), (None, None, None), False,
-    )
-    send, keep = partial_grads(
-        meta_late, table, (tokens, below_a, below_b, above_a, above_b, far_a, far_b),
-        (out_grad, out_grad, out_grad, out_grad), (OWN, BELOW, ABOVE, FAR), True,
-    )
-    send_x, keep_x = partial_grads(meta, table_x, (far_a, far_b), (g_far,), (None,), True, acc)
+    near = (tokens, below, above)
+    far = (far_a, far_b)
+    (acc,) = partial_grads(meta, table, near, (out_grad,) * 3, (OWN, BELOW, ABOVE), False)
+    (acc_x,) = partial_grads(meta, table_x, near, (g_own, g_below, g_above), (None,) * 3, False)
+    send, keep = partial_grads(meta_late, table, far, (out_grad,), (FAR,), True, acc)
+    send_x, keep_x = partial_grads(meta_late, table_x, far, (g_far,), (None,), True, acc_x)
+
     share = delta.shape[1]
     quarter = places // 4
-    ours = (keep + move(send, CORE_SWAP, "dp")) * shrink
-    far_half = move(ours[quarter:].astype(jnp.float16), X_HI_SWAP, "dp")
+
+    def z_sum(value):
+        packed = value.astype(jnp.float16)
+        total = value[:share]
+        for k in (4, 3, 5, 2, 6, 1, 7):
+            got = move(packed[share * k : share * (k + 1)], z_shift(k), "dp")
+            total = total + got.astype(jnp.float32)
+        return total
+
+    own_back = move(send, CORE_SWAP, "dp")
+    own_sum = (keep + own_back) * shrink
     other = ((keep_x + move(send_x, CORE_SWAP, "dp")) * shrink).astype(jnp.float16)
     near_x = move(other[:quarter], X_SWAP)
     far_x = move(other[quarter:], DIAGONAL, ("dp", "tensor"))
-    ours = (
-        ours[:quarter]
-        + far_half.astype(jnp.float32)
-        + near_x.astype(jnp.float32)
-        + far_x.astype(jnp.float32)
-    )
-    packed = ours.astype(jnp.float16)
-    grads = ours[:share]
-    for k in (4, 3, 5, 2, 6, 1, 7):
-        got = move(packed[share * k : share * (k + 1)], z_shift(k), "dp")
-        grads = grads + got.astype(jnp.float32)
-    grads = grads * grow
+    from_far = move(z_sum(own_sum[quarter:]), X_HI_SWAP, "dp")
+    ours = own_sum[:quarter] + near_x.astype(jnp.float32) + far_x.astype(jnp.float32)
+    grads = (z_sum(ours) + from_far) * grow
     square_sum = jnp.broadcast_to(jnp.sum(grads * grads), (8, 128))
     for axis, size in (("dp", 32), ("tensor", 8)):
         spread = jnp.broadcast_to(square_sum[None], (size, 8, 128))

time: 261 us -> 252 us (0.966)
  waiting for transfers between devices: 119 us -> 77.4 us
  starting transfers between devices: 45.1 us -> 72.8 us
  Pallas kernels: 41.7 us -> 44.9 us
  local copies, waits for them, and re-layouts: 11.5 us -> 14.2 us
    ppermute x29 -> x34, waiting for transfers between devices: 119 us -> 77.4 us  [move(): return lax.ppermute(value, axis, pairs)]
    ppermute x29 -> x34, starting transfers between devices: 45.1 us -> 72.8 us  [move(): return lax.ppermute(value, axis, pairs)]
    mul x1 -> x0, other arithmetic: 3.2 us -> none  [on_device(): ours = (keep + move(send, CORE_SWAP, 'dp')) * shrink]
    pallas_call x3 -> x4, Pallas kernels: 41.7 us -> 44.9 us  [partial_grads(): pl.pallas_call(functools.partial(grads_kernel, plan, depths, split, acc i...]
    dynamic_slice x1 -> x2, local copies, waits for them, and re-layouts: 3.81 us -> 5.35 us  [theirs(): return lax.dynamic_slice_in_dim(source, chunks[index] * 128, 128, 0)]
  transfers between devices with their start and end apart: 29 -> 34, of which waited for: 18 -> 19; matrix products, arithmetic and copies ran while one was open for 6% -> 9% of each run, Pallas kernels for 16% -> 14%
where the time goes in v2:
time: 252 us; the launch traced here: 250 us
  waiting for transfers between devices  77.4 us (31%)
  starting transfers between devices  72.8 us (29%)
  Pallas kernels  44.9 us (18%)
  blocking collectives  26.8 us (11%)
  local copies, waits for them, and re-layouts  14.2 us (6%)
  other arithmetic  11.5 us (5%)
  between operations  2.88 us (1%)
    ppermute x34, waiting for transfers between devices, move(): return lax.ppermute(value, axis, pairs)  77.4 us
    ppermute x34, starting transfers between devices, move(): return lax.ppermute(value, axis, pairs)  72.8 us
    pallas_call x4, Pallas kernels, partial_grads(): pl.pallas_call(functools.partial(grads_kernel, plan, depths, split, acc i...  44.9 us
    all_to_all x2, blocking collectives, on_device(): square_sum = jnp.sum(lax.all_to_all(spread, axis, 0, 0, tiled=True), axis=0)  26.8 us
    dynamic_slice x2, local copies, waits for them, and re-layouts, theirs(): return lax.dynamic_slice_in_dim(source, chunks[index] * 128, 128, 0)  5.35 us
  transfers between devices with their start and end apart: 34, of which 19 were waited for; matrix products, arithmetic and copies ran while one was open for 9% of the time, Pallas kernels for 14%

profile of v2, /device:TPU:4, one launch (start us, length us, event | category | flops | bytes accessed | tf_op | source)
XLA Modules:
  0.0 250.4 jit_solution(11673521298187705731)
XLA Ops:
  5.4 3.2 %constant_dynamic-slice_fusion = (bf16[128,3328]{1,0:T(8,128)(2,1)}, bf16[128,3328]{1,0:T(8,128)(2,1)}, bf16[128,3328]{1,0:T(8,128)(2,1)}) fusion(bf16[1024,3328]{1,0:T(8,128)(2,1)} %refs_2_.1, s32[]{:T(128)S(6)} %select_n.15, s32[]{:T(128)S(6)} %select_n.14, s32[]{:T(128)S(6)} %select_n.13), kind=kLoop, calls=%fused_computation.25 | loop fusion | bytes 5111820 | tf_op jit(solution)/shard_map/dynamic_slice | solution.py:179
  9.8 4.4 %abs_reduce_fusion = bf16[]{:T(256)} fusion(bf16[1024,3328]{1,0:T(8,128)(2,1)} %refs_2_.1), kind=kLoop, calls=%fused_computation | loop fusion | flops 6815743 | bytes 6815746 | tf_op jit(solution)/shard_map/reduce_max | solution.py:189
  19.7 3.3 %collective-permute-start.2 = (f32[8,128]{1,0:T(8,128)S(1)}, f32[8,128]{1,0:T(8,128)S(1)}, u32[]{:S(2)}, u32[]{:S(2)}) collective-permute-start(f32[8,128]{1,0:T(8,128)S(1)} %fusion.22), channel_id=1, source_target_pairs={{0,32},{8,40},{16,48},{24,56},{32,0},{40,8},{48,16},{56,24},{64,96... | collective-permute-start | bytes 12296 | tf_op jit(solution)/shard_map/ppermute | solution.py:170
  24.6 6.8 %collective-permute-start.3 = (f32[8,128]{1,0:T(8,128)S(1)}, f32[8,128]{1,0:T(8,128)S(1)}, u32[]{:S(2)}, u32[]{:S(2)}) collective-permute-start(f32[8,128]{1,0:T(8,128)S(1)} %max.25), channel_id=1, source_target_pairs={{0,64},{8,72},{16,80},{24,88},{32,96},{40,104},{48,112},{56,120},{... | collective-permute-start | bytes 12296 | tf_op jit(solution)/shard_map/ppermute | solution.py:170
  37.4 11.4 %collective-permute-done.6.refs_1_ = bf16[128,8192]{1,0:T(8,128)(2,1)S(1)} collective-permute-done((bf16[128,8192]{1,0:T(8,128)(2,1)}, bf16[128,8192]{1,0:T(8,128)(2,1)S(1)}, u32[]{:S(2)}, u32[]{:S(2)}) %collective-permute-start.6) | collective-permute-done | bytes 2097184 | tf_op jit(solution)/shard_map/ppermute | solution.py:170
  64.3 17.1 %collective-permute-done.15.refs_5_ = bf16[128,3328]{1,0:T(8,128)(2,1)} collective-permute-done((bf16[128,3328]{1,0:T(8,128)(2,1)}, bf16[128,3328]{1,0:T(8,128)(2,1)}, u32[]{:S(2)}, u32[]{:S(2)}) %collective-permute-start.15) | collective-permute-done | bytes 852000 | tf_op jit(solution)/shard_map/ppermute | solution.py:170
  81.3 18.3 %collective-permute-done.13.refs_3_ = bf16[128,3328]{1,0:T(8,128)(2,1)} collective-permute-done((bf16[128,3328]{1,0:T(8,128)(2,1)}, bf16[128,3328]{1,0:T(8,128)(2,1)}, u32[]{:S(2)}, u32[]{:S(2)}) %collective-permute-start.13) | collective-permute-done | bytes 852000 | tf_op jit(solution)/shard_map/ppermute | solution.py:170
  99.6 13.0 %shard_map.69.refs_3_ = f32[128,128,128]{2,1,0:T(8,128)} custom-call(s32[7]{0:T(128)} %stack.40.meta, s32[3,128]{1,0:T(4,128)} %copy-done.6, bf16[128,8192]{1,0:T(8,128)(2,1)} %refs_0_.3, bf16[128,8192]{1,0:T(8,128)(2,1)} %copy-done, bf16[128,8192]{1,0:T(8,128)(2,1)} %collective-permute-done.8.refs_2_, bf16[128,3328]{1,0:T(8,128)(2,1)} %collective-permute-done.13.refs_3_, ...), custom_call_target="tpu_custom_call" | custom-call | flops 1610612736 | bytes 30000000 | tf_op jit(solution)/shard_map/pallas_call | solution.py:141
  115.6 9.1 %shard_map.70 = (f32[64,128,128]{2,1,0:T(8,128)}, f32[64,128,128]{2,1,0:T(8,128)}) custom-call(s32[7]{0:T(128)} %stack.40.meta, s32[3,128]{1,0:T(4,128)} %copy-done.6, bf16[64,8192]{1,0:T(8,128)(2,1)} %copy-done.3, bf16[64,8192]{1,0:T(8,128)(2,1)} %collective-permute-done.9.refs_1_, bf16[128,3328]{1,0:T(8,128)(2,1)} %collective-permute-done.12.refs_2_, ...), custom_call_target="tpu_custom_call" | custom-call | flops 536870912 | bytes 30000000 | tf_op jit(solution)/shard_map/pallas_call | solution.py:141
  124.9 13.0 %shard_map.67.refs_3_ = f32[128,128,128]{2,1,0:T(8,128)} custom-call(s32[7]{0:T(128)} %stack.40.meta, s32[3,128]{1,0:T(4,128)} %copy-done.5, bf16[128,8192]{1,0:T(8,128)(2,1)} %refs_0_.3, bf16[128,8192]{1,0:T(8,128)(2,1)} %copy-done, bf16[128,8192]{1,0:T(8,128)(2,1)} %collective-permute-done.8.refs_2_, bf16[1024,3328]{1,0:T(8,128)(2,1)} %refs_2_.1, ...), custom_call_target="tpu_custom_call" | custom-call | flops 1610612736 | bytes 30000000 | tf_op jit(solution)/shard_map/pallas_call | solution.py:141
  137.9 9.7 %shard_map.68 = (f32[64,128,128]{2,1,0:T(8,128)}, f32[64,128,128]{2,1,0:T(8,128)}) custom-call(s32[7]{0:T(128)} %stack.40.meta, s32[3,128]{1,0:T(4,128)} %copy-done.5, bf16[64,8192]{1,0:T(8,128)(2,1)} %copy-done.3, bf16[64,8192]{1,0:T(8,128)(2,1)} %collective-permute-done.9.refs_1_, bf16[1024,3328]{1,0:T(8,128)(2,1)} %refs_2_.1, ...), custom_call_target="tpu_custom_call" | custom-call | flops 536870912 | bytes 30000000 | tf_op jit(solution)/shard_map/pallas_call | solution.py:141
  148.2 3.2 %multiply_convert_fusion = f16[64,128,128]{2,1,0:T(8,128)(2,1)S(1)} fusion(f32[64,128,128]{2,1,0:T(8,128)S(1)} %copy-done.2, f32[64,128,128]{2,1,0:T(8,128)} %collective-permute-done.16, f32[]{:T(128)} %bitcast.7), kind=kLoop, calls=%fused_computation.1 | loop fusion | flops 3145728 | bytes 10485764 | tf_op jit(solution)/shard_map/convert_element_type | solution.py:222
  156.8 7.3 %collective-permute-start.26 = (f16[4,128,128]{2,1,0:T(8,128)(2,1)S(1)}, f16[4,128,128]{2,1,0:T(8,128)(2,1)S(1)}, u32[]{:S(2)}, u32[]{:S(2)}) collective-permute-start(f16[4,128,128]{2,1,0:T(8,128)(2,1)S(1)} %get-tuple-element.34), channel_id=1, source_target_pairs={{0,64},{8,72},{16,80},{24,88},{32,96},{40,104},{48,112},{56,120},{... | collective-permute-start | bytes 393224 | tf_op jit(solution)/shard_map/ppermute | solution.py:170
  166.0 3.2 %collective-permute-start.28 = (f16[4,128,128]{2,1,0:T(8,128)(2,1)S(1)}, f16[4,128,128]{2,1,0:T(8,128)(2,1)S(1)}, u32[]{:S(2)}, u32[]{:S(2)}) collective-permute-start(f16[4,128,128]{2,1,0:T(8,128)(2,1)S(1)} %get-tuple-element.39), channel_id=1, source_target_pairs={{0,80},{8,88},{16,96},{24,104},{32,112},{40,120},{48,0},{56,8},{64... | collective-permute-start | bytes 393224 | tf_op jit(solution)/shard_map/ppermute | solution.py:170
  169.2 8.1 %collective-permute-start.29 = (f16[4,128,128]{2,1,0:T(8,128)(2,1)S(1)}, f16[4,128,128]{2,1,0:T(8,128)(2,1)S(1)}, u32[]{:S(2)}, u32[]{:S(2)}) collective-permute-start(f16[4,128,128]{2,1,0:T(8,128)(2,1)S(1)} %get-tuple-element.38), channel_id=1, source_target_pairs={{0,32},{8,40},{16,48},{24,56},{32,64},{40,72},{48,80},{56,88},{64,... | collective-permute-start | bytes 393224 | tf_op jit(solution)/shard_map/ppermute | solution.py:170
  178.6 5.9 %collective-permute-start.30 = (f16[4,128,128]{2,1,0:T(8,128)(2,1)S(1)}, f16[4,128,128]{2,1,0:T(8,128)(2,1)S(1)}, u32[]{:S(2)}, u32[]{:S(2)}) collective-permute-start(f16[4,128,128]{2,1,0:T(8,128)(2,1)S(1)} %get-tuple-element.37), channel_id=1, source_target_pairs={{0,96},{8,104},{16,112},{24,120},{32,0},{40,8},{48,16},{56,24},{64... | collective-permute-start | bytes 393224 | tf_op jit(solution)/shard_map/ppermute | solution.py:170
  184.5 3.2 %collective-permute-start.32 = (f16[4,128,128]{2,1,0:T(8,128)(2,1)S(1)}, f16[4,128,128]{2,1,0:T(8,128)(2,1)S(1)}, u32[]{:S(2)}, u32[]{:S(2)}) collective-permute-start(f16[4,128,128]{2,1,0:T(8,128)(2,1)S(1)} %get-tuple-element.35), channel_id=1, source_target_pairs={{0,112},{8,120},{16,0},{24,8},{32,16},{40,24},{48,32},{56,40},{64,... | collective-permute-start | bytes 393224 | tf_op jit(solution)/shard_map/ppermute | solution.py:170
  193.1 4.9 %collective-permute-start.19 = (f16[4,128,128]{2,1,0:T(8,128)(2,1)S(1)}, f16[4,128,128]{2,1,0:T(8,128)(2,1)S(1)}, u32[]{:S(2)}, u32[]{:S(2)}) collective-permute-start(f16[4,128,128]{2,1,0:T(8,128)(2,1)S(1)} %get-tuple-element.41), channel_id=1, source_target_pairs={{0,64},{8,72},{16,80},{24,88},{32,96},{40,104},{48,112},{56,120},{... | collective-permute-start | bytes 393224 | tf_op jit(solution)/shard_map/ppermute | solution.py:170
  199.7 3.4 %collective-permute-start.21 = (f16[4,128,128]{2,1,0:T(8,128)(2,1)S(1)}, f16[4,128,128]{2,1,0:T(8,128)(2,1)S(1)}, u32[]{:S(2)}, u32[]{:S(2)}) collective-permute-start(f16[4,128,128]{2,1,0:T(8,128)(2,1)S(1)} %get-tuple-element.46), channel_id=1, source_target_pairs={{0,80},{8,88},{16,96},{24,104},{32,112},{40,120},{48,0},{56,8},{64... | collective-permute-start | bytes 393224 | tf_op jit(solution)/shard_map/ppermute | solution.py:170
  203.3 3.9 %collective-permute-start.23 = (f16[4,128,128]{2,1,0:T(8,128)(2,1)S(1)}, f16[4,128,128]{2,1,0:T(8,128)(2,1)S(1)}, u32[]{:S(2)}, u32[]{:S(2)}) collective-permute-start(f16[4,128,128]{2,1,0:T(8,128)(2,1)S(1)} %get-tuple-element.44), channel_id=1, source_target_pairs={{0,96},{8,104},{16,112},{24,120},{32,0},{40,8},{48,16},{56,24},{64... | collective-permute-start | bytes 393224 | tf_op jit(solution)/shard_map/ppermute | solution.py:170
  207.2 7.3 %collective-permute-done.20 = f16[4,128,128]{2,1,0:T(8,128)(2,1)S(1)} collective-permute-done((f16[4,128,128]{2,1,0:T(8,128)(2,1)S(1)}, f16[4,128,128]{2,1,0:T(8,128)(2,1)S(1)}, u32[]{:S(2)}, u32[]{:S(2)}) %collective-permute-start.20) | collective-permute-done | bytes 131104 | tf_op jit(solution)/shard_map/ppermute | solution.py:170
  214.5 3.1 %collective-permute-done.22 = f16[4,128,128]{2,1,0:T(8,128)(2,1)S(1)} collective-permute-done((f16[4,128,128]{2,1,0:T(8,128)(2,1)S(1)}, f16[4,128,128]{2,1,0:T(8,128)(2,1)S(1)}, u32[]{:S(2)}, u32[]{:S(2)}) %collective-permute-start.22) | collective-permute-done | bytes 131104 | tf_op jit(solution)/shard_map/ppermute | solution.py:170
  221.5 17.3 %all_to_all.10 = f32[32,8,128]{2,1,0:T(8,128)S(1)} all-to-all(f32[32,8,128]{2,1,0:T(8,128)S(1)} %broadcast_in_dim_broadcast_in_dim_broadcast_in_dim.3), channel_id=1, replica_groups=mesh['dp'=32,'tensor'=8] {'dp'}, dimensions={0} | all-to-all | bytes 262144 | tf_op jit(solution)/shard_map/all_to_all | solution.py:231
  238.9 9.5 %all_to_all.11 = f32[8,8,128]{2,1,0:T(8,128)S(1)} all-to-all(f32[8,8,128]{2,1,0:T(8,128)S(1)} %broadcast_in_dim.5), channel_id=1, replica_groups=mesh['dp'=32,'tensor'=8] {'tensor'}, dimensions={0} | all-to-all | bytes 65536 | tf_op jit(solution)/shard_map/all_to_all | solution.py:231
  (98 shorter events, 57.9 us)
Async XLA Ops:
  0.0 48.9 %collective-permute-start.6 = (bf16[128,8192]{1,0:T(8,128)(2,1)}, bf16[128,8192]{1,0:T(8,128)(2,1)S(1)}, u32[]{:S(2)}, u32[]{:S(2)}) collective-permute-start(bf16[128,8192]{1,0:T(8,128)(2,1)} %refs_0_.3), channel_id=1, source_target_pairs={{0,2},{1,3},{2,4},{3,5},{4,6},{5,7},{6,0},{7,1},{8,10},{9,11},{10,... | collective-permute-start | bytes 6291464 | tf_op jit(solution)/shard_map/ppermute | solution.py:170
  1.6 48.7 %collective-permute-start.8 = (bf16[128,8192]{1,0:T(8,128)(2,1)}, bf16[128,8192]{1,0:T(8,128)(2,1)}, u32[]{:S(2)}, u32[]{:S(2)}) collective-permute-start(bf16[128,8192]{1,0:T(8,128)(2,1)} %refs_0_.3), channel_id=1, source_target_pairs={{0,6},{1,7},{2,0},{3,1},{4,2},{5,3},{6,4},{7,5},{8,14},{9,15},{10,... | collective-permute-start | bytes 6291464 | tf_op jit(solution)/shard_map/ppermute | solution.py:170
  8.6 52.6 %collective-permute-start.14 = (bf16[128,3328]{1,0:T(8,128)(2,1)}, bf16[128,3328]{1,0:T(8,128)(2,1)}, u32[]{:S(2)}, u32[]{:S(2)}) collective-permute-start(bf16[128,3328]{1,0:T(8,128)(2,1)} %get-tuple-element.30), channel_id=1, source_target_pairs={{0,1},{1,0},{2,3},{3,2},{4,5},{5,4},{6,7},{7,6},{8,9},{9,8},{10,11... | collective-permute-start | bytes 2555912 | tf_op jit(solution)/shard_map/ppermute | solution.py:170
  36.6 23.8 %collective-permute-start.5 = (f32[8,128]{1,0:T(8,128)S(1)}, f32[8,128]{1,0:T(8,128)S(1)}, u32[]{:S(2)}, u32[]{:S(2)}) collective-permute-start(f32[8,128]{1,0:T(8,128)S(1)} %max.27), channel_id=1, source_target_pairs={{0,128},{8,136},{16,144},{24,152},{32,160},{40,168},{48,176},{56,1... | collective-permute-start | bytes 12296 | tf_op jit(solution)/shard_map/ppermute | solution.py:170
  50.0 64.6 %collective-permute-start.7 = (bf16[64,8192]{1,0:T(8,128)(2,1)}, bf16[64,8192]{1,0:T(8,128)(2,1)S(1)}, u32[]{:S(2)}, u32[]{:S(2)}) collective-permute-start(bf16[64,8192]{1,0:T(8,128)(2,1)} %slice.102), channel_id=1, source_target_pairs={{0,2},{1,3},{2,4},{3,5},{4,6},{5,7},{6,0},{7,1},{8,10},{9,11},{10,... | collective-permute-start | bytes 3145736 | tf_op jit(solution)/shard_map/ppermute | solution.py:170
  52.6 62.1 %collective-permute-start.9 = (bf16[64,8192]{1,0:T(8,128)(2,1)}, bf16[64,8192]{1,0:T(8,128)(2,1)}, u32[]{:S(2)}, u32[]{:S(2)}) collective-permute-start(bf16[64,8192]{1,0:T(8,128)(2,1)} %slice.103), channel_id=1, source_target_pairs={{0,6},{1,7},{2,0},{3,1},{4,2},{5,3},{6,4},{7,5},{8,14},{9,15},{10,... | collective-permute-start | bytes 3145736 | tf_op jit(solution)/shard_map/ppermute | solution.py:170
  59.2 22.1 %collective-permute-start.15 = (bf16[128,3328]{1,0:T(8,128)(2,1)}, bf16[128,3328]{1,0:T(8,128)(2,1)}, u32[]{:S(2)}, u32[]{:S(2)}) collective-permute-start(bf16[128,3328]{1,0:T(8,128)(2,1)} %get-tuple-element.29), channel_id=1, source_target_pairs={{0,1},{1,0},{2,3},{3,2},{4,5},{5,4},{6,7},{7,6},{8,9},{9,8},{10,11... | collective-permute-start | bytes 2555912 | tf_op jit(solution)/shard_map/ppermute | solution.py:170
  60.4 39.2 %collective-permute-start.13 = (bf16[128,3328]{1,0:T(8,128)(2,1)}, bf16[128,3328]{1,0:T(8,128)(2,1)}, u32[]{:S(2)}, u32[]{:S(2)}) collective-permute-start(bf16[128,3328]{1,0:T(8,128)(2,1)} %constant_dynamic-slice_fusion.3), channel_id=1, source_target_pairs={{0,1},{1,0},{2,3},{3,2},{4,5},{5,4},{6,7},{7,6},{8,9},{9,8},{10,11... | collective-permute-start | bytes 2555912 | tf_op jit(solution)/shard_map/ppermute | solution.py:170
  61.2 53.4 %collective-permute-start.12 = (bf16[128,3328]{1,0:T(8,128)(2,1)}, bf16[128,3328]{1,0:T(8,128)(2,1)}, u32[]{:S(2)}, u32[]{:S(2)}) collective-permute-start(bf16[128,3328]{1,0:T(8,128)(2,1)} %get-tuple-element.31), channel_id=1, source_target_pairs={{0,1},{1,0},{2,3},{3,2},{4,5},{5,4},{6,7},{7,6},{8,9},{9,8},{10,11... | collective-permute-start | bytes 2555912 | tf_op jit(solution)/shard_map/ppermute | solution.py:170
  124.8 23.4 %collective-permute-start.16 = (f32[64,128,128]{2,1,0:T(8,128)}, f32[64,128,128]{2,1,0:T(8,128)}, u32[]{:S(2)}, u32[]{:S(2)}) collective-permute-start(f32[64,128,128]{2,1,0:T(8,128)} %get-tuple-element.21), channel_id=1, source_target_pairs={{0,8},{8,0},{16,24},{24,16},{32,40},{40,32},{48,56},{56,48},{64,72... | collective-permute-start | bytes 12582920 | tf_op jit(solution)/shard_map/ppermute | solution.py:170
  152.2 40.0 %collective-permute-start.17 = (f16[32,128,128]{2,1,0:T(8,128)(2,1)S(1)}, f16[32,128,128]{2,1,0:T(8,128)(2,1)S(1)}, u32[]{:S(2)}, u32[]{:S(2)}) collective-permute-start(f16[32,128,128]{2,1,0:T(8,128)(2,1)S(1)} %get-tuple-element.32), channel_id=1, source_target_pairs={{0,1},{1,0},{2,3},{3,2},{4,5},{5,4},{6,7},{7,6},{8,9},{9,8},{10,11... | collective-permute-start | bytes 3145736 | tf_op jit(solution)/shard_map/ppermute | solution.py:170
  153.4 38.7 %collective-permute-start.18 = (f16[32,128,128]{2,1,0:T(8,128)(2,1)S(1)}, f16[32,128,128]{2,1,0:T(8,128)(2,1)S(1)}, u32[]{:S(2)}, u32[]{:S(2)}) collective-permute-start(f16[32,128,128]{2,1,0:T(8,128)(2,1)S(1)} %get-tuple-element.33), channel_id=1, source_target_pairs={{0,129},{1,128},{2,131},{3,130},{4,133},{5,132},{6,135},{7,134},{8... | collective-permute-start | bytes 3145736 | tf_op jit(solution)/shard_map/ppermute | solution.py:170
  156.8 12.3 %collective-permute-start.26 = (f16[4,128,128]{2,1,0:T(8,128)(2,1)S(1)}, f16[4,128,128]{2,1,0:T(8,128)(2,1)S(1)}, u32[]{:S(2)}, u32[]{:S(2)}) collective-permute-start(f16[4,128,128]{2,1,0:T(8,128)(2,1)S(1)} %get-tuple-element.34), channel_id=1, source_target_pairs={{0,64},{8,72},{16,80},{24,88},{32,96},{40,104},{48,112},{56,120},{... | collective-permute-start | bytes 393224 | tf_op jit(solution)/shard_map/ppermute | solution.py:170
  164.1 14.5 %collective-permute-start.27 = (f16[4,128,128]{2,1,0:T(8,128)(2,1)S(1)}, f16[4,128,128]{2,1,0:T(8,128)(2,1)S(1)}, u32[]{:S(2)}, u32[]{:S(2)}) collective-permute-start(f16[4,128,128]{2,1,0:T(8,128)(2,1)S(1)} %get-tuple-element.40), channel_id=1, source_target_pairs={{0,48},{8,56},{16,64},{24,72},{32,80},{40,88},{48,96},{56,104},{64... | collective-permute-start | bytes 393224 | tf_op jit(solution)/shard_map/ppermute | solution.py:170
  166.0 18.5 %collective-permute-start.28 = (f16[4,128,128]{2,1,0:T(8,128)(2,1)S(1)}, f16[4,128,128]{2,1,0:T(8,128)(2,1)S(1)}, u32[]{:S(2)}, u32[]{:S(2)}) collective-permute-start(f16[4,128,128]{2,1,0:T(8,128)(2,1)S(1)} %get-tuple-element.39), channel_id=1, source_target_pairs={{0,80},{8,88},{16,96},{24,104},{32,112},{40,120},{48,0},{56,8},{64... | collective-permute-start | bytes 393224 | tf_op jit(solution)/shard_map/ppermute | solution.py:170
  169.2 15.4 %collective-permute-start.29 = (f16[4,128,128]{2,1,0:T(8,128)(2,1)S(1)}, f16[4,128,128]{2,1,0:T(8,128)(2,1)S(1)}, u32[]{:S(2)}, u32[]{:S(2)}) collective-permute-start(f16[4,128,128]{2,1,0:T(8,128)(2,1)S(1)} %get-tuple-element.38), channel_id=1, source_target_pairs={{0,32},{8,40},{16,48},{24,56},{32,64},{40,72},{48,80},{56,88},{64,... | collective-permute-start | bytes 393224 | tf_op jit(solution)/shard_map/ppermute | solution.py:170
  178.6 9.5 %collective-permute-start.30 = (f16[4,128,128]{2,1,0:T(8,128)(2,1)S(1)}, f16[4,128,128]{2,1,0:T(8,128)(2,1)S(1)}, u32[]{:S(2)}, u32[]{:S(2)}) collective-permute-start(f16[4,128,128]{2,1,0:T(8,128)(2,1)S(1)} %get-tuple-element.37), channel_id=1, source_target_pairs={{0,96},{8,104},{16,112},{24,120},{32,0},{40,8},{48,16},{56,24},{64... | collective-permute-start | bytes 393224 | tf_op jit(solution)/shard_map/ppermute | solution.py:170
  190.9 12.4 %collective-permute-start.33 = (f32[4,128,128]{2,1,0:T(8,128)S(1)}, f32[4,128,128]{2,1,0:T(8,128)S(1)}, u32[]{:S(2)}, u32[]{:S(2)}) collective-permute-start(f32[4,128,128]{2,1,0:T(8,128)S(1)} %fusion.6), channel_id=1, source_target_pairs={{0,128},{8,136},{16,144},{24,152},{32,160},{40,168},{48,176},{56,1... | collective-permute-start | bytes 786440 | tf_op jit(solution)/shard_map/ppermute | solution.py:170
  193.1 14.1 %collective-permute-start.19 = (f16[4,128,128]{2,1,0:T(8,128)(2,1)S(1)}, f16[4,128,128]{2,1,0:T(8,128)(2,1)S(1)}, u32[]{:S(2)}, u32[]{:S(2)}) collective-permute-start(f16[4,128,128]{2,1,0:T(8,128)(2,1)S(1)} %get-tuple-element.41), channel_id=1, source_target_pairs={{0,64},{8,72},{16,80},{24,88},{32,96},{40,104},{48,112},{56,120},{... | collective-permute-start | bytes 393224 | tf_op jit(solution)/shard_map/ppermute | solution.py:170
  198.0 16.5 %collective-permute-start.20 = (f16[4,128,128]{2,1,0:T(8,128)(2,1)S(1)}, f16[4,128,128]{2,1,0:T(8,128)(2,1)S(1)}, u32[]{:S(2)}, u32[]{:S(2)}) collective-permute-start(f16[4,128,128]{2,1,0:T(8,128)(2,1)S(1)} %get-tuple-element.47), channel_id=1, source_target_pairs={{0,48},{8,56},{16,64},{24,72},{32,80},{40,88},{48,96},{56,104},{64... | collective-permute-start | bytes 393224 | tf_op jit(solution)/shard_map/ppermute | solution.py:170
  199.7 14.8 %collective-permute-start.21 = (f16[4,128,128]{2,1,0:T(8,128)(2,1)S(1)}, f16[4,128,128]{2,1,0:T(8,128)(2,1)S(1)}, u32[]{:S(2)}, u32[]{:S(2)}) collective-permute-start(f16[4,128,128]{2,1,0:T(8,128)(2,1)S(1)} %get-tuple-element.46), channel_id=1, source_target_pairs={{0,80},{8,88},{16,96},{24,104},{32,112},{40,120},{48,0},{56,8},{64... | collective-permute-start | bytes 393224 | tf_op jit(solution)/shard_map/ppermute | solution.py:170
  203.1 14.5 %collective-permute-start.22 = (f16[4,128,128]{2,1,0:T(8,128)(2,1)S(1)}, f16[4,128,128]{2,1,0:T(8,128)(2,1)S(1)}, u32[]{:S(2)}, u32[]{:S(2)}) collective-permute-start(f16[4,128,128]{2,1,0:T(8,128)(2,1)S(1)} %get-tuple-element.45), channel_id=1, source_target_pairs={{0,32},{8,40},{16,48},{24,56},{32,64},{40,72},{48,80},{56,88},{64,... | collective-permute-start | bytes 393224 | tf_op jit(solution)/shard_map/ppermute | solution.py:170
  203.3 15.4 %collective-permute-start.23 = (f16[4,128,128]{2,1,0:T(8,128)(2,1)S(1)}, f16[4,128,128]{2,1,0:T(8,128)(2,1)S(1)}, u32[]{:S(2)}, u32[]{:S(2)}) collective-permute-start(f16[4,128,128]{2,1,0:T(8,128)(2,1)S(1)} %get-tuple-element.44), channel_id=1, source_target_pairs={{0,96},{8,104},{16,112},{24,120},{32,0},{40,8},{48,16},{56,24},{64... | collective-permute-start | bytes 393224 | tf_op jit(solution)/shard_map/ppermute | solution.py:170
  207.2 12.5 %collective-permute-start.24 = (f16[4,128,128]{2,1,0:T(8,128)(2,1)S(1)}, f16[4,128,128]{2,1,0:T(8,128)(2,1)S(1)}, u32[]{:S(2)}, u32[]{:S(2)}) collective-permute-start(f16[4,128,128]{2,1,0:T(8,128)(2,1)S(1)} %get-tuple-element.43), channel_id=1, source_target_pairs={{0,16},{8,24},{16,32},{24,40},{32,48},{40,56},{48,64},{56,72},{64,... | collective-permute-start | bytes 393224 | tf_op jit(solution)/shard_map/ppermute | solution.py:170
  (19 other events, 366.9 us)

commit v3 on v2

--- a/solution.py
+++ b/solution.py
@@ -9,8 +9,7 @@
 from jax.sharding import PartitionSpec as P
 
 
-UNROLL = 8
-CHUNKS = 4
+CHUNK = 32
 X_SWAP = [(t, t ^ 1) for t in range(8)]
 Y_UP = [(t, (t + 2) % 8) for t in range(8)]
 Y_DOWN = [(t, (t + 6) % 8) for t in range(8)]
@@ -19,6 +18,9 @@
 DIAGONAL = [(d * 8 + t, (d ^ 16) * 8 + (t ^ 1)) for d in range(32) for t in range(8)]
 
 
+Z_GROUPS = [[xh * 16 + z * 2 + c for z in range(8)] for xh in range(2) for c in range(2)]
+
+
 def z_swap(bit):
     return [(d, d ^ (bit * 2)) for d in range(32)]
 
@@ -27,10 +29,11 @@
     return [(d, (d // 16) * 16 + (d + 2 * k) % 16) for d in range(32)]
 
 
+Z_STEPS = (4, 3, 5, 2, 6, 1, 7)
 CORE, Z, X_HI, OWN, BELOW, ABOVE, FAR = range(7)
 
 
-def grads_kernel(plan, depths, split, with_acc, meta, slots_ref, *refs):
+def grads_kernel(plan, depths, split, with_acc, own, meta, slots_ref, *refs):
     count = len(plan)
     pieces = refs[:count]
     at = count
@@ -41,7 +44,7 @@
         at += 1
     outs_hbm = refs[at : at + (2 if split else 1)]
     at += len(outs_hbm)
-    x_buf, g_buf, o_buf, in_sem, out_sem = refs[at:]
+    x_buf, g_buf, o_buf, in_sem, acc_sem, out_sem = refs[at:]
     places = o_buf.shape[0]
     copies = []
     row = 0
@@ -59,19 +62,23 @@
             pltpu.make_async_copy(block, g_buf.at[pl.ds(row, size), :], in_sem.at[len(copies)])
         )
         row += size
-    piece = places // CHUNKS
-    loads = []
+    chunks = places // CHUNK
+    unroll = CHUNK // 2 if with_acc else CHUNK
+
+    def acc_load(i):
+        span = pl.ds(i * CHUNK, CHUNK)
+        return pltpu.make_async_copy(acc_hbm.at[span], o_buf.at[span], acc_sem.at[i])
+
+    def store(target, start, i):
+        return pltpu.make_async_copy(
+            o_buf.at[pl.ds(i * CHUNK, CHUNK)], target.at[pl.ds(start * CHUNK, CHUNK)], out_sem.at[i]
+        )
+
+    for copy in copies:
+        copy.start()
     if with_acc:
-        loads = [
-            pltpu.make_async_copy(
-                acc_hbm.at[pl.ds(i * piece, piece)],
-                o_buf.at[pl.ds(i * piece, piece)],
-                in_sem.at[len(copies) + i],
-            )
-            for i in range(CHUNKS)
-        ]
-    for copy in copies + loads:
-        copy.start()
+        for i in range(chunks):
+            acc_load(i).start()
     for copy in copies:
         copy.wait()
     core, z, x_hi = meta[CORE], meta[Z], meta[X_HI]
@@ -83,13 +90,13 @@
         ahead = lax.bitwise_and(lax.shift_right_logical(place, 2), 7)
         owner_core = lax.bitwise_xor(core, 1 - part)
         owner_x = lax.bitwise_xor(x_hi, far_half)
-        owner_z = lax.bitwise_and(z + ahead, 7)
+        owner_z = lax.bitwise_and((z * (1 - far_half) if own else z) + ahead, 7)
         return owner_x * 64 + owner_z * 8 + owner_core * 4 + lax.bitwise_and(place, 3)
 
     def trip(step, carry):
         values = []
-        for u in range(UNROLL):
-            place = step * UNROLL + u
+        for u in range(unroll):
+            place = step * unroll + u
             slot = slot_of(place)
             row = pl.multiple_of(slots_ref[0, slot] * 128, 128)
             col = pl.multiple_of(slots_ref[1, slot] * 128, 128)
@@ -104,29 +111,32 @@
             if split:
                 value = jnp.where(slot < live, value, 0.0)
             values.append(value)
-        for u in range(UNROLL):
-            o_buf[step * UNROLL + u] = values[u]
+        for u in range(unroll):
+            o_buf[step * unroll + u] = values[u]
         return carry
 
-    stores = []
-    for i in range(CHUNKS):
-        target = outs_hbm[i * len(outs_hbm) // CHUNKS]
-        start = i % (CHUNKS // len(outs_hbm)) * piece
-        stores.append(
-            pltpu.make_async_copy(
-                o_buf.at[pl.ds(i * piece, piece)], target.at[pl.ds(start, piece)], out_sem.at[i]
-            )
-        )
-    for i in range(CHUNKS):
-        if loads:
-            loads[i].wait()
-        lax.fori_loop(i * piece // UNROLL, (i + 1) * piece // UNROLL, trip, 0)
-        stores[i].start()
-    for store in stores:
-        store.wait()
-
-
-def partial_grads(meta, slot_table, pieces, grads, sources, split, acc=None):
+    each = CHUNK // unroll
+
+    def chunk(i, carry):
+        lax.fori_loop(i * each, (i + 1) * each, trip, 0)
+        store(outs_hbm[0], i, i).start()
+        return carry
+
+    if split:
+        stores = [store(outs_hbm[i * 2 // chunks], i % (chunks // 2), i) for i in range(chunks)]
+        for i in range(chunks):
+            if with_acc:
+                acc_load(i).wait()
+            lax.fori_loop(i * each, (i + 1) * each, trip, 0)
+            stores[i].start()
+    else:
+        stores = [store(outs_hbm[0], i, i) for i in range(chunks)]
+        lax.fori_loop(0, chunks, chunk, 0)
+    for copy in stores:
+        copy.wait()
+
+
+def partial_grads(name, meta, slot_table, pieces, grads, sources, split, acc=None):
     plan = tuple(piece.shape[0] for piece in pieces)
     depth = sum(plan)
     depths = tuple((128, source) for source in sources)
@@ -139,7 +149,7 @@
     extra = () if acc is None else (acc,)
     operands = (*pieces, *grads, *extra)
     return pl.pallas_call(
-        functools.partial(grads_kernel, plan, depths, split, acc is not None),
+        functools.partial(grads_kernel, plan, depths, split, acc is not None, name.startswith("own")),
         out_shape=out_shape,
         in_specs=[pl.BlockSpec(memory_space=pltpu.SMEM)] * 2 + [any_spec] * len(operands),
         out_specs=tuple(any_spec for _ in out_shape),
@@ -147,8 +157,9 @@
             pltpu.VMEM((depth, pieces[0].shape[1]), jnp.bfloat16),
             pltpu.VMEM((depth, grads[0].shape[1]), jnp.bfloat16),
             pltpu.VMEM(block, jnp.float32),
-            pltpu.SemaphoreType.DMA((len(operands) + CHUNKS,)),
-            pltpu.SemaphoreType.DMA((CHUNKS,)),
+            pltpu.SemaphoreType.DMA((len(operands),)),
+            pltpu.SemaphoreType.DMA((places // CHUNK,)),
+            pltpu.SemaphoreType.DMA((places // CHUNK,)),
         ],
         compiler_params=pltpu.CompilerParams(vmem_limit_bytes=56 * 1024 * 1024),
         cost_estimate=pl.CostEstimate(
@@ -178,14 +189,16 @@
     def theirs(source, index):
         return lax.dynamic_slice_in_dim(source, chunks[index] * 128, 128, 0)
 
-    below, above = move(tokens, Y_UP), move(tokens, Y_DOWN)
+    part_a, part_b = tokens[:64], tokens[64:]
+    below_a, above_b = move(part_a, Y_UP), move(part_b, Y_DOWN)
+    below_b, above_a = move(part_b, Y_UP), move(part_a, Y_DOWN)
     first_rows, later = lax.optimization_barrier((theirs(out_grad, 0), out_grad))
     g_own = move(first_rows, X_SWAP)
     table_x = move(table, X_SWAP)
     g_below, g_above, g_far = (
         move(theirs(later, i), X_SWAP) for i in (1, 2, 3)
     )
-    far_a, far_b = move(below[:64], Y_UP), move(above[64:], Y_DOWN)
+    far_a, far_b = move(below_a, Y_UP), move(above_b, Y_DOWN)
     top = jnp.broadcast_to(jnp.max(jnp.abs(later)).astype(jnp.float32), (8, 128))
     for pairs, axis in (
         (CORE_SWAP, "dp"),
@@ -199,12 +212,16 @@
     top = jnp.clip(top[0, 0], 1e-30, 1e37)
     meta_late, shrink, grow = lax.optimization_barrier((meta, 0.25 / top, 4.0 * top))
 
-    near = (tokens, below, above)
+    near = (tokens, below_a, below_b, above_a, above_b)
     far = (far_a, far_b)
-    (acc,) = partial_grads(meta, table, near, (out_grad,) * 3, (OWN, BELOW, ABOVE), False)
-    (acc_x,) = partial_grads(meta, table_x, near, (g_own, g_below, g_above), (None,) * 3, False)
-    send, keep = partial_grads(meta_late, table, far, (out_grad,), (FAR,), True, acc)
-    send_x, keep_x = partial_grads(meta_late, table_x, far, (g_far,), (None,), True, acc_x)
+    (acc,) = partial_grads(
+        "own_near", meta, table, near, (out_grad,) * 3, (OWN, BELOW, ABOVE), False
+    )
+    (acc_x,) = partial_grads(
+        "across_near", meta, table_x, near, (g_own, g_below, g_above), (None,) * 3, False
+    )
+    send, keep = partial_grads("own_far", meta_late, table, far, (out_grad,), (FAR,), True, acc)
+    send_x, keep_x = partial_grads("across_far", meta_late, table_x, far, (g_far,), (None,), True, acc_x)
 
     share = delta.shape[1]
     quarter = places // 4
@@ -212,18 +229,23 @@
     def z_sum(value):
         packed = value.astype(jnp.float16)
         total = value[:share]
-        for k in (4, 3, 5, 2, 6, 1, 7):
+        for k in Z_STEPS:
             got = move(packed[share * k : share * (k + 1)], z_shift(k), "dp")
             total = total + got.astype(jnp.float32)
         return total
 
     own_back = move(send, CORE_SWAP, "dp")
-    own_sum = (keep + own_back) * shrink
+    own_sum = lax.optimization_barrier((keep + own_back) * shrink)
     other = ((keep_x + move(send_x, CORE_SWAP, "dp")) * shrink).astype(jnp.float16)
     near_x = move(other[:quarter], X_SWAP)
     far_x = move(other[quarter:], DIAGONAL, ("dp", "tensor"))
-    from_far = move(z_sum(own_sum[quarter:]), X_HI_SWAP, "dp")
-    ours = own_sum[:quarter] + near_x.astype(jnp.float32) + far_x.astype(jnp.float32)
+    own_near, own_packed = lax.optimization_barrier(
+        (own_sum[:quarter], own_sum[quarter:].astype(jnp.float16))
+    )
+    pieces = lax.all_to_all(own_packed, "dp", 0, 0, axis_index_groups=Z_GROUPS, tiled=True)
+    pieces = jnp.sum(pieces.reshape(-1, share, 128, 128).astype(jnp.float32), axis=0)
+    from_far = move(pieces, X_HI_SWAP, "dp")
+    ours = own_near + near_x.astype(jnp.float32) + far_x.astype(jnp.float32)
     grads = (z_sum(ours) + from_far) * grow
     square_sum = jnp.broadcast_to(jnp.sum(grads * grads), (8, 128))
     for axis, size in (("dp", 32), ("tensor", 8)):

time: 252 us -> 247 us (0.980)
  starting transfers between devices: 72.8 us -> 57.8 us
  other arithmetic: 11.5 us -> 18.7 us
  Pallas kernels: 44.9 us -> 40.6 us
    ppermute x34 -> x29, starting transfers between devices: 72.8 us -> 50.6 us  [move(): return lax.ppermute(value, axis, pairs)]
    all_to_all x0 -> x1, starting transfers between devices: none -> 7.22 us  [on_device(): lax.all_to_all(own_packed, 'dp', 0, 0, axis_index_groups=Z_GROUPS, tiled=...]
    pallas_call x4, Pallas kernels: 44.9 us -> 40.6 us  [partial_grads(): pl.pallas_call(functools.partial(grads_kernel, plan, depths, split, acc i...]
    mul x0 -> x1, other arithmetic: none -> 3.03 us  [on_device(): own_sum = lax.optimization_barrier((keep + own_back) * shrink)]
    ppermute x34 -> x29, waiting for transfers between devices: 77.4 us -> 79.8 us  [move(): return lax.ppermute(value, axis, pairs)]
  transfers between devices with their start and end apart: 34 -> 30, of which waited for: 19 -> 10; matrix products, arithmetic and copies ran while one was open for 9% -> 10% of each run, Pallas kernels for 14% -> 17%
where the time goes in v3:
time: 247 us; the launch traced here: 245 us
  waiting for transfers between devices  79.8 us (32%)
  starting transfers between devices  57.8 us (23%)
  Pallas kernels  40.6 us (16%)
  blocking collectives  29 us (12%)
  other arithmetic  18.7 us (8%)
  local copies, waits for them, and re-layouts  15.9 us (6%)
  between operations  2.98 us (1%)
    ppermute x29, waiting for transfers between devices, move(): return lax.ppermute(value, axis, pairs)  79.8 us
    ppermute x29, starting transfers between devices, move(): return lax.ppermute(value, axis, pairs)  50.6 us
    pallas_call x4, Pallas kernels, partial_grads(): pl.pallas_call(functools.partial(grads_kernel, plan, depths, split, acc i...  40.6 us
    all_to_all x2, blocking collectives, on_device(): square_sum = jnp.sum(lax.all_to_all(spread, axis, 0, 0, tiled=True), axis=0)  29 us
    all_to_all x1, starting transfers between devices, on_device(): lax.all_to_all(own_packed, 'dp', 0, 0, axis_index_groups=Z_GROUPS, tiled=...  7.22 us
    dynamic_slice x2, local copies, waits for them, and re-layouts, theirs(): return lax.dynamic_slice_in_dim(source, chunks[index] * 128, 128, 0)  5.35 us
  transfers between devices with their start and end apart: 30, of which 10 were waited for; matrix products, arithmetic and copies ran while one was open for 10% of the time, Pallas kernels for 17%

profile of v3, /device:TPU:4, one launch (start us, length us, event | category | flops | bytes accessed | tf_op | source)
XLA Modules:
  0.0 244.7 jit_solution(11905812166974223778)
XLA Ops:
  0.0 3.1 %fusion.11 = (bf16[64,8192]{1,0:T(8,128)(2,1)}, bf16[64,8192]{1,0:T(8,128)(2,1)}) fusion(bf16[128,8192]{1,0:T(8,128)(2,1)} %refs_0_.3), kind=kLoop, calls=%fused_computation.25 | loop fusion | bytes 4194304 | tf_op jit(solution)/shard_map/slice | solution.py:192
  8.5 4.4 %abs_reduce_fusion = bf16[]{:T(256)} fusion(bf16[1024,3328]{1,0:T(8,128)(2,1)} %refs_2_.1), kind=kLoop, calls=%fused_computation | loop fusion | flops 6815743 | bytes 6815746 | tf_op jit(solution)/shard_map/reduce_max | solution.py:202
  19.7 10.9 %collective-permute-done.6.refs_1_ = bf16[64,8192]{1,0:T(8,128)(2,1)S(1)} collective-permute-done((bf16[64,8192]{1,0:T(8,128)(2,1)}, bf16[64,8192]{1,0:T(8,128)(2,1)S(1)}, u32[]{:S(2)}, u32[]{:S(2)}) %collective-permute-start.6) | collective-permute-done | bytes 1048608 | tf_op jit(solution)/shard_map/ppermute | solution.py:181
  30.9 2.9 %collective-permute-start.9 = (bf16[64,8192]{1,0:T(8,128)(2,1)S(1)}, bf16[64,8192]{1,0:T(8,128)(2,1)}, u32[]{:S(2)}, u32[]{:S(2)}) collective-permute-start(bf16[64,8192]{1,0:T(8,128)(2,1)S(1)} %collective-permute-done.8.refs_4_), channel_id=1, source_target_pairs={{0,6},{1,7},{2,0},{3,1},{4,2},{5,3},{6,4},{7,5},{8,14},{9,15},{10,... | collective-permute-start | bytes 3145736 | tf_op jit(solution)/shard_map/ppermute | solution.py:181
  33.8 3.3 %collective-permute-start.2 = (f32[8,128]{1,0:T(8,128)S(1)}, f32[8,128]{1,0:T(8,128)S(1)}, u32[]{:S(2)}, u32[]{:S(2)}) collective-permute-start(f32[8,128]{1,0:T(8,128)S(1)} %fusion.13), channel_id=1, source_target_pairs={{0,32},{8,40},{16,48},{24,56},{32,0},{40,8},{48,16},{56,24},{64,96... | collective-permute-start | bytes 12296 | tf_op jit(solution)/shard_map/ppermute | solution.py:181
  38.7 6.8 %collective-permute-start.3 = (f32[8,128]{1,0:T(8,128)S(1)}, f32[8,128]{1,0:T(8,128)S(1)}, u32[]{:S(2)}, u32[]{:S(2)}) collective-permute-start(f32[8,128]{1,0:T(8,128)S(1)} %max.25), channel_id=1, source_target_pairs={{0,64},{8,72},{16,80},{24,88},{32,96},{40,104},{48,112},{56,120},{... | collective-permute-start | bytes 12296 | tf_op jit(solution)/shard_map/ppermute | solution.py:181
  48.3 3.2 %constant_dynamic-slice_fusion = (bf16[128,3328]{1,0:T(8,128)(2,1)}, bf16[128,3328]{1,0:T(8,128)(2,1)}, bf16[128,3328]{1,0:T(8,128)(2,1)}) fusion(bf16[1024,3328]{1,0:T(8,128)(2,1)} %refs_2_.1, s32[]{:T(128)S(6)} %select_n.15, s32[]{:T(128)S(6)} %select_n.14, s32[]{:T(128)S(6)} %select_n.13), kind=kLoop, calls=%fused_computation.19 | loop fusion | bytes 5111820 | tf_op jit(solution)/shard_map/dynamic_slice | solution.py:190
  54.4 3.0 %collective-permute-done.5 = f32[8,128]{1,0:T(8,128)S(1)} collective-permute-done((f32[8,128]{1,0:T(8,128)S(1)}, f32[8,128]{1,0:T(8,128)S(1)}, u32[]{:S(2)}, u32[]{:S(2)}) %collective-permute-start.5) | collective-permute-done | bytes 4128 | tf_op jit(solution)/shard_map/ppermute | solution.py:181
  61.8 10.8 %shard_map.67.refs_3_ = f32[128,128,128]{2,1,0:T(8,128)} custom-call(s32[7]{0:T(128)} %stack.40.meta, s32[3,128]{1,0:T(4,128)} %add_add_fusion.slots_ref, bf16[128,8192]{1,0:T(8,128)(2,1)} %refs_0_.3, bf16[64,8192]{1,0:T(8,128)(2,1)} %copy-done.1, bf16[64,8192]{1,0:T(8,128)(2,1)} %copy-done.3, bf16[64,8192]{1,0:T(8,128)(2,1)} %collective-permute-done.11.refs_3_, ...), custom_call_target="tpu_custom_call" | custom-call | flops 1610612736 | bytes 30000000 | tf_op jit(solution)/shard_map/pallas_call | solution.py:151
  76.6 9.8 %shard_map.68 = (f32[64,128,128]{2,1,0:T(8,128)}, f32[64,128,128]{2,1,0:T(8,128)}) custom-call(s32[7]{0:T(128)} %stack.40.meta, s32[3,128]{1,0:T(4,128)} %add_add_fusion.slots_ref, bf16[64,8192]{1,0:T(8,128)(2,1)} %collective-permute-done.7.refs_0_, bf16[64,8192]{1,0:T(8,128)(2,1)} %collective-permute-done.9.refs_1_, bf16[1024,3328]{1,0:T(8,128)(2,1)} %refs_2_.1, ...), custom_call_target="tpu_custom_call" | custom-call | flops 536870912 | bytes 30000000 | tf_op jit(solution)/shard_map/pallas_call | solution.py:151
  86.4 29.6 %collective-permute-done.13.slots_ref = s32[3,128]{1,0:T(4,128)S(1)} collective-permute-done((s32[3,128]{1,0:T(4,128)S(1)}, s32[3,128]{1,0:T(4,128)S(1)}, u32[]{:S(2)}, u32[]{:S(2)}) %collective-permute-start.13) | collective-permute-done | bytes 1568 | tf_op jit(solution)/shard_map/ppermute | solution.py:181
  118.3 10.8 %shard_map.69.refs_3_ = f32[128,128,128]{2,1,0:T(8,128)} custom-call(s32[7]{0:T(128)} %stack.40.meta, s32[3,128]{1,0:T(4,128)} %copy-done.10, bf16[128,8192]{1,0:T(8,128)(2,1)} %refs_0_.3, bf16[64,8192]{1,0:T(8,128)(2,1)} %copy-done.1, bf16[64,8192]{1,0:T(8,128)(2,1)} %copy-done.3, bf16[64,8192]{1,0:T(8,128)(2,1)} %collective-permute-done.11.refs_3_, ...), custom_call_target="tpu_custom_call" | custom-call | flops 1610612736 | bytes 30000000 | tf_op jit(solution)/shard_map/pallas_call | solution.py:151
  130.0 9.3 %shard_map.70 = (f32[64,128,128]{2,1,0:T(8,128)}, f32[64,128,128]{2,1,0:T(8,128)}) custom-call(s32[7]{0:T(128)} %stack.40.meta, s32[3,128]{1,0:T(4,128)} %copy-done.10, bf16[64,8192]{1,0:T(8,128)(2,1)} %collective-permute-done.7.refs_0_, bf16[64,8192]{1,0:T(8,128)(2,1)} %collective-permute-done.9.refs_1_, bf16[128,3328]{1,0:T(8,128)(2,1)} %copy-done.4, ...), custom_call_target="tpu_custom_call" | custom-call | flops 536870912 | bytes 30000000 | tf_op jit(solution)/shard_map/pallas_call | solution.py:151
  139.9 3.0 %add_multiply_fusion = f32[64,128,128]{2,1,0:T(8,128)S(1)} fusion(f32[64,128,128]{2,1,0:T(8,128)S(1)} %copy-done, f32[64,128,128]{2,1,0:T(8,128)} %collective-permute-done.12, f32[]{:T(128)} %bitcast.7), kind=kLoop, calls=%fused_computation.2 | loop fusion | flops 2097152 | bytes 12582916 | tf_op jit(solution)/shard_map/mul | solution.py:238
  144.3 7.2 %all-to-all-start = ((f16[32,128,128]{2,1,0:T(8,128)(2,1)}), f16[32,128,128]{2,1,0:T(8,128)(2,1)S(1)}, u32[]{:S(2)}, u32[]{:S(2)}) async-start(f16[32,128,128]{2,1,0:T(8,128)(2,1)} %get-tuple-element.25), calls=%async_computation | async-start | bytes 2097152 | tf_op jit(solution)/shard_map/all_to_all | solution.py:245
  151.5 4.5 %multiply_convert_fusion = f16[64,128,128]{2,1,0:T(8,128)(2,1)S(1)} fusion(f32[64,128,128]{2,1,0:T(8,128)} %get-tuple-element.23, f32[64,128,128]{2,1,0:T(8,128)} %collective-permute-done.18, f32[]{:T(128)} %bitcast.7), kind=kLoop, calls=%fused_computation.1 | loop fusion | flops 3145728 | bytes 10485764 | tf_op jit(solution)/shard_map/convert_element_type | solution.py:239
  158.8 22.9 %collective-permute-done.20 = f16[32,128,128]{2,1,0:T(8,128)(2,1)S(1)} collective-permute-done((f16[32,128,128]{2,1,0:T(8,128)(2,1)S(1)}, f16[32,128,128]{2,1,0:T(8,128)(2,1)S(1)}, u32[]{:S(2)}, u32[]{:S(2)}) %collective-permute-start.20) | collective-permute-done | bytes 1048608 | tf_op jit(solution)/shard_map/ppermute | solution.py:181
  184.3 3.0 %collective-permute-start.27 = (f16[4,128,128]{2,1,0:T(8,128)(2,1)S(1)}, f16[4,128,128]{2,1,0:T(8,128)(2,1)S(1)}, u32[]{:S(2)}, u32[]{:S(2)}) collective-permute-start(f16[4,128,128]{2,1,0:T(8,128)(2,1)S(1)} %get-tuple-element.41), channel_id=1, source_target_pairs={{0,112},{8,120},{16,0},{24,8},{32,16},{40,24},{48,32},{56,40},{64,... | collective-permute-start | bytes 393224 | tf_op jit(solution)/shard_map/ppermute | solution.py:181
  187.3 2.9 %collective-permute-start.25 = (f16[4,128,128]{2,1,0:T(8,128)(2,1)S(1)}, f16[4,128,128]{2,1,0:T(8,128)(2,1)S(1)}, u32[]{:S(2)}, u32[]{:S(2)}) collective-permute-start(f16[4,128,128]{2,1,0:T(8,128)(2,1)S(1)} %get-tuple-element.43), channel_id=1, source_target_pairs={{0,96},{8,104},{16,112},{24,120},{32,0},{40,8},{48,16},{56,24},{64... | collective-permute-start | bytes 393224 | tf_op jit(solution)/shard_map/ppermute | solution.py:181
  192.8 5.3 %collective-permute-start.23 = (f16[4,128,128]{2,1,0:T(8,128)(2,1)S(1)}, f16[4,128,128]{2,1,0:T(8,128)(2,1)S(1)}, u32[]{:S(2)}, u32[]{:S(2)}) collective-permute-start(f16[4,128,128]{2,1,0:T(8,128)(2,1)S(1)} %get-tuple-element.45), channel_id=1, source_target_pairs={{0,80},{8,88},{16,96},{24,104},{32,112},{40,120},{48,0},{56,8},{64... | collective-permute-start | bytes 393224 | tf_op jit(solution)/shard_map/ppermute | solution.py:181
  198.1 5.3 %collective-permute-start.21 = (f16[4,128,128]{2,1,0:T(8,128)(2,1)S(1)}, f16[4,128,128]{2,1,0:T(8,128)(2,1)S(1)}, u32[]{:S(2)}, u32[]{:S(2)}) collective-permute-start(f16[4,128,128]{2,1,0:T(8,128)(2,1)S(1)} %get-tuple-element.40), channel_id=1, source_target_pairs={{0,64},{8,72},{16,80},{24,88},{32,96},{40,104},{48,112},{56,120},{... | collective-permute-start | bytes 393224 | tf_op jit(solution)/shard_map/ppermute | solution.py:181
  203.5 5.1 %collective-permute-done.24 = f16[4,128,128]{2,1,0:T(8,128)(2,1)S(1)} collective-permute-done((f16[4,128,128]{2,1,0:T(8,128)(2,1)S(1)}, f16[4,128,128]{2,1,0:T(8,128)(2,1)S(1)}, u32[]{:S(2)}, u32[]{:S(2)}) %collective-permute-start.24) | collective-permute-done | bytes 131104 | tf_op jit(solution)/shard_map/ppermute | solution.py:181
  213.8 20.2 %all_to_all.15 = f32[32,8,128]{2,1,0:T(8,128)S(1)} all-to-all(f32[32,8,128]{2,1,0:T(8,128)S(1)} %broadcast_in_dim_broadcast_in_dim_broadcast_in_dim.3), channel_id=1, replica_groups=mesh['dp'=32,'tensor'=8] {'dp'}, dimensions={0} | all-to-all | bytes 262144 | tf_op jit(solution)/shard_map/all_to_all | solution.py:253
  234.0 8.8 %all_to_all.16 = f32[8,8,128]{2,1,0:T(8,128)S(1)} all-to-all(f32[8,8,128]{2,1,0:T(8,128)S(1)} %broadcast_in_dim.5), channel_id=1, replica_groups=mesh['dp'=32,'tensor'=8] {'tensor'}, dimensions={0} | all-to-all | bytes 65536 | tf_op jit(solution)/shard_map/all_to_all | solution.py:253
  (97 shorter events, 45.6 us)
Async XLA Ops:
  3.1 27.5 %collective-permute-start.6 = (bf16[64,8192]{1,0:T(8,128)(2,1)}, bf16[64,8192]{1,0:T(8,128)(2,1)S(1)}, u32[]{:S(2)}, u32[]{:S(2)}) collective-permute-start(bf16[64,8192]{1,0:T(8,128)(2,1)} %get-tuple-element.39), channel_id=1, source_target_pairs={{0,2},{1,3},{2,4},{3,5},{4,6},{5,7},{6,0},{7,1},{8,10},{9,11},{10,... | collective-permute-start | bytes 3145736 | tf_op jit(solution)/shard_map/ppermute | solution.py:181
  4.7 26.2 %collective-permute-start.8 = (bf16[64,8192]{1,0:T(8,128)(2,1)}, bf16[64,8192]{1,0:T(8,128)(2,1)S(1)}, u32[]{:S(2)}, u32[]{:S(2)}) collective-permute-start(bf16[64,8192]{1,0:T(8,128)(2,1)} %get-tuple-element.38), channel_id=1, source_target_pairs={{0,6},{1,7},{2,0},{3,1},{4,2},{5,3},{6,4},{7,5},{8,14},{9,15},{10,... | collective-permute-start | bytes 3145736 | tf_op jit(solution)/shard_map/ppermute | solution.py:181
  13.7 45.9 %collective-permute-start.10 = (bf16[64,8192]{1,0:T(8,128)(2,1)}, bf16[64,8192]{1,0:T(8,128)(2,1)S(1)}, u32[]{:S(2)}, u32[]{:S(2)}) collective-permute-start(bf16[64,8192]{1,0:T(8,128)(2,1)} %get-tuple-element.38), channel_id=1, source_target_pairs={{0,2},{1,3},{2,4},{3,5},{4,6},{5,7},{6,0},{7,1},{8,10},{9,11},{10,... | collective-permute-start | bytes 3145736 | tf_op jit(solution)/shard_map/ppermute | solution.py:181
  14.1 46.8 %collective-permute-start.11 = (bf16[64,8192]{1,0:T(8,128)(2,1)}, bf16[64,8192]{1,0:T(8,128)(2,1)}, u32[]{:S(2)}, u32[]{:S(2)}) collective-permute-start(bf16[64,8192]{1,0:T(8,128)(2,1)} %get-tuple-element.39), channel_id=1, source_target_pairs={{0,6},{1,7},{2,0},{3,1},{4,2},{5,3},{6,4},{7,5},{8,14},{9,15},{10,... | collective-permute-start | bytes 3145736 | tf_op jit(solution)/shard_map/ppermute | solution.py:181
  17.7 16.1 %collective-permute-start.1 = (f32[8,128]{1,0:T(8,128)S(1)}, f32[8,128]{1,0:T(8,128)S(1)}, u32[]{:S(2)}, u32[]{:S(2)}) collective-permute-start(f32[8,128]{1,0:T(8,128)S(1)} %broadcast_maximum_fusion), channel_id=1, source_target_pairs={{0,16},{8,24},{16,0},{24,8},{32,48},{40,56},{48,32},{56,40},{64,80... | collective-permute-start | bytes 12296 | tf_op jit(solution)/shard_map/ppermute | solution.py:181
  30.6 44.0 %collective-permute-start.7 = (bf16[64,8192]{1,0:T(8,128)(2,1)S(1)}, bf16[64,8192]{1,0:T(8,128)(2,1)}, u32[]{:S(2)}, u32[]{:S(2)}) collective-permute-start(bf16[64,8192]{1,0:T(8,128)(2,1)S(1)} %collective-permute-done.6.refs_1_), channel_id=1, source_target_pairs={{0,2},{1,3},{2,4},{3,5},{4,6},{5,7},{6,0},{7,1},{8,10},{9,11},{10,... | collective-permute-start | bytes 3145736 | tf_op jit(solution)/shard_map/ppermute | solution.py:181
  30.9 44.8 %collective-permute-start.9 = (bf16[64,8192]{1,0:T(8,128)(2,1)S(1)}, bf16[64,8192]{1,0:T(8,128)(2,1)}, u32[]{:S(2)}, u32[]{:S(2)}) collective-permute-start(bf16[64,8192]{1,0:T(8,128)(2,1)S(1)} %collective-permute-done.8.refs_4_), channel_id=1, source_target_pairs={{0,6},{1,7},{2,0},{3,1},{4,2},{5,3},{6,4},{7,5},{8,14},{9,15},{10,... | collective-permute-start | bytes 3145736 | tf_op jit(solution)/shard_map/ppermute | solution.py:181
  57.5 58.6 %collective-permute-start.15 = (bf16[128,3328]{1,0:T(8,128)(2,1)}, bf16[128,3328]{1,0:T(8,128)(2,1)S(1)}, u32[]{:S(2)}, u32[]{:S(2)}) collective-permute-start(bf16[128,3328]{1,0:T(8,128)(2,1)} %constant_dynamic-slice_fusion.3), channel_id=1, source_target_pairs={{0,1},{1,0},{2,3},{3,2},{4,5},{5,4},{6,7},{7,6},{8,9},{9,8},{10,11... | collective-permute-start | bytes 2555912 | tf_op jit(solution)/shard_map/ppermute | solution.py:181
  59.6 56.4 %collective-permute-start.16 = (bf16[128,3328]{1,0:T(8,128)(2,1)}, bf16[128,3328]{1,0:T(8,128)(2,1)S(1)}, u32[]{:S(2)}, u32[]{:S(2)}) collective-permute-start(bf16[128,3328]{1,0:T(8,128)(2,1)} %get-tuple-element.32), channel_id=1, source_target_pairs={{0,1},{1,0},{2,3},{3,2},{4,5},{5,4},{6,7},{7,6},{8,9},{9,8},{10,11... | collective-permute-start | bytes 2555912 | tf_op jit(solution)/shard_map/ppermute | solution.py:181
  60.9 55.2 %collective-permute-start.17 = (bf16[128,3328]{1,0:T(8,128)(2,1)}, bf16[128,3328]{1,0:T(8,128)(2,1)S(1)}, u32[]{:S(2)}, u32[]{:S(2)}) collective-permute-start(bf16[128,3328]{1,0:T(8,128)(2,1)} %get-tuple-element.31), channel_id=1, source_target_pairs={{0,1},{1,0},{2,3},{3,2},{4,5},{5,4},{6,7},{7,6},{8,9},{9,8},{10,11... | collective-permute-start | bytes 2555912 | tf_op jit(solution)/shard_map/ppermute | solution.py:181
  74.6 41.5 %collective-permute-start.13 = (s32[3,128]{1,0:T(4,128)S(1)}, s32[3,128]{1,0:T(4,128)S(1)}, u32[]{:S(2)}, u32[]{:S(2)}) collective-permute-start(s32[3,128]{1,0:T(4,128)S(1)} %copy-done.9), channel_id=1, source_target_pairs={{0,1},{1,0},{2,3},{3,2},{4,5},{5,4},{6,7},{7,6},{8,9},{9,8},{10,11... | collective-permute-start | bytes 4616 | tf_op jit(solution)/shard_map/ppermute | solution.py:181
  75.8 53.3 %collective-permute-start.14 = (bf16[128,3328]{1,0:T(8,128)(2,1)}, bf16[128,3328]{1,0:T(8,128)(2,1)S(1)}, u32[]{:S(2)}, u32[]{:S(2)}) collective-permute-start(bf16[128,3328]{1,0:T(8,128)(2,1)} %get-tuple-element.33), channel_id=1, source_target_pairs={{0,1},{1,0},{2,3},{3,2},{4,5},{5,4},{6,7},{7,6},{8,9},{9,8},{10,11... | collective-permute-start | bytes 2555912 | tf_op jit(solution)/shard_map/ppermute | solution.py:181
  116.0 23.8 %collective-permute-start.12 = (f32[64,128,128]{2,1,0:T(8,128)}, f32[64,128,128]{2,1,0:T(8,128)}, u32[]{:S(2)}, u32[]{:S(2)}) collective-permute-start(f32[64,128,128]{2,1,0:T(8,128)} %get-tuple-element.19), channel_id=1, source_target_pairs={{0,8},{8,0},{16,24},{24,16},{32,40},{40,32},{48,56},{56,48},{64,72... | collective-permute-start | bytes 12582920 | tf_op jit(solution)/shard_map/ppermute | solution.py:181
  139.3 12.2 %collective-permute-start.18 = (f32[64,128,128]{2,1,0:T(8,128)}, f32[64,128,128]{2,1,0:T(8,128)}, u32[]{:S(2)}, u32[]{:S(2)}) collective-permute-start(f32[64,128,128]{2,1,0:T(8,128)} %get-tuple-element.24), channel_id=1, source_target_pairs={{0,8},{8,0},{16,24},{24,16},{32,40},{40,32},{48,56},{56,48},{64,72... | collective-permute-start | bytes 12582920 | tf_op jit(solution)/shard_map/ppermute | solution.py:181
  144.3 46.0 %all-to-all-start = ((f16[32,128,128]{2,1,0:T(8,128)(2,1)}), f16[32,128,128]{2,1,0:T(8,128)(2,1)S(1)}, u32[]{:S(2)}, u32[]{:S(2)}) async-start(f16[32,128,128]{2,1,0:T(8,128)(2,1)} %get-tuple-element.25), calls=%async_computation | async-start | bytes 2097152 | tf_op jit(solution)/shard_map/all_to_all | solution.py:245
  156.8 24.9 %collective-permute-start.20 = (f16[32,128,128]{2,1,0:T(8,128)(2,1)S(1)}, f16[32,128,128]{2,1,0:T(8,128)(2,1)S(1)}, u32[]{:S(2)}, u32[]{:S(2)}) collective-permute-start(f16[32,128,128]{2,1,0:T(8,128)(2,1)S(1)} %get-tuple-element.37), channel_id=1, source_target_pairs={{0,129},{1,128},{2,131},{3,130},{4,133},{5,132},{6,135},{7,134},{8... | collective-permute-start | bytes 3145736 | tf_op jit(solution)/shard_map/ppermute | solution.py:181
  156.9 25.1 %collective-permute-start.19 = (f16[32,128,128]{2,1,0:T(8,128)(2,1)S(1)}, f16[32,128,128]{2,1,0:T(8,128)(2,1)S(1)}, u32[]{:S(2)}, u32[]{:S(2)}) collective-permute-start(f16[32,128,128]{2,1,0:T(8,128)(2,1)S(1)} %get-tuple-element.36), channel_id=1, source_target_pairs={{0,1},{1,0},{2,3},{3,2},{4,5},{5,4},{6,7},{7,6},{8,9},{9,8},{10,11... | collective-permute-start | bytes 3145736 | tf_op jit(solution)/shard_map/ppermute | solution.py:181
  187.3 10.8 %collective-permute-start.26 = (f16[4,128,128]{2,1,0:T(8,128)(2,1)S(1)}, f16[4,128,128]{2,1,0:T(8,128)(2,1)S(1)}, u32[]{:S(2)}, u32[]{:S(2)}) collective-permute-start(f16[4,128,128]{2,1,0:T(8,128)(2,1)S(1)} %get-tuple-element.42), channel_id=1, source_target_pairs={{0,16},{8,24},{16,32},{24,40},{32,48},{40,56},{48,64},{56,72},{64,... | collective-permute-start | bytes 393224 | tf_op jit(solution)/shard_map/ppermute | solution.py:181
  187.3 10.8 %collective-permute-start.25 = (f16[4,128,128]{2,1,0:T(8,128)(2,1)S(1)}, f16[4,128,128]{2,1,0:T(8,128)(2,1)S(1)}, u32[]{:S(2)}, u32[]{:S(2)}) collective-permute-start(f16[4,128,128]{2,1,0:T(8,128)(2,1)S(1)} %get-tuple-element.43), channel_id=1, source_target_pairs={{0,96},{8,104},{16,112},{24,120},{32,0},{40,8},{48,16},{56,24},{64... | collective-permute-start | bytes 393224 | tf_op jit(solution)/shard_map/ppermute | solution.py:181
  190.4 20.9 %collective-permute-start.28 = (f32[4,128,128]{2,1,0:T(8,128)S(1)}, f32[4,128,128]{2,1,0:T(8,128)S(1)}, u32[]{:S(2)}, u32[]{:S(2)}) collective-permute-start(f32[4,128,128]{2,1,0:T(8,128)S(1)} %convert_reduce_fusion), channel_id=1, source_target_pairs={{0,128},{8,136},{16,144},{24,152},{32,160},{40,168},{48,176},{56,1... | collective-permute-start | bytes 786440 | tf_op jit(solution)/shard_map/ppermute | solution.py:181
  192.8 15.8 %collective-permute-start.24 = (f16[4,128,128]{2,1,0:T(8,128)(2,1)S(1)}, f16[4,128,128]{2,1,0:T(8,128)(2,1)S(1)}, u32[]{:S(2)}, u32[]{:S(2)}) collective-permute-start(f16[4,128,128]{2,1,0:T(8,128)(2,1)S(1)} %get-tuple-element.44), channel_id=1, source_target_pairs={{0,32},{8,40},{16,48},{24,56},{32,64},{40,72},{48,80},{56,88},{64,... | collective-permute-start | bytes 393224 | tf_op jit(solution)/shard_map/ppermute | solution.py:181
  192.8 15.8 %collective-permute-start.23 = (f16[4,128,128]{2,1,0:T(8,128)(2,1)S(1)}, f16[4,128,128]{2,1,0:T(8,128)(2,1)S(1)}, u32[]{:S(2)}, u32[]{:S(2)}) collective-permute-start(f16[4,128,128]{2,1,0:T(8,128)(2,1)S(1)} %get-tuple-element.45), channel_id=1, source_target_pairs={{0,80},{8,88},{16,96},{24,104},{32,112},{40,120},{48,0},{56,8},{64... | collective-permute-start | bytes 393224 | tf_op jit(solution)/shard_map/ppermute | solution.py:181
  198.1 13.2 %collective-permute-start.22 = (f16[4,128,128]{2,1,0:T(8,128)(2,1)S(1)}, f16[4,128,128]{2,1,0:T(8,128)(2,1)S(1)}, u32[]{:S(2)}, u32[]{:S(2)}) collective-permute-start(f16[4,128,128]{2,1,0:T(8,128)(2,1)S(1)} %get-tuple-element.46), channel_id=1, source_target_pairs={{0,48},{8,56},{16,64},{24,72},{32,80},{40,88},{48,96},{56,104},{64... | collective-permute-start | bytes 393224 | tf_op jit(solution)/shard_map/ppermute | solution.py:181
  198.1 13.2 %collective-permute-start.21 = (f16[4,128,128]{2,1,0:T(8,128)(2,1)S(1)}, f16[4,128,128]{2,1,0:T(8,128)(2,1)S(1)}, u32[]{:S(2)}, u32[]{:S(2)}) collective-permute-start(f16[4,128,128]{2,1,0:T(8,128)(2,1)S(1)} %get-tuple-element.40), channel_id=1, source_target_pairs={{0,64},{8,72},{16,80},{24,88},{32,96},{40,104},{48,112},{56,120},{... | collective-permute-start | bytes 393224 | tf_op jit(solution)/shard_map/ppermute | solution.py:181
  (19 other events, 269.8 us)

commit v4 on v3

--- a/solution.py
+++ b/solution.py
@@ -63,7 +63,7 @@
         )
         row += size
     chunks = places // CHUNK
-    unroll = CHUNK // 2 if with_acc else CHUNK
+    unroll = CHUNK // 4 if with_acc else CHUNK // 2
 
     def acc_load(i):
         span = pl.ds(i * CHUNK, CHUNK)
@@ -87,11 +87,17 @@
     def slot_of(place):
         part = lax.shift_right_logical(place, 6)
         far_half = lax.bitwise_and(lax.shift_right_logical(place, 5), 1)
-        ahead = lax.bitwise_and(lax.shift_right_logical(place, 2), 7)
+        ahead = lax.bitwise_and(lax.shift_right_logical(place, 1), 7)
+        item = lax.bitwise_and(lax.shift_right_logical(place, 4), 1) * 2 + lax.bitwise_and(place, 1)
+        if own:
+            ahead = jnp.where(
+                far_half == 1, lax.bitwise_and(lax.shift_right_logical(place, 2), 7), ahead
+            )
+            item = jnp.where(far_half == 1, lax.bitwise_and(place, 3), item)
         owner_core = lax.bitwise_xor(core, 1 - part)
         owner_x = lax.bitwise_xor(x_hi, far_half)
         owner_z = lax.bitwise_and((z * (1 - far_half) if own else z) + ahead, 7)
-        return owner_x * 64 + owner_z * 8 + owner_core * 4 + lax.bitwise_and(place, 3)
+        return owner_x * 64 + owner_z * 8 + owner_core * 4 + item
 
     def trip(step, carry):
         values = []
@@ -210,7 +216,7 @@
     ):
         top = jnp.maximum(top, move(top, pairs, axis))
     top = jnp.clip(top[0, 0], 1e-30, 1e37)
-    meta_late, shrink, grow = lax.optimization_barrier((meta, 0.25 / top, 4.0 * top))
+    shrink, grow = lax.optimization_barrier((0.25 / top, 4.0 * top))
 
     near = (tokens, below_a, below_b, above_a, above_b)
     far = (far_a, far_b)
@@ -220,33 +226,46 @@
     (acc_x,) = partial_grads(
         "across_near", meta, table_x, near, (g_own, g_below, g_above), (None,) * 3, False
     )
-    send, keep = partial_grads("own_far", meta_late, table, far, (out_grad,), (FAR,), True, acc)
-    send_x, keep_x = partial_grads("across_far", meta_late, table_x, far, (g_far,), (None,), True, acc_x)
+    send, keep = partial_grads("own_far", meta, table, far, (out_grad,), (FAR,), True, acc)
+    send_x, keep_x = partial_grads("across_far", meta, table_x, far, (g_far,), (None,), True, acc_x)
 
     share = delta.shape[1]
     quarter = places // 4
 
-    def z_sum(value):
-        packed = value.astype(jnp.float16)
-        total = value[:share]
+    width = share // 2
+
+    def z_sum(value, packed):
+        total = value[:width]
         for k in Z_STEPS:
-            got = move(packed[share * k : share * (k + 1)], z_shift(k), "dp")
+            got = move(packed[width * k : width * (k + 1)], z_shift(k), "dp")
             total = total + got.astype(jnp.float32)
         return total
 
     own_back = move(send, CORE_SWAP, "dp")
-    own_sum = lax.optimization_barrier((keep + own_back) * shrink)
-    other = ((keep_x + move(send_x, CORE_SWAP, "dp")) * shrink).astype(jnp.float16)
-    near_x = move(other[:quarter], X_SWAP)
-    far_x = move(other[quarter:], DIAGONAL, ("dp", "tensor"))
+    own_sum, shrink_x = lax.optimization_barrier(((keep + own_back) * shrink, shrink))
+    other = ((keep_x + move(send_x, CORE_SWAP, "dp")) * shrink_x).astype(jnp.float16)
+    part = quarter // 2
+    got_x = []
+    for h in range(2):
+        near_x = move(other[h * part : (h + 1) * part], X_SWAP)
+        far_x = other[quarter + h * part : quarter + (h + 1) * part]
+        got_x.append((near_x, move(far_x, DIAGONAL, ("dp", "tensor"))))
     own_near, own_packed = lax.optimization_barrier(
         (own_sum[:quarter], own_sum[quarter:].astype(jnp.float16))
     )
     pieces = lax.all_to_all(own_packed, "dp", 0, 0, axis_index_groups=Z_GROUPS, tiled=True)
     pieces = jnp.sum(pieces.reshape(-1, share, 128, 128).astype(jnp.float32), axis=0)
     from_far = move(pieces, X_HI_SWAP, "dp")
-    ours = own_near + near_x.astype(jnp.float32) + far_x.astype(jnp.float32)
-    grads = (z_sum(ours) + from_far) * grow
+    halves = []
+    for h in range(2):
+        ours = own_near[:part] if h == 0 else own_near[part:]
+        for got in got_x[h]:
+            ours = ours + got.astype(jnp.float32)
+        ours = lax.optimization_barrier(ours)
+        packed = ours.astype(jnp.float16)
+        packed, own_near = lax.optimization_barrier((packed, own_near))
+        halves.append(z_sum(ours, packed))
+    grads = (jnp.concatenate(halves, axis=0) + from_far) * grow
     square_sum = jnp.broadcast_to(jnp.sum(grads * grads), (8, 128))
     for axis, size in (("dp", 32), ("tensor", 8)):
         spread = jnp.broadcast_to(square_sum[None], (size, 8, 128))

time: 247 us -> 267 us (1.081)
  starting transfers between devices: 57.8 us -> 72.4 us
  waiting for transfers between devices: 79.8 us -> 84.4 us
  Pallas kernels: 40.6 us -> 45.2 us
    ppermute x29 -> x38, starting transfers between devices: 50.6 us -> 65.2 us  [move(): return lax.ppermute(value, axis, pairs)]
    pallas_call x4, Pallas kernels: 40.6 us -> 45.2 us  [partial_grads(): pl.pallas_call(functools.partial(grads_kernel, plan, depths, split, acc i...]
    ppermute x29 -> x38, waiting for transfers between devices: 79.8 us -> 84.4 us  [move(): return lax.ppermute(value, axis, pairs)]
    reduce_max x1, other arithmetic: 4.42 us -> 1.48 us  [on_device(): jnp.max(jnp.abs(later)).astype(jnp.float32)]
    convert_element_type x2 -> x3, other arithmetic: 6.52 us -> 4.66 us  [the longest x1 4.45 us: on_device(): ((keep_x + move(send_x, CORE_SWAP, 'dp')) * shrink_x).astype(jnp.float16)]
  transfers between devices with their start and end apart: 30 -> 39, of which waited for: 10 -> 18; matrix products, arithmetic and copies ran while one was open for 10% -> 9% of each run, Pallas kernels for 17% -> 17%
where the time goes in v4:
time: 267 us; the launch traced here: 265 us
  waiting for transfers between devices  84.4 us (32%)
  starting transfers between devices  72.4 us (27%)
  Pallas kernels  45.2 us (17%)
  blocking collectives  28.5 us (11%)
  other arithmetic  16.7 us (6%)
  local copies, waits for them, and re-layouts  14.7 us (6%)
  between operations  3 us (1%)
    ppermute x38, waiting for transfers between devices, move(): return lax.ppermute(value, axis, pairs)  84.4 us
    ppermute x38, starting transfers between devices, move(): return lax.ppermute(value, axis, pairs)  65.2 us
    pallas_call x4, Pallas kernels, partial_grads(): pl.pallas_call(functools.partial(grads_kernel, plan, depths, split, acc i...  45.2 us
    all_to_all x2, blocking collectives, on_device(): square_sum = jnp.sum(lax.all_to_all(spread, axis, 0, 0, tiled=True), axis=0)  28.5 us
    all_to_all x1, starting transfers between devices, on_device(): lax.all_to_all(own_packed, 'dp', 0, 0, axis_index_groups=Z_GROUPS, tiled=...  7.21 us
  transfers between devices with their start and end apart: 39, of which 18 were waited for; matrix products, arithmetic and copies ran while one was open for 9% of the time, Pallas kernels for 17%

profile of v4, /device:TPU:4, one launch (start us, length us, event | category | flops | bytes accessed | tf_op | source)
XLA Modules:
  0.0 265.0 jit_solution(18010811352218784832)
XLA Ops:
  9.6 21.0 %collective-permute-done.refs_1_ = bf16[64,8192]{1,0:T(8,128)(2,1)S(1)} collective-permute-done((bf16[64,8192]{1,0:T(8,128)(2,1)}, bf16[64,8192]{1,0:T(8,128)(2,1)S(1)}, u32[]{:S(2)}, u32[]{:S(2)}) %collective-permute-start) | collective-permute-done | bytes 1048608 | tf_op jit(solution)/shard_map/ppermute | solution.py:187
  39.2 3.2 %constant_dynamic-slice_fusion = (bf16[128,3328]{1,0:T(8,128)(2,1)}, bf16[128,3328]{1,0:T(8,128)(2,1)}, bf16[128,3328]{1,0:T(8,128)(2,1)}) fusion(bf16[1024,3328]{1,0:T(8,128)(2,1)} %refs_2_.1, s32[]{:T(128)S(6)} %select_n.15, s32[]{:T(128)S(6)} %select_n.14, s32[]{:T(128)S(6)} %select_n.13), kind=kLoop, calls=%fused_computation.27 | loop fusion | bytes 5111820 | tf_op jit(solution)/shard_map/dynamic_slice | solution.py:196
  42.4 10.8 %collective-permute-done.4.refs_2_ = bf16[64,8192]{1,0:T(8,128)(2,1)} collective-permute-done((bf16[64,8192]{1,0:T(8,128)(2,1)}, bf16[64,8192]{1,0:T(8,128)(2,1)}, u32[]{:S(2)}, u32[]{:S(2)}) %collective-permute-start.4) | collective-permute-done | bytes 1048608 | tf_op jit(solution)/shard_map/ppermute | solution.py:187
  55.2 11.5 %shard_map.67.refs_3_ = f32[128,128,128]{2,1,0:T(8,128)} custom-call(s32[7]{0:T(128)} %stack.40.meta, s32[3,128]{1,0:T(4,128)} %add_add_fusion.slots_ref, bf16[128,8192]{1,0:T(8,128)(2,1)} %refs_0_.3, bf16[64,8192]{1,0:T(8,128)(2,1)} %copy-done.1, bf16[64,8192]{1,0:T(8,128)(2,1)} %collective-permute-done.4.refs_2_, ...), custom_call_target="tpu_custom_call" | custom-call | flops 1610612736 | bytes 30000000 | tf_op jit(solution)/shard_map/pallas_call | solution.py:157
  66.7 7.9 %collective-permute-done.1.refs_0_ = bf16[64,8192]{1,0:T(8,128)(2,1)} collective-permute-done((bf16[64,8192]{1,0:T(8,128)(2,1)S(1)}, bf16[64,8192]{1,0:T(8,128)(2,1)}, u32[]{:S(2)}, u32[]{:S(2)}) %collective-permute-start.1) | collective-permute-done | bytes 1048608 | tf_op jit(solution)/shard_map/ppermute | solution.py:187
  76.6 11.7 %shard_map.68 = (f32[64,128,128]{2,1,0:T(8,128)}, f32[64,128,128]{2,1,0:T(8,128)}) custom-call(s32[7]{0:T(128)} %stack.40.meta, s32[3,128]{1,0:T(4,128)} %add_add_fusion.slots_ref, bf16[64,8192]{1,0:T(8,128)(2,1)} %collective-permute-done.1.refs_0_, bf16[64,8192]{1,0:T(8,128)(2,1)} %collective-permute-done.3.refs_1_, bf16[1024,3328]{1,0:T(8,128)(2,1)} %refs_2_.1, ...), custom_call_target="tpu_custom_call" | custom-call | flops 536870912 | bytes 30000000 | tf_op jit(solution)/shard_map/pallas_call | solution.py:157
  88.3 5.3 %collective-permute-done.13.slots_ref = s32[3,128]{1,0:T(4,128)S(1)} collective-permute-done((s32[3,128]{1,0:T(4,128)S(1)}, s32[3,128]{1,0:T(4,128)S(1)}, u32[]{:S(2)}, u32[]{:S(2)}) %collective-permute-start.13) | collective-permute-done | bytes 1568 | tf_op jit(solution)/shard_map/ppermute | solution.py:187
  94.1 11.6 %shard_map.69.refs_3_ = f32[128,128,128]{2,1,0:T(8,128)} custom-call(s32[7]{0:T(128)} %stack.40.meta, s32[3,128]{1,0:T(4,128)} %copy-done.6, bf16[128,8192]{1,0:T(8,128)(2,1)} %refs_0_.3, bf16[64,8192]{1,0:T(8,128)(2,1)} %copy-done.1, bf16[64,8192]{1,0:T(8,128)(2,1)} %collective-permute-done.4.refs_2_, bf16[64,8192]{1,0:T(8,128)(2,1)} %collective-permute-done.5.refs_3_, ...), custom_call_target="tpu_custom_call" | custom-call | flops 1610612736 | bytes 30000000 | tf_op jit(solution)/shard_map/pallas_call | solution.py:157
  105.7 3.5 %collective-permute-done.14.refs_2_ = bf16[128,3328]{1,0:T(8,128)(2,1)S(1)} collective-permute-done((bf16[128,3328]{1,0:T(8,128)(2,1)}, bf16[128,3328]{1,0:T(8,128)(2,1)S(1)}, u32[]{:S(2)}, u32[]{:S(2)}) %collective-permute-start.14) | collective-permute-done | bytes 852000 | tf_op jit(solution)/shard_map/ppermute | solution.py:187
  110.1 10.4 %shard_map.70 = (f32[64,128,128]{2,1,0:T(8,128)}, f32[64,128,128]{2,1,0:T(8,128)}) custom-call(s32[7]{0:T(128)} %stack.40.meta, s32[3,128]{1,0:T(4,128)} %copy-done.6, bf16[64,8192]{1,0:T(8,128)(2,1)} %collective-permute-done.1.refs_0_, bf16[64,8192]{1,0:T(8,128)(2,1)} %collective-permute-done.3.refs_1_, bf16[128,3328]{1,0:T(8,128)(2,1)} %copy-done.3, ...), custom_call_target="tpu_custom_call" | custom-call | flops 536870912 | bytes 30000000 | tf_op jit(solution)/shard_map/pallas_call | solution.py:157
  124.0 4.1 %collective-permute-done.7 = f32[8,128]{1,0:T(8,128)S(1)} collective-permute-done((f32[8,128]{1,0:T(8,128)S(1)}, f32[8,128]{1,0:T(8,128)S(1)}, u32[]{:S(2)}, u32[]{:S(2)}) %collective-permute-start.7) | collective-permute-done | bytes 4128 | tf_op jit(solution)/shard_map/ppermute | solution.py:187
  131.7 3.3 %collective-permute-start.9 = (f32[8,128]{1,0:T(8,128)S(1)}, f32[8,128]{1,0:T(8,128)S(1)}, u32[]{:S(2)}, u32[]{:S(2)}) collective-permute-start(f32[8,128]{1,0:T(8,128)S(1)} %fusion.17), channel_id=1, source_target_pairs={{0,32},{8,40},{16,48},{24,56},{32,0},{40,8},{48,16},{56,24},{64,96... | collective-permute-start | bytes 12296 | tf_op jit(solution)/shard_map/ppermute | solution.py:187
  136.6 6.8 %collective-permute-start.10 = (f32[8,128]{1,0:T(8,128)S(1)}, f32[8,128]{1,0:T(8,128)S(1)}, u32[]{:S(2)}, u32[]{:S(2)}) collective-permute-start(f32[8,128]{1,0:T(8,128)S(1)} %max.25), channel_id=1, source_target_pairs={{0,64},{8,72},{16,80},{24,88},{32,96},{40,104},{48,112},{56,120},{... | collective-permute-start | bytes 12296 | tf_op jit(solution)/shard_map/ppermute | solution.py:187
  149.1 4.6 %collective-permute-done.12 = f32[8,128]{1,0:T(8,128)S(1)} collective-permute-done((f32[8,128]{1,0:T(8,128)S(1)}, f32[8,128]{1,0:T(8,128)S(1)}, u32[]{:S(2)}, u32[]{:S(2)}) %collective-permute-start.12) | collective-permute-done | bytes 4128 | tf_op jit(solution)/shard_map/ppermute | solution.py:187
  155.0 4.3 %add_multiply_fusion = f32[64,128,128]{2,1,0:T(8,128)S(1)} fusion(f32[64,128,128]{2,1,0:T(8,128)} %get-tuple-element.20, f32[64,128,128]{2,1,0:T(8,128)} %collective-permute-done.6, f32[]{:T(128)} %bitcast.10), kind=kLoop, calls=%fused_computation.2 | loop fusion | flops 2097152 | bytes 12582916 | tf_op jit(solution)/shard_map/mul | solution.py:245
  160.6 7.2 %all-to-all-start = ((f16[32,128,128]{2,1,0:T(8,128)(2,1)}), f16[32,128,128]{2,1,0:T(8,128)(2,1)}, u32[]{:S(2)}, u32[]{:S(2)}) async-start(f16[32,128,128]{2,1,0:T(8,128)(2,1)} %get-tuple-element.33), calls=%async_computation | async-start | bytes 2097152 | tf_op jit(solution)/shard_map/all_to_all | solution.py:256
  167.8 4.5 %multiply_convert_fusion = f16[64,128,128]{2,1,0:T(8,128)(2,1)S(1)} fusion(f32[64,128,128]{2,1,0:T(8,128)} %get-tuple-element.27, f32[64,128,128]{2,1,0:T(8,128)} %collective-permute-done.18, f32[]{:T(128)} %bitcast.10), kind=kLoop, calls=%fused_computation.1 | loop fusion | flops 3145728 | bytes 10485764 | tf_op jit(solution)/shard_map/convert_element_type | solution.py:246
  177.6 9.2 %collective-permute-done.20 = f16[16,128,128]{2,1,0:T(8,128)(2,1)S(1)} collective-permute-done((f16[16,128,128]{2,1,0:T(8,128)(2,1)S(1)}, f16[16,128,128]{2,1,0:T(8,128)(2,1)S(1)}, u32[]{:S(2)}, u32[]{:S(2)}) %collective-permute-start.20) | collective-permute-done | bytes 524320 | tf_op jit(solution)/shard_map/ppermute | solution.py:187
  187.4 5.1 %collective-permute-done.29 = f16[16,128,128]{2,1,0:T(8,128)(2,1)S(1)} collective-permute-done((f16[16,128,128]{2,1,0:T(8,128)(2,1)S(1)}, f16[16,128,128]{2,1,0:T(8,128)(2,1)S(1)}, u32[]{:S(2)}, u32[]{:S(2)}) %collective-permute-start.29) | collective-permute-done | bytes 524320 | tf_op jit(solution)/shard_map/ppermute | solution.py:187
  200.1 3.8 %collective-permute-start.32 = (f16[2,128,128]{2,1,0:T(8,128)(2,1)S(1)}, f16[2,128,128]{2,1,0:T(8,128)(2,1)S(1)}, u32[]{:S(2)}, u32[]{:S(2)}) collective-permute-start(f16[2,128,128]{2,1,0:T(8,128)(2,1)S(1)} %get-tuple-element.58), channel_id=1, source_target_pairs={{0,80},{8,88},{16,96},{24,104},{32,112},{40,120},{48,0},{56,8},{64... | collective-permute-start | bytes 196616 | tf_op jit(solution)/shard_map/ppermute | solution.py:187
  209.5 3.5 %collective-permute-start.27 = (f16[2,128,128]{2,1,0:T(8,128)(2,1)S(1)}, f16[2,128,128]{2,1,0:T(8,128)(2,1)S(1)}, u32[]{:S(2)}, u32[]{:S(2)}) collective-permute-start(f16[2,128,128]{2,1,0:T(8,128)(2,1)S(1)} %get-tuple-element.47), channel_id=1, source_target_pairs={{0,112},{8,120},{16,0},{24,8},{32,16},{40,24},{48,32},{56,40},{64,... | collective-permute-start | bytes 196616 | tf_op jit(solution)/shard_map/ppermute | solution.py:187
  222.0 3.3 %collective-permute-start.21 = (f16[2,128,128]{2,1,0:T(8,128)(2,1)S(1)}, f16[2,128,128]{2,1,0:T(8,128)(2,1)S(1)}, u32[]{:S(2)}, u32[]{:S(2)}) collective-permute-start(f16[2,128,128]{2,1,0:T(8,128)(2,1)S(1)} %get-tuple-element.46), channel_id=1, source_target_pairs={{0,64},{8,72},{16,80},{24,88},{32,96},{40,104},{48,112},{56,120},{... | collective-permute-start | bytes 196616 | tf_op jit(solution)/shard_map/ppermute | solution.py:187
  234.5 18.3 %all_to_all.15 = f32[32,8,128]{2,1,0:T(8,128)S(1)} all-to-all(f32[32,8,128]{2,1,0:T(8,128)S(1)} %broadcast_in_dim_broadcast_in_dim_broadcast_in_dim.3), channel_id=1, replica_groups=mesh['dp'=32,'tensor'=8] {'dp'}, dimensions={0} | all-to-all | bytes 262144 | tf_op jit(solution)/shard_map/all_to_all | solution.py:272
  252.8 10.3 %all_to_all.16 = f32[8,8,128]{2,1,0:T(8,128)S(1)} all-to-all(f32[8,8,128]{2,1,0:T(8,128)S(1)} %broadcast_in_dim.5), channel_id=1, replica_groups=mesh['dp'=32,'tensor'=8] {'tensor'}, dimensions={0} | all-to-all | bytes 65536 | tf_op jit(solution)/shard_map/all_to_all | solution.py:272
  (118 shorter events, 77.1 us)
Async XLA Ops:
  3.1 27.5 %collective-permute-start = (bf16[64,8192]{1,0:T(8,128)(2,1)}, bf16[64,8192]{1,0:T(8,128)(2,1)S(1)}, u32[]{:S(2)}, u32[]{:S(2)}) collective-permute-start(bf16[64,8192]{1,0:T(8,128)(2,1)} %get-tuple-element.45), channel_id=1, source_target_pairs={{0,2},{1,3},{2,4},{3,5},{4,6},{5,7},{6,0},{7,1},{8,10},{9,11},{10,... | collective-permute-start | bytes 3145736 | tf_op jit(solution)/shard_map/ppermute | solution.py:187
  4.7 26.2 %collective-permute-start.2 = (bf16[64,8192]{1,0:T(8,128)(2,1)}, bf16[64,8192]{1,0:T(8,128)(2,1)S(1)}, u32[]{:S(2)}, u32[]{:S(2)}) collective-permute-start(bf16[64,8192]{1,0:T(8,128)(2,1)} %get-tuple-element.44), channel_id=1, source_target_pairs={{0,6},{1,7},{2,0},{3,1},{4,2},{5,3},{6,4},{7,5},{8,14},{9,15},{10,... | collective-permute-start | bytes 3145736 | tf_op jit(solution)/shard_map/ppermute | solution.py:187
  6.3 46.8 %collective-permute-start.4 = (bf16[64,8192]{1,0:T(8,128)(2,1)}, bf16[64,8192]{1,0:T(8,128)(2,1)}, u32[]{:S(2)}, u32[]{:S(2)}) collective-permute-start(bf16[64,8192]{1,0:T(8,128)(2,1)} %get-tuple-element.44), channel_id=1, source_target_pairs={{0,2},{1,3},{2,4},{3,5},{4,6},{5,7},{6,0},{7,1},{8,10},{9,11},{10,... | collective-permute-start | bytes 3145736 | tf_op jit(solution)/shard_map/ppermute | solution.py:187
  6.7 47.6 %collective-permute-start.5 = (bf16[64,8192]{1,0:T(8,128)(2,1)}, bf16[64,8192]{1,0:T(8,128)(2,1)}, u32[]{:S(2)}, u32[]{:S(2)}) collective-permute-start(bf16[64,8192]{1,0:T(8,128)(2,1)} %get-tuple-element.45), channel_id=1, source_target_pairs={{0,6},{1,7},{2,0},{3,1},{4,2},{5,3},{6,4},{7,5},{8,14},{9,15},{10,... | collective-permute-start | bytes 3145736 | tf_op jit(solution)/shard_map/ppermute | solution.py:187
  30.6 44.0 %collective-permute-start.1 = (bf16[64,8192]{1,0:T(8,128)(2,1)S(1)}, bf16[64,8192]{1,0:T(8,128)(2,1)}, u32[]{:S(2)}, u32[]{:S(2)}) collective-permute-start(bf16[64,8192]{1,0:T(8,128)(2,1)S(1)} %collective-permute-done.refs_1_), channel_id=1, source_target_pairs={{0,2},{1,3},{2,4},{3,5},{4,6},{5,7},{6,0},{7,1},{8,10},{9,11},{10,... | collective-permute-start | bytes 3145736 | tf_op jit(solution)/shard_map/ppermute | solution.py:187
  30.9 44.8 %collective-permute-start.3 = (bf16[64,8192]{1,0:T(8,128)(2,1)S(1)}, bf16[64,8192]{1,0:T(8,128)(2,1)}, u32[]{:S(2)}, u32[]{:S(2)}) collective-permute-start(bf16[64,8192]{1,0:T(8,128)(2,1)S(1)} %collective-permute-done.2.refs_4_), channel_id=1, source_target_pairs={{0,6},{1,7},{2,0},{3,1},{4,2},{5,3},{6,4},{7,5},{8,14},{9,15},{10,... | collective-permute-start | bytes 3145736 | tf_op jit(solution)/shard_map/ppermute | solution.py:187
  35.9 57.6 %collective-permute-start.15 = (bf16[128,3328]{1,0:T(8,128)(2,1)}, bf16[128,3328]{1,0:T(8,128)(2,1)}, u32[]{:S(2)}, u32[]{:S(2)}) collective-permute-start(bf16[128,3328]{1,0:T(8,128)(2,1)} %constant_dynamic-slice_fusion.3), channel_id=1, source_target_pairs={{0,1},{1,0},{2,3},{3,2},{4,5},{5,4},{6,7},{7,6},{8,9},{9,8},{10,11... | collective-permute-start | bytes 2555912 | tf_op jit(solution)/shard_map/ppermute | solution.py:187
  53.1 40.4 %collective-permute-start.16 = (bf16[128,3328]{1,0:T(8,128)(2,1)}, bf16[128,3328]{1,0:T(8,128)(2,1)}, u32[]{:S(2)}, u32[]{:S(2)}) collective-permute-start(bf16[128,3328]{1,0:T(8,128)(2,1)} %get-tuple-element.36), channel_id=1, source_target_pairs={{0,1},{1,0},{2,3},{3,2},{4,5},{5,4},{6,7},{7,6},{8,9},{9,8},{10,11... | collective-permute-start | bytes 2555912 | tf_op jit(solution)/shard_map/ppermute | solution.py:187
  54.3 39.2 %collective-permute-start.17 = (bf16[128,3328]{1,0:T(8,128)(2,1)}, bf16[128,3328]{1,0:T(8,128)(2,1)}, u32[]{:S(2)}, u32[]{:S(2)}) collective-permute-start(bf16[128,3328]{1,0:T(8,128)(2,1)} %get-tuple-element.35), channel_id=1, source_target_pairs={{0,1},{1,0},{2,3},{3,2},{4,5},{5,4},{6,7},{7,6},{8,9},{9,8},{10,11... | collective-permute-start | bytes 2555912 | tf_op jit(solution)/shard_map/ppermute | solution.py:187
  74.5 19.0 %collective-permute-start.13 = (s32[3,128]{1,0:T(4,128)S(1)}, s32[3,128]{1,0:T(4,128)S(1)}, u32[]{:S(2)}, u32[]{:S(2)}) collective-permute-start(s32[3,128]{1,0:T(4,128)S(1)} %copy-done.5), channel_id=1, source_target_pairs={{0,1},{1,0},{2,3},{3,2},{4,5},{5,4},{6,7},{7,6},{8,9},{9,8},{10,11... | collective-permute-start | bytes 4616 | tf_op jit(solution)/shard_map/ppermute | solution.py:187
  75.7 33.5 %collective-permute-start.14 = (bf16[128,3328]{1,0:T(8,128)(2,1)}, bf16[128,3328]{1,0:T(8,128)(2,1)S(1)}, u32[]{:S(2)}, u32[]{:S(2)}) collective-permute-start(bf16[128,3328]{1,0:T(8,128)(2,1)} %get-tuple-element.37), channel_id=1, source_target_pairs={{0,1},{1,0},{2,3},{3,2},{4,5},{5,4},{6,7},{7,6},{8,9},{9,8},{10,11... | collective-permute-start | bytes 2555912 | tf_op jit(solution)/shard_map/ppermute | solution.py:187
  93.5 61.4 %collective-permute-start.6 = (f32[64,128,128]{2,1,0:T(8,128)}, f32[64,128,128]{2,1,0:T(8,128)}, u32[]{:S(2)}, u32[]{:S(2)}) collective-permute-start(f32[64,128,128]{2,1,0:T(8,128)} %get-tuple-element.21), channel_id=1, source_target_pairs={{0,8},{8,0},{16,24},{24,16},{32,40},{40,32},{48,56},{56,48},{64,72... | collective-permute-start | bytes 12582920 | tf_op jit(solution)/shard_map/ppermute | solution.py:187
  120.5 47.3 %collective-permute-start.18 = (f32[64,128,128]{2,1,0:T(8,128)}, f32[64,128,128]{2,1,0:T(8,128)}, u32[]{:S(2)}, u32[]{:S(2)}) collective-permute-start(f32[64,128,128]{2,1,0:T(8,128)} %get-tuple-element.28), channel_id=1, source_target_pairs={{0,8},{8,0},{16,24},{24,16},{32,40},{40,32},{48,56},{56,48},{64,72... | collective-permute-start | bytes 12582920 | tf_op jit(solution)/shard_map/ppermute | solution.py:187
  160.6 53.9 %all-to-all-start = ((f16[32,128,128]{2,1,0:T(8,128)(2,1)}), f16[32,128,128]{2,1,0:T(8,128)(2,1)}, u32[]{:S(2)}, u32[]{:S(2)}) async-start(f16[32,128,128]{2,1,0:T(8,128)(2,1)} %get-tuple-element.33), calls=%async_computation | async-start | bytes 2097152 | tf_op jit(solution)/shard_map/all_to_all | solution.py:256
  172.8 14.0 %collective-permute-start.20 = (f16[16,128,128]{2,1,0:T(8,128)(2,1)S(1)}, f16[16,128,128]{2,1,0:T(8,128)(2,1)S(1)}, u32[]{:S(2)}, u32[]{:S(2)}) collective-permute-start(f16[16,128,128]{2,1,0:T(8,128)(2,1)S(1)} %get-tuple-element.43), channel_id=1, source_target_pairs={{0,129},{1,128},{2,131},{3,130},{4,133},{5,132},{6,135},{7,134},{8... | collective-permute-start | bytes 1572872 | tf_op jit(solution)/shard_map/ppermute | solution.py:187
  173.5 13.5 %collective-permute-start.19 = (f16[16,128,128]{2,1,0:T(8,128)(2,1)S(1)}, f16[16,128,128]{2,1,0:T(8,128)(2,1)S(1)}, u32[]{:S(2)}, u32[]{:S(2)}) collective-permute-start(f16[16,128,128]{2,1,0:T(8,128)(2,1)S(1)} %get-tuple-element.40), channel_id=1, source_target_pairs={{0,1},{1,0},{2,3},{3,2},{4,5},{5,4},{6,7},{7,6},{8,9},{9,8},{10,11... | collective-permute-start | bytes 1572872 | tf_op jit(solution)/shard_map/ppermute | solution.py:187
  174.6 17.8 %collective-permute-start.29 = (f16[16,128,128]{2,1,0:T(8,128)(2,1)S(1)}, f16[16,128,128]{2,1,0:T(8,128)(2,1)S(1)}, u32[]{:S(2)}, u32[]{:S(2)}) collective-permute-start(f16[16,128,128]{2,1,0:T(8,128)(2,1)S(1)} %get-tuple-element.41), channel_id=1, source_target_pairs={{0,129},{1,128},{2,131},{3,130},{4,133},{5,132},{6,135},{7,134},{8... | collective-permute-start | bytes 1572872 | tf_op jit(solution)/shard_map/ppermute | solution.py:187
  176.8 15.9 %collective-permute-start.28 = (f16[16,128,128]{2,1,0:T(8,128)(2,1)S(1)}, f16[16,128,128]{2,1,0:T(8,128)(2,1)S(1)}, u32[]{:S(2)}, u32[]{:S(2)}) collective-permute-start(f16[16,128,128]{2,1,0:T(8,128)(2,1)S(1)} %get-tuple-element.42), channel_id=1, source_target_pairs={{0,1},{1,0},{2,3},{3,2},{4,5},{5,4},{6,7},{7,6},{8,9},{9,8},{10,11... | collective-permute-start | bytes 1572872 | tf_op jit(solution)/shard_map/ppermute | solution.py:187
  197.1 12.3 %collective-permute-start.34 = (f16[2,128,128]{2,1,0:T(8,128)(2,1)S(1)}, f16[2,128,128]{2,1,0:T(8,128)(2,1)S(1)}, u32[]{:S(2)}, u32[]{:S(2)}) collective-permute-start(f16[2,128,128]{2,1,0:T(8,128)(2,1)S(1)} %get-tuple-element.56), channel_id=1, source_target_pairs={{0,96},{8,104},{16,112},{24,120},{32,0},{40,8},{48,16},{56,24},{64... | collective-permute-start | bytes 196616 | tf_op jit(solution)/shard_map/ppermute | solution.py:187
  200.1 13.0 %collective-permute-start.33 = (f16[2,128,128]{2,1,0:T(8,128)(2,1)S(1)}, f16[2,128,128]{2,1,0:T(8,128)(2,1)S(1)}, u32[]{:S(2)}, u32[]{:S(2)}) collective-permute-start(f16[2,128,128]{2,1,0:T(8,128)(2,1)S(1)} %get-tuple-element.57), channel_id=1, source_target_pairs={{0,32},{8,40},{16,48},{24,56},{32,64},{40,72},{48,80},{56,88},{64,... | collective-permute-start | bytes 196616 | tf_op jit(solution)/shard_map/ppermute | solution.py:187
  200.1 13.0 %collective-permute-start.32 = (f16[2,128,128]{2,1,0:T(8,128)(2,1)S(1)}, f16[2,128,128]{2,1,0:T(8,128)(2,1)S(1)}, u32[]{:S(2)}, u32[]{:S(2)}) collective-permute-start(f16[2,128,128]{2,1,0:T(8,128)(2,1)S(1)} %get-tuple-element.58), channel_id=1, source_target_pairs={{0,80},{8,88},{16,96},{24,104},{32,112},{40,120},{48,0},{56,8},{64... | collective-permute-start | bytes 196616 | tf_op jit(solution)/shard_map/ppermute | solution.py:187
  204.0 12.0 %collective-permute-start.31 = (f16[2,128,128]{2,1,0:T(8,128)(2,1)S(1)}, f16[2,128,128]{2,1,0:T(8,128)(2,1)S(1)}, u32[]{:S(2)}, u32[]{:S(2)}) collective-permute-start(f16[2,128,128]{2,1,0:T(8,128)(2,1)S(1)} %get-tuple-element.59), channel_id=1, source_target_pairs={{0,48},{8,56},{16,64},{24,72},{32,80},{40,88},{48,96},{56,104},{64... | collective-permute-start | bytes 196616 | tf_op jit(solution)/shard_map/ppermute | solution.py:187
  213.0 12.2 %collective-permute-start.25 = (f16[2,128,128]{2,1,0:T(8,128)(2,1)S(1)}, f16[2,128,128]{2,1,0:T(8,128)(2,1)S(1)}, u32[]{:S(2)}, u32[]{:S(2)}) collective-permute-start(f16[2,128,128]{2,1,0:T(8,128)(2,1)S(1)} %get-tuple-element.49), channel_id=1, source_target_pairs={{0,96},{8,104},{16,112},{24,120},{32,0},{40,8},{48,16},{56,24},{64... | collective-permute-start | bytes 196616 | tf_op jit(solution)/shard_map/ppermute | solution.py:187
  216.0 13.0 %collective-permute-start.24 = (f16[2,128,128]{2,1,0:T(8,128)(2,1)S(1)}, f16[2,128,128]{2,1,0:T(8,128)(2,1)S(1)}, u32[]{:S(2)}, u32[]{:S(2)}) collective-permute-start(f16[2,128,128]{2,1,0:T(8,128)(2,1)S(1)} %get-tuple-element.50), channel_id=1, source_target_pairs={{0,32},{8,40},{16,48},{24,56},{32,64},{40,72},{48,80},{56,88},{64,... | collective-permute-start | bytes 196616 | tf_op jit(solution)/shard_map/ppermute | solution.py:187
  (26 other events, 407.5 us)

commit v5 on v3

--- a/solution.py
+++ b/solution.py
@@ -210,7 +210,7 @@
     ):
         top = jnp.maximum(top, move(top, pairs, axis))
     top = jnp.clip(top[0, 0], 1e-30, 1e37)
-    meta_late, shrink, grow = lax.optimization_barrier((meta, 0.25 / top, 4.0 * top))
+    shrink, grow = lax.optimization_barrier((0.25 / top, 4.0 * top))
 
     near = (tokens, below_a, below_b, above_a, above_b)
     far = (far_a, far_b)
@@ -220,8 +220,8 @@
     (acc_x,) = partial_grads(
         "across_near", meta, table_x, near, (g_own, g_below, g_above), (None,) * 3, False
     )
-    send, keep = partial_grads("own_far", meta_late, table, far, (out_grad,), (FAR,), True, acc)
-    send_x, keep_x = partial_grads("across_far", meta_late, table_x, far, (g_far,), (None,), True, acc_x)
+    send, keep = partial_grads("own_far", meta, table, far, (out_grad,), (FAR,), True, acc)
+    send_x, keep_x = partial_grads("across_far", meta, table_x, far, (g_far,), (None,), True, acc_x)
 
     share = delta.shape[1]
     quarter = places // 4
@@ -235,8 +235,8 @@
         return total
 
     own_back = move(send, CORE_SWAP, "dp")
-    own_sum = lax.optimization_barrier((keep + own_back) * shrink)
-    other = ((keep_x + move(send_x, CORE_SWAP, "dp")) * shrink).astype(jnp.float16)
+    own_sum, shrink_x = lax.optimization_barrier(((keep + own_back) * shrink, shrink))
+    other = ((keep_x + move(send_x, CORE_SWAP, "dp")) * shrink_x).astype(jnp.float16)
     near_x = move(other[:quarter], X_SWAP)
     far_x = move(other[quarter:], DIAGONAL, ("dp", "tensor"))
     own_near, own_packed = lax.optimization_barrier(

time: 247 us -> 254 us (1.028)
  waiting for transfers between devices: 79.8 us -> 92.9 us
  blocking collectives: 29 us -> 26.1 us
    ppermute x29, waiting for transfers between devices: 79.8 us -> 92.9 us  [move(): return lax.ppermute(value, axis, pairs)]
    reduce_max x1, other arithmetic: 4.42 us -> 1.48 us  [on_device(): jnp.max(jnp.abs(later)).astype(jnp.float32)]
    all_to_all x2, blocking collectives: 29 us -> 26.1 us  [on_device(): square_sum = jnp.sum(lax.all_to_all(spread, axis, 0, 0, tiled=True), axis=0)]
  transfers between devices with their start and end apart: 30 -> 30, of which waited for: 10 -> 16; matrix products, arithmetic and copies ran while one was open for 10% -> 9% of each run, Pallas kernels for 17% -> 16%
where the time goes in v5:
time: 254 us; the launch traced here: 253 us
  waiting for transfers between devices  92.9 us (37%)
  starting transfers between devices  59.1 us (23%)
  Pallas kernels  41.1 us (16%)
  blocking collectives  26.1 us (10%)
  other arithmetic  17.1 us (7%)
  local copies, waits for them, and re-layouts  13.6 us (5%)
  between operations  2.9 us (1%)
    ppermute x29, waiting for transfers between devices, move(): return lax.ppermute(value, axis, pairs)  92.9 us
    ppermute x29, starting transfers between devices, move(): return lax.ppermute(value, axis, pairs)  51.9 us
    pallas_call x4, Pallas kernels, partial_grads(): pl.pallas_call(functools.partial(grads_kernel, plan, depths, split, acc i...  41.1 us
    all_to_all x2, blocking collectives, on_device(): square_sum = jnp.sum(lax.all_to_all(spread, axis, 0, 0, tiled=True), axis=0)  26.1 us
    all_to_all x1, starting transfers between devices, on_device(): lax.all_to_all(own_packed, 'dp', 0, 0, axis_index_groups=Z_GROUPS, tiled=...  7.21 us
    dynamic_slice x2, local copies, waits for them, and re-layouts, theirs(): return lax.dynamic_slice_in_dim(source, chunks[index] * 128, 128, 0)  5.29 us
  transfers between devices with their start and end apart: 30, of which 16 were waited for; matrix products, arithmetic and copies ran while one was open for 9% of the time, Pallas kernels for 16%

profile of v5, /device:TPU:4, one launch (start us, length us, event | category | flops | bytes accessed | tf_op | source)
XLA Modules:
  0.0 252.8 jit_solution(15368459192844791354)
XLA Ops:
  9.2 20.8 %collective-permute-done.refs_1_ = bf16[64,8192]{1,0:T(8,128)(2,1)S(1)} collective-permute-done((bf16[64,8192]{1,0:T(8,128)(2,1)S(1)}, bf16[64,8192]{1,0:T(8,128)(2,1)S(1)}, u32[]{:S(2)}, u32[]{:S(2)}) %collective-permute-start) | collective-permute-done | bytes 1048608 | tf_op jit(solution)/shard_map/ppermute | solution.py:181
  38.8 3.2 %constant_dynamic-slice_fusion = (bf16[128,3328]{1,0:T(8,128)(2,1)}, bf16[128,3328]{1,0:T(8,128)(2,1)}, bf16[128,3328]{1,0:T(8,128)(2,1)}) fusion(bf16[1024,3328]{1,0:T(8,128)(2,1)} %refs_2_.1, s32[]{:T(128)S(6)} %select_n.15, s32[]{:T(128)S(6)} %select_n.14, s32[]{:T(128)S(6)} %select_n.13), kind=kLoop, calls=%fused_computation.19 | loop fusion | bytes 5111820 | tf_op jit(solution)/shard_map/dynamic_slice | solution.py:190
  41.9 10.6 %collective-permute-done.4.refs_2_ = bf16[64,8192]{1,0:T(8,128)(2,1)} collective-permute-done((bf16[64,8192]{1,0:T(8,128)(2,1)}, bf16[64,8192]{1,0:T(8,128)(2,1)}, u32[]{:S(2)}, u32[]{:S(2)}) %collective-permute-start.4) | collective-permute-done | bytes 1048608 | tf_op jit(solution)/shard_map/ppermute | solution.py:181
  54.6 10.8 %shard_map.67.refs_3_ = f32[128,128,128]{2,1,0:T(8,128)} custom-call(s32[7]{0:T(128)} %stack.40.meta, s32[3,128]{1,0:T(4,128)} %add_add_fusion.slots_ref, bf16[128,8192]{1,0:T(8,128)(2,1)} %refs_0_.3, bf16[64,8192]{1,0:T(8,128)(2,1)} %copy-done, bf16[64,8192]{1,0:T(8,128)(2,1)} %collective-permute-done.4.refs_2_, ...), custom_call_target="tpu_custom_call" | custom-call | flops 1610612736 | bytes 30000000 | tf_op jit(solution)/shard_map/pallas_call | solution.py:151
  65.4 8.6 %collective-permute-done.1.refs_0_ = bf16[64,8192]{1,0:T(8,128)(2,1)} collective-permute-done((bf16[64,8192]{1,0:T(8,128)(2,1)S(1)}, bf16[64,8192]{1,0:T(8,128)(2,1)}, u32[]{:S(2)}, u32[]{:S(2)}) %collective-permute-start.1) | collective-permute-done | bytes 1048608 | tf_op jit(solution)/shard_map/ppermute | solution.py:181
  76.0 10.4 %shard_map.68 = (f32[64,128,128]{2,1,0:T(8,128)}, f32[64,128,128]{2,1,0:T(8,128)}) custom-call(s32[7]{0:T(128)} %stack.40.meta, s32[3,128]{1,0:T(4,128)} %add_add_fusion.slots_ref, bf16[64,8192]{1,0:T(8,128)(2,1)} %collective-permute-done.1.refs_0_, bf16[64,8192]{1,0:T(8,128)(2,1)} %collective-permute-done.3.refs_1_, bf16[1024,3328]{1,0:T(8,128)(2,1)} %refs_2_.1, ...), custom_call_target="tpu_custom_call" | custom-call | flops 536870912 | bytes 30000000 | tf_op jit(solution)/shard_map/pallas_call | solution.py:151
  86.4 6.6 %collective-permute-done.13.slots_ref = s32[3,128]{1,0:T(4,128)S(1)} collective-permute-done((s32[3,128]{1,0:T(4,128)S(1)}, s32[3,128]{1,0:T(4,128)S(1)}, u32[]{:S(2)}, u32[]{:S(2)}) %collective-permute-start.13) | collective-permute-done | bytes 1568 | tf_op jit(solution)/shard_map/ppermute | solution.py:181
  93.5 10.9 %shard_map.69.refs_3_ = f32[128,128,128]{2,1,0:T(8,128)} custom-call(s32[7]{0:T(128)} %stack.40.meta, s32[3,128]{1,0:T(4,128)} %copy-done.5, bf16[128,8192]{1,0:T(8,128)(2,1)} %refs_0_.3, bf16[64,8192]{1,0:T(8,128)(2,1)} %copy-done, bf16[64,8192]{1,0:T(8,128)(2,1)} %collective-permute-done.4.refs_2_, bf16[64,8192]{1,0:T(8,128)(2,1)} %collective-permute-done.5.refs_3_, ...), custom_call_target="tpu_custom_call" | custom-call | flops 1610612736 | bytes 30000000 | tf_op jit(solution)/shard_map/pallas_call | solution.py:151
  104.4 4.2 %collective-permute-done.14.refs_2_ = bf16[128,3328]{1,0:T(8,128)(2,1)S(1)} collective-permute-done((bf16[128,3328]{1,0:T(8,128)(2,1)}, bf16[128,3328]{1,0:T(8,128)(2,1)S(1)}, u32[]{:S(2)}, u32[]{:S(2)}) %collective-permute-start.14) | collective-permute-done | bytes 852000 | tf_op jit(solution)/shard_map/ppermute | solution.py:181
  109.6 9.1 %shard_map.70 = (f32[64,128,128]{2,1,0:T(8,128)}, f32[64,128,128]{2,1,0:T(8,128)}) custom-call(s32[7]{0:T(128)} %stack.40.meta, s32[3,128]{1,0:T(4,128)} %copy-done.5, bf16[64,8192]{1,0:T(8,128)(2,1)} %collective-permute-done.1.refs_0_, bf16[64,8192]{1,0:T(8,128)(2,1)} %collective-permute-done.3.refs_1_, bf16[128,3328]{1,0:T(8,128)(2,1)} %copy-done.2, ...), custom_call_target="tpu_custom_call" | custom-call | flops 536870912 | bytes 30000000 | tf_op jit(solution)/shard_map/pallas_call | solution.py:151
  122.2 4.1 %collective-permute-done.7 = f32[8,128]{1,0:T(8,128)S(1)} collective-permute-done((f32[8,128]{1,0:T(8,128)S(1)}, f32[8,128]{1,0:T(8,128)S(1)}, u32[]{:S(2)}, u32[]{:S(2)}) %collective-permute-start.7) | collective-permute-done | bytes 4128 | tf_op jit(solution)/shard_map/ppermute | solution.py:181
  129.9 3.3 %collective-permute-start.9 = (f32[8,128]{1,0:T(8,128)S(1)}, f32[8,128]{1,0:T(8,128)S(1)}, u32[]{:S(2)}, u32[]{:S(2)}) collective-permute-start(f32[8,128]{1,0:T(8,128)S(1)} %fusion.13), channel_id=1, source_target_pairs={{0,32},{8,40},{16,48},{24,56},{32,0},{40,8},{48,16},{56,24},{64,96... | collective-permute-start | bytes 12296 | tf_op jit(solution)/shard_map/ppermute | solution.py:181
  134.8 6.8 %collective-permute-start.10 = (f32[8,128]{1,0:T(8,128)S(1)}, f32[8,128]{1,0:T(8,128)S(1)}, u32[]{:S(2)}, u32[]{:S(2)}) collective-permute-start(f32[8,128]{1,0:T(8,128)S(1)} %max.25), channel_id=1, source_target_pairs={{0,64},{8,72},{16,80},{24,88},{32,96},{40,104},{48,112},{56,120},{... | collective-permute-start | bytes 12296 | tf_op jit(solution)/shard_map/ppermute | solution.py:181
  147.3 4.6 %collective-permute-done.12 = f32[8,128]{1,0:T(8,128)S(1)} collective-permute-done((f32[8,128]{1,0:T(8,128)S(1)}, f32[8,128]{1,0:T(8,128)S(1)}, u32[]{:S(2)}, u32[]{:S(2)}) %collective-permute-start.12) | collective-permute-done | bytes 4128 | tf_op jit(solution)/shard_map/ppermute | solution.py:181
  153.1 4.3 %add_multiply_fusion = f32[64,128,128]{2,1,0:T(8,128)S(1)} fusion(f32[64,128,128]{2,1,0:T(8,128)} %get-tuple-element.17, f32[64,128,128]{2,1,0:T(8,128)} %collective-permute-done.6, f32[]{:T(128)} %bitcast.10), kind=kLoop, calls=%fused_computation.2 | loop fusion | flops 2097152 | bytes 12582916 | tf_op jit(solution)/shard_map/mul | solution.py:238
  158.8 7.2 %all-to-all-start = ((f16[32,128,128]{2,1,0:T(8,128)(2,1)}), f16[32,128,128]{2,1,0:T(8,128)(2,1)S(1)}, u32[]{:S(2)}, u32[]{:S(2)}) async-start(f16[32,128,128]{2,1,0:T(8,128)(2,1)} %get-tuple-element.27), calls=%async_computation | async-start | bytes 2097152 | tf_op jit(solution)/shard_map/all_to_all | solution.py:245
  166.0 4.5 %multiply_convert_fusion = f16[64,128,128]{2,1,0:T(8,128)(2,1)S(1)} fusion(f32[64,128,128]{2,1,0:T(8,128)} %get-tuple-element.24, f32[64,128,128]{2,1,0:T(8,128)} %collective-permute-done.18, f32[]{:T(128)} %bitcast.10), kind=kLoop, calls=%fused_computation.1 | loop fusion | flops 3145728 | bytes 10485764 | tf_op jit(solution)/shard_map/convert_element_type | solution.py:239
  173.1 17.8 %collective-permute-done.20 = f16[32,128,128]{2,1,0:T(8,128)(2,1)S(1)} collective-permute-done((f16[32,128,128]{2,1,0:T(8,128)(2,1)S(1)}, f16[32,128,128]{2,1,0:T(8,128)(2,1)S(1)}, u32[]{:S(2)}, u32[]{:S(2)}) %collective-permute-start.20) | collective-permute-done | bytes 1048608 | tf_op jit(solution)/shard_map/ppermute | solution.py:181
  193.5 3.0 %collective-permute-start.27 = (f16[4,128,128]{2,1,0:T(8,128)(2,1)S(1)}, f16[4,128,128]{2,1,0:T(8,128)(2,1)S(1)}, u32[]{:S(2)}, u32[]{:S(2)}) collective-permute-start(f16[4,128,128]{2,1,0:T(8,128)(2,1)S(1)} %get-tuple-element.43), channel_id=1, source_target_pairs={{0,112},{8,120},{16,0},{24,8},{32,16},{40,24},{48,32},{56,40},{64,... | collective-permute-start | bytes 393224 | tf_op jit(solution)/shard_map/ppermute | solution.py:181
  202.4 3.8 %collective-permute-start.23 = (f16[4,128,128]{2,1,0:T(8,128)(2,1)S(1)}, f16[4,128,128]{2,1,0:T(8,128)(2,1)S(1)}, u32[]{:S(2)}, u32[]{:S(2)}) collective-permute-start(f16[4,128,128]{2,1,0:T(8,128)(2,1)S(1)} %get-tuple-element.47), channel_id=1, source_target_pairs={{0,80},{8,88},{16,96},{24,104},{32,112},{40,120},{48,0},{56,8},{64... | collective-permute-start | bytes 393224 | tf_op jit(solution)/shard_map/ppermute | solution.py:181
  207.5 7.0 %collective-permute-start.21 = (f16[4,128,128]{2,1,0:T(8,128)(2,1)S(1)}, f16[4,128,128]{2,1,0:T(8,128)(2,1)S(1)}, u32[]{:S(2)}, u32[]{:S(2)}) collective-permute-start(f16[4,128,128]{2,1,0:T(8,128)(2,1)S(1)} %get-tuple-element.42), channel_id=1, source_target_pairs={{0,64},{8,72},{16,80},{24,88},{32,96},{40,104},{48,112},{56,120},{... | collective-permute-start | bytes 393224 | tf_op jit(solution)/shard_map/ppermute | solution.py:181
  216.7 5.5 %collective-permute-done.21 = f16[4,128,128]{2,1,0:T(8,128)(2,1)S(1)} collective-permute-done((f16[4,128,128]{2,1,0:T(8,128)(2,1)S(1)}, f16[4,128,128]{2,1,0:T(8,128)(2,1)S(1)}, u32[]{:S(2)}, u32[]{:S(2)}) %collective-permute-start.21) | collective-permute-done | bytes 131104 | tf_op jit(solution)/shard_map/ppermute | solution.py:181
  224.7 16.6 %all_to_all.15 = f32[32,8,128]{2,1,0:T(8,128)S(1)} all-to-all(f32[32,8,128]{2,1,0:T(8,128)S(1)} %broadcast_in_dim_broadcast_in_dim_broadcast_in_dim.3), channel_id=1, replica_groups=mesh['dp'=32,'tensor'=8] {'dp'}, dimensions={0} | all-to-all | bytes 262144 | tf_op jit(solution)/shard_map/all_to_all | solution.py:253
  241.3 9.5 %all_to_all.16 = f32[8,8,128]{2,1,0:T(8,128)S(1)} all-to-all(f32[8,8,128]{2,1,0:T(8,128)S(1)} %broadcast_in_dim.5), channel_id=1, replica_groups=mesh['dp'=32,'tensor'=8] {'tensor'}, dimensions={0} | all-to-all | bytes 65536 | tf_op jit(solution)/shard_map/all_to_all | solution.py:253
  (92 shorter events, 56.8 us)
Async XLA Ops:
  2.8 27.2 %collective-permute-start = (bf16[64,8192]{1,0:T(8,128)(2,1)S(1)}, bf16[64,8192]{1,0:T(8,128)(2,1)S(1)}, u32[]{:S(2)}, u32[]{:S(2)}) collective-permute-start(bf16[64,8192]{1,0:T(8,128)(2,1)S(1)} %get-tuple-element.41), channel_id=1, source_target_pairs={{0,2},{1,3},{2,4},{3,5},{4,6},{5,7},{6,0},{7,1},{8,10},{9,11},{10,... | collective-permute-start | bytes 3145736 | tf_op jit(solution)/shard_map/ppermute | solution.py:181
  4.3 26.2 %collective-permute-start.2 = (bf16[64,8192]{1,0:T(8,128)(2,1)}, bf16[64,8192]{1,0:T(8,128)(2,1)S(1)}, u32[]{:S(2)}, u32[]{:S(2)}) collective-permute-start(bf16[64,8192]{1,0:T(8,128)(2,1)} %get-tuple-element.40), channel_id=1, source_target_pairs={{0,6},{1,7},{2,0},{3,1},{4,2},{5,3},{6,4},{7,5},{8,14},{9,15},{10,... | collective-permute-start | bytes 3145736 | tf_op jit(solution)/shard_map/ppermute | solution.py:181
  6.0 46.6 %collective-permute-start.4 = (bf16[64,8192]{1,0:T(8,128)(2,1)}, bf16[64,8192]{1,0:T(8,128)(2,1)}, u32[]{:S(2)}, u32[]{:S(2)}) collective-permute-start(bf16[64,8192]{1,0:T(8,128)(2,1)} %get-tuple-element.40), channel_id=1, source_target_pairs={{0,2},{1,3},{2,4},{3,5},{4,6},{5,7},{6,0},{7,1},{8,10},{9,11},{10,... | collective-permute-start | bytes 3145736 | tf_op jit(solution)/shard_map/ppermute | solution.py:181
  6.4 47.4 %collective-permute-start.5 = (bf16[64,8192]{1,0:T(8,128)(2,1)S(1)}, bf16[64,8192]{1,0:T(8,128)(2,1)}, u32[]{:S(2)}, u32[]{:S(2)}) collective-permute-start(bf16[64,8192]{1,0:T(8,128)(2,1)S(1)} %get-tuple-element.41), channel_id=1, source_target_pairs={{0,6},{1,7},{2,0},{3,1},{4,2},{5,3},{6,4},{7,5},{8,14},{9,15},{10,... | collective-permute-start | bytes 3145736 | tf_op jit(solution)/shard_map/ppermute | solution.py:181
  30.0 44.0 %collective-permute-start.1 = (bf16[64,8192]{1,0:T(8,128)(2,1)S(1)}, bf16[64,8192]{1,0:T(8,128)(2,1)}, u32[]{:S(2)}, u32[]{:S(2)}) collective-permute-start(bf16[64,8192]{1,0:T(8,128)(2,1)S(1)} %collective-permute-done.refs_1_), channel_id=1, source_target_pairs={{0,2},{1,3},{2,4},{3,5},{4,6},{5,7},{6,0},{7,1},{8,10},{9,11},{10,... | collective-permute-start | bytes 3145736 | tf_op jit(solution)/shard_map/ppermute | solution.py:181
  30.6 44.6 %collective-permute-start.3 = (bf16[64,8192]{1,0:T(8,128)(2,1)S(1)}, bf16[64,8192]{1,0:T(8,128)(2,1)}, u32[]{:S(2)}, u32[]{:S(2)}) collective-permute-start(bf16[64,8192]{1,0:T(8,128)(2,1)S(1)} %collective-permute-done.2.refs_4_), channel_id=1, source_target_pairs={{0,6},{1,7},{2,0},{3,1},{4,2},{5,3},{6,4},{7,5},{8,14},{9,15},{10,... | collective-permute-start | bytes 3145736 | tf_op jit(solution)/shard_map/ppermute | solution.py:181
  35.6 57.4 %collective-permute-start.15 = (bf16[128,3328]{1,0:T(8,128)(2,1)}, bf16[128,3328]{1,0:T(8,128)(2,1)}, u32[]{:S(2)}, u32[]{:S(2)}) collective-permute-start(bf16[128,3328]{1,0:T(8,128)(2,1)} %constant_dynamic-slice_fusion.3), channel_id=1, source_target_pairs={{0,1},{1,0},{2,3},{3,2},{4,5},{5,4},{6,7},{7,6},{8,9},{9,8},{10,11... | collective-permute-start | bytes 2555912 | tf_op jit(solution)/shard_map/ppermute | solution.py:181
  52.6 40.4 %collective-permute-start.16 = (bf16[128,3328]{1,0:T(8,128)(2,1)}, bf16[128,3328]{1,0:T(8,128)(2,1)}, u32[]{:S(2)}, u32[]{:S(2)}) collective-permute-start(bf16[128,3328]{1,0:T(8,128)(2,1)} %get-tuple-element.34), channel_id=1, source_target_pairs={{0,1},{1,0},{2,3},{3,2},{4,5},{5,4},{6,7},{7,6},{8,9},{9,8},{10,11... | collective-permute-start | bytes 2555912 | tf_op jit(solution)/shard_map/ppermute | solution.py:181
  53.8 39.2 %collective-permute-start.17 = (bf16[128,3328]{1,0:T(8,128)(2,1)}, bf16[128,3328]{1,0:T(8,128)(2,1)}, u32[]{:S(2)}, u32[]{:S(2)}) collective-permute-start(bf16[128,3328]{1,0:T(8,128)(2,1)} %get-tuple-element.33), channel_id=1, source_target_pairs={{0,1},{1,0},{2,3},{3,2},{4,5},{5,4},{6,7},{7,6},{8,9},{9,8},{10,11... | collective-permute-start | bytes 2555912 | tf_op jit(solution)/shard_map/ppermute | solution.py:181
  74.0 19.0 %collective-permute-start.13 = (s32[3,128]{1,0:T(4,128)S(1)}, s32[3,128]{1,0:T(4,128)S(1)}, u32[]{:S(2)}, u32[]{:S(2)}) collective-permute-start(s32[3,128]{1,0:T(4,128)S(1)} %copy-done.4), channel_id=1, source_target_pairs={{0,1},{1,0},{2,3},{3,2},{4,5},{5,4},{6,7},{7,6},{8,9},{9,8},{10,11... | collective-permute-start | bytes 4616 | tf_op jit(solution)/shard_map/ppermute | solution.py:181
  75.2 33.5 %collective-permute-start.14 = (bf16[128,3328]{1,0:T(8,128)(2,1)}, bf16[128,3328]{1,0:T(8,128)(2,1)S(1)}, u32[]{:S(2)}, u32[]{:S(2)}) collective-permute-start(bf16[128,3328]{1,0:T(8,128)(2,1)} %get-tuple-element.35), channel_id=1, source_target_pairs={{0,1},{1,0},{2,3},{3,2},{4,5},{5,4},{6,7},{7,6},{8,9},{9,8},{10,11... | collective-permute-start | bytes 2555912 | tf_op jit(solution)/shard_map/ppermute | solution.py:181
  93.0 60.2 %collective-permute-start.6 = (f32[64,128,128]{2,1,0:T(8,128)}, f32[64,128,128]{2,1,0:T(8,128)}, u32[]{:S(2)}, u32[]{:S(2)}) collective-permute-start(f32[64,128,128]{2,1,0:T(8,128)} %get-tuple-element.18), channel_id=1, source_target_pairs={{0,8},{8,0},{16,24},{24,16},{32,40},{40,32},{48,56},{56,48},{64,72... | collective-permute-start | bytes 12582920 | tf_op jit(solution)/shard_map/ppermute | solution.py:181
  118.7 47.3 %collective-permute-start.18 = (f32[64,128,128]{2,1,0:T(8,128)}, f32[64,128,128]{2,1,0:T(8,128)}, u32[]{:S(2)}, u32[]{:S(2)}) collective-permute-start(f32[64,128,128]{2,1,0:T(8,128)} %get-tuple-element.25), channel_id=1, source_target_pairs={{0,8},{8,0},{16,24},{24,16},{32,40},{40,32},{48,56},{56,48},{64,72... | collective-permute-start | bytes 12582920 | tf_op jit(solution)/shard_map/ppermute | solution.py:181
  158.8 40.6 %all-to-all-start = ((f16[32,128,128]{2,1,0:T(8,128)(2,1)}), f16[32,128,128]{2,1,0:T(8,128)(2,1)S(1)}, u32[]{:S(2)}, u32[]{:S(2)}) async-start(f16[32,128,128]{2,1,0:T(8,128)(2,1)} %get-tuple-element.27), calls=%async_computation | async-start | bytes 2097152 | tf_op jit(solution)/shard_map/all_to_all | solution.py:245
  171.3 19.6 %collective-permute-start.20 = (f16[32,128,128]{2,1,0:T(8,128)(2,1)S(1)}, f16[32,128,128]{2,1,0:T(8,128)(2,1)S(1)}, u32[]{:S(2)}, u32[]{:S(2)}) collective-permute-start(f16[32,128,128]{2,1,0:T(8,128)(2,1)S(1)} %get-tuple-element.39), channel_id=1, source_target_pairs={{0,129},{1,128},{2,131},{3,130},{4,133},{5,132},{6,135},{7,134},{8... | collective-permute-start | bytes 3145736 | tf_op jit(solution)/shard_map/ppermute | solution.py:181
  172.0 19.3 %collective-permute-start.19 = (f16[32,128,128]{2,1,0:T(8,128)(2,1)S(1)}, f16[32,128,128]{2,1,0:T(8,128)(2,1)S(1)}, u32[]{:S(2)}, u32[]{:S(2)}) collective-permute-start(f16[32,128,128]{2,1,0:T(8,128)(2,1)S(1)} %get-tuple-element.38), channel_id=1, source_target_pairs={{0,1},{1,0},{2,3},{3,2},{4,5},{5,4},{6,7},{7,6},{8,9},{9,8},{10,11... | collective-permute-start | bytes 3145736 | tf_op jit(solution)/shard_map/ppermute | solution.py:181
  193.5 8.9 %collective-permute-start.27 = (f16[4,128,128]{2,1,0:T(8,128)(2,1)S(1)}, f16[4,128,128]{2,1,0:T(8,128)(2,1)S(1)}, u32[]{:S(2)}, u32[]{:S(2)}) collective-permute-start(f16[4,128,128]{2,1,0:T(8,128)(2,1)S(1)} %get-tuple-element.43), channel_id=1, source_target_pairs={{0,112},{8,120},{16,0},{24,8},{32,16},{40,24},{48,32},{56,40},{64,... | collective-permute-start | bytes 393224 | tf_op jit(solution)/shard_map/ppermute | solution.py:181
  196.5 9.7 %collective-permute-start.26 = (f16[4,128,128]{2,1,0:T(8,128)(2,1)S(1)}, f16[4,128,128]{2,1,0:T(8,128)(2,1)S(1)}, u32[]{:S(2)}, u32[]{:S(2)}) collective-permute-start(f16[4,128,128]{2,1,0:T(8,128)(2,1)S(1)} %get-tuple-element.44), channel_id=1, source_target_pairs={{0,16},{8,24},{16,32},{24,40},{32,48},{40,56},{48,64},{56,72},{64,... | collective-permute-start | bytes 393224 | tf_op jit(solution)/shard_map/ppermute | solution.py:181
  196.5 11.0 %collective-permute-start.25 = (f16[4,128,128]{2,1,0:T(8,128)(2,1)S(1)}, f16[4,128,128]{2,1,0:T(8,128)(2,1)S(1)}, u32[]{:S(2)}, u32[]{:S(2)}) collective-permute-start(f16[4,128,128]{2,1,0:T(8,128)(2,1)S(1)} %get-tuple-element.45), channel_id=1, source_target_pairs={{0,96},{8,104},{16,112},{24,120},{32,0},{40,8},{48,16},{56,24},{64... | collective-permute-start | bytes 393224 | tf_op jit(solution)/shard_map/ppermute | solution.py:181
  199.7 22.6 %collective-permute-start.28 = (f32[4,128,128]{2,1,0:T(8,128)S(1)}, f32[4,128,128]{2,1,0:T(8,128)S(1)}, u32[]{:S(2)}, u32[]{:S(2)}) collective-permute-start(f32[4,128,128]{2,1,0:T(8,128)S(1)} %convert_reduce_fusion), channel_id=1, source_target_pairs={{0,128},{8,136},{16,144},{24,152},{32,160},{40,168},{48,176},{56,1... | collective-permute-start | bytes 786440 | tf_op jit(solution)/shard_map/ppermute | solution.py:181
  202.4 12.1 %collective-permute-start.24 = (f16[4,128,128]{2,1,0:T(8,128)(2,1)S(1)}, f16[4,128,128]{2,1,0:T(8,128)(2,1)S(1)}, u32[]{:S(2)}, u32[]{:S(2)}) collective-permute-start(f16[4,128,128]{2,1,0:T(8,128)(2,1)S(1)} %get-tuple-element.46), channel_id=1, source_target_pairs={{0,32},{8,40},{16,48},{24,56},{32,64},{40,72},{48,80},{56,88},{64,... | collective-permute-start | bytes 393224 | tf_op jit(solution)/shard_map/ppermute | solution.py:181
  202.4 12.1 %collective-permute-start.23 = (f16[4,128,128]{2,1,0:T(8,128)(2,1)S(1)}, f16[4,128,128]{2,1,0:T(8,128)(2,1)S(1)}, u32[]{:S(2)}, u32[]{:S(2)}) collective-permute-start(f16[4,128,128]{2,1,0:T(8,128)(2,1)S(1)} %get-tuple-element.47), channel_id=1, source_target_pairs={{0,80},{8,88},{16,96},{24,104},{32,112},{40,120},{48,0},{56,8},{64... | collective-permute-start | bytes 393224 | tf_op jit(solution)/shard_map/ppermute | solution.py:181
  206.2 10.5 %collective-permute-start.22 = (f16[4,128,128]{2,1,0:T(8,128)(2,1)S(1)}, f16[4,128,128]{2,1,0:T(8,128)(2,1)S(1)}, u32[]{:S(2)}, u32[]{:S(2)}) collective-permute-start(f16[4,128,128]{2,1,0:T(8,128)(2,1)S(1)} %get-tuple-element.48), channel_id=1, source_target_pairs={{0,48},{8,56},{16,64},{24,72},{32,80},{40,88},{48,96},{56,104},{64... | collective-permute-start | bytes 393224 | tf_op jit(solution)/shard_map/ppermute | solution.py:181
  207.5 14.7 %collective-permute-start.21 = (f16[4,128,128]{2,1,0:T(8,128)(2,1)S(1)}, f16[4,128,128]{2,1,0:T(8,128)(2,1)S(1)}, u32[]{:S(2)}, u32[]{:S(2)}) collective-permute-start(f16[4,128,128]{2,1,0:T(8,128)(2,1)S(1)} %get-tuple-element.42), channel_id=1, source_target_pairs={{0,64},{8,72},{16,80},{24,88},{32,96},{40,104},{48,112},{56,120},{... | collective-permute-start | bytes 393224 | tf_op jit(solution)/shard_map/ppermute | solution.py:181
  (16 other events, 304.9 us)
